TPU v7x, 32 devices: a whole 2x2x4 slice. The times are simulated.
32 devices in a mesh: dp: 8 (over z, y), tensor: 4 (over x, core).
Axes of the slice: x: 2, y: 2, z: 4, core: 2. Of those that a mesh axis runs over, the one named last changes fastest.
Arguments:
- master: float32 [2, 8192, 2048], P(None, 'dp', 'tensor'), may hold values from -0.0625 to 0.0625
- momentum: float32 [2, 8192, 2048], P(None, 'dp', 'tensor'), may hold values from -6 to 6
- gradient: float32 [2, 8192, 2048], P(None, 'dp', 'tensor'), may hold values from -60 to 60
- bucket_table: int32 [4, 8], P('tensor'), may hold values from 0 to 3, as said below
- tokens: bfloat16 [2048, 8192], P('dp', 'tensor'), may hold values from -6 to 6
- norm_gain: float32 [8192], replicated, may hold values from 0.1 to 1.9
Outputs:
- new_master: float32 [2, 8192, 2048], P(None, 'dp', 'tensor')
- new_momentum: float32 [2, 8192, 2048], P(None, 'dp', 'tensor')
- key_values: bfloat16 [2048, 2048], P('dp', 'tensor')
Inputs may be any that keep to these rules, and one draw needn't show every extreme that they name: `bucket_table`: in each row of 8 entries every value from 0 to 3 appears exactly twice.
All inputs are finite; a program needn't handle non-finite values.
Results may differ from a plain program's by a relative error of at most 0.001.
The roundings to bfloat16 on the way count: a program that leaves them out, or rounds other values in their place, can miss the bound.
Values may be sent and summed in bfloat16 or wider, within the bound.
No kernel may reach another device: no remote copies, remote signals or barrier semaphores. Data moves between devices by JAX's collectives and lax.ppermute only.
A program may use at most 128 MiB of HBM per device.

v0:
```python
import functools
import math

import jax
import jax.numpy as jnp
from jax import lax
from jax.experimental import pallas as pl
from jax.experimental.pallas import tpu as pltpu
from jax.sharding import PartitionSpec as P


HD = 128
NS_ITERS = 3

beta_momentum = 0.95
learn_rate = 0.05
first_coeff = 3.4445
cube_coeff = -4.775
fifth_coeff = 2.0315
frob_epsilon = 1e-07
rms_epsilon = 1e-05

CHUNKS = 2
ROWS = 256
MIB = 1 << 20
CODE_ROWS = 16
CODE_BITS = 14.9
LEAST = 2.0**-100

bf16 = jnp.bfloat16
f32 = jnp.float32
HIGHEST = lax.Precision.HIGHEST


def head_of(table, place, count):
    bucket = place // 2
    lower = jnp.int32(0)
    upper = jnp.int32(0)
    for i in range(count):
        j = count - 1 - i
        lower = jnp.where(table[j] == bucket, j, lower)
        upper = jnp.where(table[i] == bucket, i, upper)
    return jnp.where(place % 2 == 0, lower, upper)


def grid_masks(size):
    rows = lax.broadcasted_iota(jnp.int32, (size, size), 0)
    cols = lax.broadcasted_iota(jnp.int32, (size, size), 1)
    return rows, cols


def pack_symmetric(full):
    half = full.shape[0] // 2
    rows, cols = grid_masks(half)
    low = full[half:, half:]
    mixed = jnp.where(rows <= cols, full[:half, :half], low)
    diag = jnp.sum(jnp.where(rows == cols, low, 0.0), axis=0, keepdims=True)
    return mixed, full[:half, half:], jnp.broadcast_to(diag, (8, half))


def unpack_symmetric(packed):
    half = packed.shape[1]
    mixed = packed[:half]
    side = packed[half : 2 * half]
    diag = packed[2 * half : 2 * half + 1]
    rows, cols = grid_masks(half)
    turned = mixed.T
    first = jnp.where(rows <= cols, mixed, turned)
    low = jnp.where(rows > cols, mixed, jnp.where(rows == cols, diag, turned))
    return jnp.concatenate(
        [
            jnp.concatenate([first, side], axis=1),
            jnp.concatenate([side.T, low], axis=1),
        ],
        axis=0,
    )


def store_packed(ref, full):
    half = full.shape[0] // 2
    mixed, side, diag = pack_symmetric(full)
    ref[0:half, :] = mixed
    ref[half : 2 * half, :] = side
    ref[2 * half : 2 * half + 8, :] = diag


def dot_t(a, b):
    return lax.dot_general(a, b, (((0,), (0,)), ((), ())), preferred_element_type=f32)


def dot_full(a, b):
    return lax.dot_general(
        a, b, (((1,), (0,)), ((), ())), precision=HIGHEST, preferred_element_type=f32
    )


def bucket_side(table, head):
    side = jnp.int32(0)
    for i in range(head):
        side = jnp.where(table[i] == table[head], 1, side)
    return side


def gram_kernel(table, place, momentum, gradient, new_momentum, update, *rest, parts, slots):
    outs = rest[:parts]
    split, total = rest[parts:]
    step = pl.program_id(0)
    layers, height, _ = momentum.shape
    wide = 2 * HD
    rows = pl.ds(pl.multiple_of(step * height, height), height)
    for head in range(layers * slots):
        layer = head // slots
        cols = slice((head % slots) * HD, (head % slots + 1) * HD)
        slope = gradient[layer, :, cols]
        fresh = beta_momentum * momentum[layer, :, cols] + slope
        new_momentum[layer, :, cols] = fresh
        change = slope + beta_momentum * fresh
        update[layer, rows, cols] = change
        first = change.astype(bf16)
        left = change - first.astype(f32)
        second = left.astype(bf16)
        third = (left - second.astype(f32)).astype(bf16)
        side = bucket_side(table, head)
        for k, plane in enumerate((first, second, third)):
            start = pl.multiple_of(k * wide + side * HD, HD)
            split[table[head], :, pl.ds(start, HD)] = plane

    for bucket in range(parts):
        planes = split[bucket]
        one = planes[:, :wide]
        two = planes[:, wide : 2 * wide]
        mixed = dot_t(one, planes)
        rough = mixed[:, :wide] + dot_t(two, two)
        rough = rough + 2.0 * (mixed[:, wide : 2 * wide] + mixed[:, 2 * wide :])

        @pl.when(step == 0)
        def _():
            total[bucket] = rough

        @pl.when(step > 0)
        def _():
            total[bucket] = total[bucket] + rough

    @pl.when(step == pl.num_programs(0) - 1)
    def _():
        for bucket in range(parts):
            rough = total[bucket]
            mixed, side, diag = pack_symmetric(0.5 * (rough + rough.T))
            away = bucket ^ place[0]
            for k in range(parts):

                @pl.when(away == k)
                def _():
                    outs[k][0:HD, :] = mixed
                    outs[k][HD : 2 * HD, :] = side
                    outs[k][2 * HD : 2 * HD + 8, :] = diag


def local_grams(table, place, momentum, gradient, parts):
    layers, height, width = momentum.shape
    slots = width // HD
    tall = min(height, ROWS)
    block = pl.BlockSpec((layers, tall, width), lambda i, t, q: (0, i, 0))
    packed = (2 * HD + 8, HD)
    return pl.pallas_call(
        functools.partial(gram_kernel, parts=parts, slots=slots),
        grid_spec=pltpu.PrefetchScalarGridSpec(
            num_scalar_prefetch=2,
            grid=(height // tall,),
            in_specs=[block, block],
            out_specs=[block, pl.BlockSpec(memory_space=pltpu.VMEM)]
            + [pl.BlockSpec(packed, lambda i, t, q: (0, 0))] * parts,
            scratch_shapes=[
                pltpu.VMEM((parts, tall, 6 * HD), bf16),
                pltpu.VMEM((parts, 2 * HD, 2 * HD), f32),
            ],
        ),
        out_shape=[
            jax.ShapeDtypeStruct(momentum.shape, f32),
            pltpu.VMEM(momentum.shape, f32),
        ]
        + [jax.ShapeDtypeStruct(packed, f32)] * parts,
        compiler_params=pltpu.CompilerParams(vmem_limit_bytes=24 * MIB),
        name="grams",
    )(table, place, hbm(momentum), hbm(gradient))


def series_kernel(*refs, step_scale):
    *pieces, sums, out = refs
    packed = pieces[0][...]
    for ref in pieces[1:]:
        packed = packed + ref[...]
    total = unpack_symmetric(packed)
    rows, cols = grid_masks(total.shape[0])
    on_diag = rows == cols
    trace = jnp.sum(jnp.where(on_diag, total, 0.0), keepdims=True)
    scale = 1.0 / (jnp.sqrt(trace) + frob_epsilon)
    gram = total * (scale * scale)
    product = None
    for iteration in range(NS_ITERS):
        square = dot_full(gram, gram)
        factor = cube_coeff * gram + fifth_coeff * square
        factor = factor + jnp.where(on_diag, first_coeff, 0.0)
        product = factor if product is None else dot_full(product, factor)
        if iteration + 1 < NS_ITERS:
            gram = dot_full(dot_full(gram, factor), factor)
    store_packed(out, product * (scale * step_scale))
    high = pieces[0].shape[0]
    out[high : high + 8, :] = jnp.zeros((8, HD), f32)
    out[high : high + sums.shape[0], :] = sums[...]


def hbm(value):
    return pltpu.with_memory_space_constraint(value, pltpu.HBM)


def vmem(value):
    return pltpu.with_memory_space_constraint(value, pltpu.VMEM)


VM = pl.BlockSpec(memory_space=pltpu.VMEM)
SM = pl.BlockSpec(memory_space=pltpu.SMEM)


def series(pieces, sums, step_scale):
    high, wide = pieces[0].shape
    return pl.pallas_call(
        functools.partial(series_kernel, step_scale=step_scale),
        in_specs=[VM] * (len(pieces) + 1),
        out_specs=VM,
        out_shape=pltpu.VMEM((high + 8, wide), f32),
        compiler_params=pltpu.CompilerParams(vmem_limit_bytes=8 * MIB),
        name="series",
    )(*[vmem(p) for p in pieces], vmem(sums))


def split_three(value):
    one = value.astype(bf16)
    left = value - one.astype(f32)
    two = left.astype(bf16)
    return one, two, (left - two.astype(f32)).astype(bf16)


def head_pair(update, rows, spots):
    pair = [update[layer, rows, cols] for layer, cols in spots]
    one, two, three = split_three(jnp.concatenate(pair, axis=1))
    return jnp.concatenate([one, one, one, two, two, three], axis=1)


def head_spots(table, bucket, slots, count):
    spots = []
    for side in range(2):
        head = head_of(table, 2 * bucket + side, count)
        spots.append((head // slots, pl.ds(pl.multiple_of(head % slots * HD, HD), HD)))
    return spots


def lead_kernel(table, place, *refs, parts, slots, heads):
    packed = refs[:parts]
    update, master, weights, factors = refs[parts:]
    layers, height, _ = master.shape
    wide = 2 * HD
    for k in range(parts):
        planes = split_three(unpack_symmetric(packed[k][0 : 2 * HD + 8, :]))
        away = k ^ place[0]
        for spot, plane in enumerate((0, 1, 2, 0, 1, 0)):
            factors[away, spot * wide : (spot + 1) * wide, :] = planes[plane]

    tall = min(height, ROWS)
    for head in range(heads):
        bucket = table[head]
        start = pl.multiple_of(bucket_side(table, head) * HD, HD)
        factor = factors[bucket, :, pl.ds(start, HD)]
        spots = head_spots(table, bucket, slots, layers * slots)
        cols = slice(head * HD, (head + 1) * HD)
        for low in range(0, height, tall):
            rows = slice(low, low + tall)
            value = head_pair(update, rows, spots)
            ortho = jnp.dot(value, factor, preferred_element_type=f32)
            weights[rows, cols] = (master[0, rows, cols] - ortho).astype(bf16)


def lead_weights(table, place, packed, update, master, chunks):
    _, height, width = master.shape
    parts = len(packed)
    slots = width // HD
    return pl.pallas_call(
        functools.partial(lead_kernel, parts=parts, slots=slots, heads=slots // chunks),
        in_specs=[SM, SM] + [VM] * (parts + 2),
        out_specs=[VM, VM],
        out_shape=[
            pltpu.VMEM((height, width // chunks), bf16),
            pltpu.VMEM((parts, 12 * HD, 2 * HD), bf16),
        ],
        compiler_params=pltpu.CompilerParams(vmem_limit_bytes=12 * MIB),
        name="lead",
    )(table, place, *[vmem(p) for p in packed], vmem(update), vmem(master))


def apply_kernel(table, factors, update, master, new_master, *refs, chunks):
    weights = refs[: chunks - 1]
    fresh, sems = refs[chunks - 1 :]
    layers, height, width = master.shape
    slots = width // HD
    tall = min(height, ROWS)
    piece = width // chunks
    parts = factors.shape[0]
    spots = [head_spots(table, bucket, slots, layers * slots) for bucket in range(parts)]
    copies = []
    for i in range(height // tall):
        rows = slice(i * tall, (i + 1) * tall)
        for bucket in range(parts):
            value = head_pair(update, rows, spots[bucket])
            ortho = jnp.dot(value, factors[bucket], preferred_element_type=f32)
            for side, (layer, cols) in enumerate(spots[bucket]):
                part = ortho[:, side * HD : (side + 1) * HD]
                fresh[layer, rows, cols] = master[layer, rows, cols] - part
        copies.append(
            pltpu.make_async_copy(fresh.at[:, rows, :], new_master.at[:, rows, :], sems.at[i])
        )
        copies[-1].start()
        for c in range(1, chunks):
            cols = slice(c * piece, (c + 1) * piece)
            weights[c - 1][rows, :] = fresh[0, rows, cols].astype(bf16)
    for copy in copies:
        copy.wait()


def apply_update(table, factors, update, master, chunks):
    _, height, width = master.shape
    return pl.pallas_call(
        functools.partial(apply_kernel, chunks=chunks),
        in_specs=[SM] + [VM] * 3,
        out_specs=[pl.BlockSpec(memory_space=pl.ANY)] + [VM] * (chunks - 1),
        scratch_shapes=[
            pltpu.VMEM(master.shape, f32),
            pltpu.SemaphoreType.DMA((height // min(height, ROWS),)),
        ],
        out_shape=[jax.ShapeDtypeStruct(master.shape, f32)]
        + [pltpu.VMEM((height, width // chunks), bf16)] * (chunks - 1),
        compiler_params=pltpu.CompilerParams(vmem_limit_bytes=12 * MIB),
        name="apply",
    )(table, vmem(factors), vmem(update), vmem(master))


def norm_kernel(place, *refs, parts, features):
    halves = refs[: 2 * parts]
    packed = refs[2 * parts : 3 * parts]
    gain, out = refs[3 * parts :]
    height, width = halves[0].shape
    high = packed[0].shape[0] - 8
    for k in range(parts):
        inverse = lax.rsqrt(packed[k][high : high + 8, :] / features + rms_epsilon)
        away = k ^ place[0] ^ place[1]
        for side in range(2):
            for low in range(0, height, HD):
                spot = (side * height + low) // HD
                column = jnp.broadcast_to(inverse[spot : spot + 1, :], (HD, HD)).T
                for i in range(parts):

                    @pl.when(away == i)
                    def _():
                        for left in range(0, width, HD):
                            cols = slice(left, left + HD)
                            values = halves[2 * i + side][low : low + HD, cols].astype(f32)
                            out[k, spot * HD : (spot + 1) * HD, cols] = (
                                values * column * gain[:, cols]
                            ).astype(bf16)


def normalise(place, halves, packed, gain, features):
    parts = len(packed)
    height, width = halves[0].shape
    return pl.pallas_call(
        functools.partial(norm_kernel, parts=parts, features=features),
        in_specs=[SM] + [VM] * (3 * parts + 1),
        out_specs=VM,
        out_shape=pltpu.VMEM((parts, 2 * height, width), bf16),
        compiler_params=pltpu.CompilerParams(vmem_limit_bytes=8 * MIB),
        name="normalise",
    )(place, *[vmem(h) for h in halves], *[vmem(p) for p in packed], vmem(gain))


def project_kernel(place, normed, *refs, members, parts):
    weights = refs[:members]
    outs = refs[members : members + parts]
    whole = refs[-1]
    height = weights[0].shape[0]
    for k in range(members):
        start = pl.multiple_of((k ^ place[2]) * height, height)
        whole[pl.ds(start, height), :] = weights[k][...]
    for m in range(parts):
        part = jnp.dot(normed[m], whole[...], preferred_element_type=f32)
        if m == 0:
            outs[m][...] = part
        else:
            encode(outs[m], part)


def encode(out, value):
    height = value.shape[0]
    top = jnp.max(jnp.abs(value), axis=0, keepdims=True)
    power = jnp.ceil(jnp.log2(jnp.maximum(top, LEAST)) - CODE_BITS)
    code = jnp.round(value * jnp.exp2(-power))
    out[0:height, :] = code.astype(jnp.int32).astype(jnp.int16)
    tail = jnp.broadcast_to(power, (CODE_ROWS, value.shape[1]))
    out[height : height + CODE_ROWS, :] = tail.astype(jnp.int32).astype(jnp.int16)


def finish_kernel(*refs, chunks, parts):
    out = refs[-1]
    for c in range(chunks):
        own, *codes = refs[c * parts : (c + 1) * parts]
        height, width = own.shape
        total = own[...]
        for code in codes:
            power = code[height : height + CODE_ROWS, :].astype(jnp.int32).astype(f32)
            value = code[0:height, :].astype(jnp.int32).astype(f32)
            total = total + value * jnp.exp2(power[0:1, :])
        out[:, c * width : (c + 1) * width] = total.astype(bf16)


def finish(pieces):
    chunks = len(pieces)
    parts = len(pieces[0])
    height, width = pieces[0][0].shape
    return pl.pallas_call(
        functools.partial(finish_kernel, chunks=chunks, parts=parts),
        in_specs=[VM] * (chunks * parts),
        out_shape=jax.ShapeDtypeStruct((height, chunks * width), bf16),
        compiler_params=pltpu.CompilerParams(vmem_limit_bytes=8 * MIB),
        name="finish",
    )(*[vmem(p) for piece in pieces for p in piece])


def project(place, normed, weights):
    parts, height, width = normed.shape
    cols = weights[0].shape[1]
    code = pltpu.VMEM((height + CODE_ROWS, cols), jnp.int16)
    return pl.pallas_call(
        functools.partial(project_kernel, members=len(weights), parts=parts),
        in_specs=[SM] + [VM] * (1 + len(weights)),
        out_specs=[VM] * parts,
        out_shape=[pltpu.VMEM((height, cols), f32)] + [code] * (parts - 1),
        scratch_shapes=[pltpu.VMEM((width, cols), bf16)],
        compiler_params=pltpu.CompilerParams(vmem_limit_bytes=8 * MIB),
        name="project",
    )(place, vmem(normed), *[vmem(w) for w in weights])


def after(value, other):
    return lax.optimization_barrier((value, other))[0]


def per_device(master, momentum, gradient, bucket_table, tokens, norm_gain, *, dp, tp):
    _, height, _ = master.shape
    share = tokens.shape[1]
    features = norm_gain.shape[0]
    count = bucket_table.shape[1]
    parts = tp
    members = dp // parts
    assert count // 2 == parts and share * tp == features and height * dp == features
    mine = lax.axis_index("dp")
    column = lax.axis_index("tensor")
    row = mine // members
    place = jnp.stack([row, column, mine % members]).astype(jnp.int32)
    table = bucket_table[0]

    def swap_dp(value, bits):
        return lax.ppermute(value, "dp", [(i, i ^ bits) for i in range(dp)])

    def swap_tensor(value, bits):
        return lax.ppermute(value, "tensor", [(i, i ^ bits) for i in range(tp)])

    half = tokens.shape[0] // 2
    flips = (0, tp // 2)
    near = lax.slice_in_dim(tokens, 0, half, axis=0)
    far = swap_tensor(lax.slice_in_dim(tokens, half, 2 * half, axis=0), tp // 2)

    def turn(value, flip):
        pairs = []
        for q in range(parts):
            for r in range(members):
                for j in range(tp):
                    target = ((j ^ flip) * members + r) * tp + (q ^ flip)
                    pairs.append(((q * members + r) * tp + j, target))
        return lax.ppermute(value, ("dp", "tensor"), pairs)

    new_momentum, update, *grams = local_grams(table, place, momentum, gradient, parts)

    local_f = tokens.astype(f32)
    sums = jnp.sum(local_f * local_f, axis=1)
    bits = tp // 2
    while bits:
        sums = sums + swap_tensor(sums, bits)
        bits //= 2

    sent = [turn(after(value, grams[0]), flip) for value, flip in zip((near, far), flips)]
    total = grams[0]
    for k in range(1, parts):
        total = total + swap_dp(grams[k], k * members)
    pieces = [total]
    bits = 1
    while bits < members:
        pieces = [sum(pieces), swap_dp(sum(pieces), bits)]
        bits *= 2
    step_scale = learn_rate * math.sqrt(max(1.0, features / (2.0 * HD)))
    own = series(pieces, sums.reshape(-1, HD), step_scale)

    packed = [own] + [swap_dp(own, k * members) for k in range(1, parts)]
    lead, factors = lead_weights(table, place, packed, update, master, CHUNKS)
    new_master, *others = apply_update(table, factors, update, master, CHUNKS)

    held = {(0, 0): after(sent[0], own), (1, tp // 2): after(sent[1], own)}
    bits = tp // 2
    while bits:
        fresh = {}
        for (side, offset), value in held.items():
            if bits < tp // 2:
                value = after(value, others[0] if others else lead)
            fresh[(side, offset ^ bits)] = swap_tensor(value, bits)
        held.update(fresh)
        bits //= 2
    halves = [held[(side, offset)] for offset in range(parts) for side in range(2)]
    gain = lax.dynamic_slice_in_dim(norm_gain, row * share, share, 0)[None, :]
    normed = normalise(place, halves, packed, gain, features)

    pieces = []
    for piece in [lead] + others:
        gathered = [piece] + [swap_dp(piece, k) for k in range(1, members)]
        partial = project(place, normed, gathered)
        sums_of = [swap_dp(partial[k], k * members) for k in range(1, parts)]
        pieces.append([partial[0]] + sums_of)
    return (new_master, new_momentum, finish(pieces))


def solution(mesh):
    placed = (
        P(None, "dp", "tensor"),
        P(None, "dp", "tensor"),
        P(None, "dp", "tensor"),
        P("tensor", None),
        P("dp", "tensor"),
        P(),
    )

    def step(*args):
        return per_device(*args, dp=mesh.shape["dp"], tp=mesh.shape["tensor"])

    return jax.shard_map(
        step,
        mesh=mesh,
        in_specs=placed,
        out_specs=(P(None, "dp", "tensor"), P(None, "dp", "tensor"), P("dp", "tensor")),
        check_vma=False,
    )
```

profile of v0, /device:TPU:0, one launch (start us, length us, event | category | flops | bytes accessed | tf_op | source)
XLA Modules:
  0.0 123.4 jit_solution(12469240771819418700)
XLA Ops:
  0.6 1.3 %fusion = (bf16[128,2048]{1,0:T(8,128)(2,1)S(1)}, bf16[128,2048]{1,0:T(8,128)(2,1)S(1)}) fusion(bf16[256,2048]{1,0:T(8,128)(2,1)} %param.10), kind=kLoop, calls=%fused_computation.4 | loop fusion | bytes 2097152 | tf_op jit(solution)/shard_map/slice | solution.py:478
  1.9 3.0 %collective-permute-start.10 = (bf16[128,2048]{1,0:T(8,128)(2,1)S(1)}, bf16[128,2048]{1,0:T(8,128)(2,1)S(1)}, u32[]{:S(2)}, u32[]{:S(2)}) collective-permute-start(bf16[128,2048]{1,0:T(8,128)(2,1)S(1)} %get-tuple-element.55), channel_id=1, source_target_pairs={{0,2},{1,3},{2,0},{3,1},{4,6},{5,7},{6,4},{7,5},{8,10},{9,11},{10,... | collective-permute-start | bytes 1572872 | tf_op jit(solution)/shard_map/ppermute | solution.py:473
  5.7 12.4 %grams.1 = (f32[2,1024,512]{2,1,0:T(8,128)}, f32[2,1024,512]{2,1,0:T(8,128)S(1)}, f32[264,128]{1,0:T(8,128)S(1)}, f32[264,128]{1,0:T(8,128)S(1)}, f32[264,128]{1,0:T(8,128)S(1)}, /*index=5*/f32[264,128]{1,0:T(8,128)S(1)}) custom-call(s32[8]{0:T(128)S(1)} %bitcast.8, s32[3]{0:T(128)S(1)} %pad_add_fusion.place, f32[2,1024,512]{2,1,0:T(8,128)} %momentum.1, ...), custom_call_target="tpu_custom_call" | custom-call | tf_op jit(solution)/shard_map/grams/pallas_call | solution.py:165
  18.0 3.6 %collective-permute-start.2 = (f32[264,128]{1,0:T(8,128)S(1)}, f32[264,128]{1,0:T(8,128)S(1)}, u32[]{:S(2)}, u32[]{:S(2)}) collective-permute-start(f32[264,128]{1,0:T(8,128)S(1)} %get-tuple-element.32), channel_id=1, source_target_pairs={{0,24},{4,28},{8,16},{12,20},{16,8},{20,12},{24,0},{28,4},{1,25},{... | collective-permute-start | bytes 405512 | tf_op jit(solution)/shard_map/ppermute | solution.py:470
  23.8 2.6 %collective-permute-done.4 = f32[256]{0:T(256)S(1)} collective-permute-done((f32[256]{0:T(256)S(1)}, f32[256]{0:T(256)S(1)}, u32[]{:S(2)}, u32[]{:S(2)}) %collective-permute-start.4) | collective-permute-done | bytes 1056 | tf_op jit(solution)/shard_map/ppermute | solution.py:473
  26.4 4.2 %collective-permute-start.11 = (bf16[128,2048]{1,0:T(8,128)(2,1)S(1)}, bf16[128,2048]{1,0:T(8,128)(2,1)}, u32[]{:S(2)}, u32[]{:S(2)}) collective-permute-start(bf16[128,2048]{1,0:T(8,128)(2,1)S(1)} %collective-permute-done.10), channel_id=1, source_target_pairs={{0,18},{1,26},{2,2},{3,10},{4,22},{5,30},{6,6},{7,14},{8,19},{9,27... | collective-permute-start | bytes 1572872 | tf_op jit(solution)/shard_map/ppermute | solution.py:487
  30.6 1.6 %collective-permute-start.5 = (f32[256]{0:T(256)S(1)}, f32[256]{0:T(256)S(1)}, u32[]{:S(2)}, u32[]{:S(2)}) collective-permute-start(f32[256]{0:T(256)S(1)} %add.27), channel_id=1, source_target_pairs={{0,1},{1,0},{2,3},{3,2},{4,5},{5,4},{6,7},{7,6},{8,9},{9,8},{10,11... | collective-permute-start | bytes 3080 | tf_op jit(solution)/shard_map/ppermute | solution.py:473
  32.2 12.7 %collective-permute-done.1 = f32[264,128]{1,0:T(8,128)S(1)} collective-permute-done((f32[264,128]{1,0:T(8,128)S(1)}, f32[264,128]{1,0:T(8,128)S(1)}, u32[]{:S(2)}, u32[]{:S(2)}) %collective-permute-start.1) | collective-permute-done | bytes 135200 | tf_op jit(solution)/shard_map/ppermute | solution.py:470
  45.0 1.6 %collective-permute-start.3 = (f32[264,128]{1,0:T(8,128)S(1)}, f32[264,128]{1,0:T(8,128)S(1)}, u32[]{:S(2)}, u32[]{:S(2)}) collective-permute-start(f32[264,128]{1,0:T(8,128)S(1)} %add_add_fusion.refs_0_), channel_id=1, source_target_pairs={{0,4},{4,0},{8,12},{12,8},{16,20},{20,16},{24,28},{28,24},{1,5},{5... | collective-permute-start | bytes 405512 | tf_op jit(solution)/shard_map/ppermute | solution.py:470
  46.6 3.5 %collective-permute-done.3.refs_1_ = f32[264,128]{1,0:T(8,128)S(1)} collective-permute-done((f32[264,128]{1,0:T(8,128)S(1)}, f32[264,128]{1,0:T(8,128)S(1)}, u32[]{:S(2)}, u32[]{:S(2)}) %collective-permute-start.3) | collective-permute-done | bytes 135200 | tf_op jit(solution)/shard_map/ppermute | solution.py:470
  50.1 4.3 %series.1.refs_0_.refs_8_ = f32[272,128]{1,0:T(8,128)S(1)} custom-call(f32[264,128]{1,0:T(8,128)S(1)} %add_add_fusion.refs_0_, f32[264,128]{1,0:T(8,128)S(1)} %collective-permute-done.3.refs_1_, f32[2,128]{1,0:T(2,128)S(1)} %add_bitcast_fusion.refs_2_), custom_call_target="tpu_custom_call" | custom-call | tf_op jit(solution)/shard_map/series/pallas_call | solution.py:227
  54.5 3.9 %collective-permute-start.15 = (bf16[128,2048]{1,0:T(8,128)(2,1)S(1)}, bf16[128,2048]{1,0:T(8,128)(2,1)}, u32[]{:S(2)}, u32[]{:S(2)}) collective-permute-start(bf16[128,2048]{1,0:T(8,128)(2,1)S(1)} %collective-permute-done.9.refs_0_), channel_id=1, source_target_pairs={{0,2},{1,3},{2,0},{3,1},{4,6},{5,7},{6,4},{7,5},{8,10},{9,11},{10,... | collective-permute-start | bytes 1572872 | tf_op jit(solution)/shard_map/ppermute | solution.py:473
  58.8 2.0 %collective-permute-start.12 = (bf16[128,2048]{1,0:T(8,128)(2,1)}, bf16[128,2048]{1,0:T(8,128)(2,1)}, u32[]{:S(2)}, u32[]{:S(2)}) collective-permute-start(bf16[128,2048]{1,0:T(8,128)(2,1)} %collective-permute-done.11.refs_5_), channel_id=1, source_target_pairs={{0,2},{1,3},{2,0},{3,1},{4,6},{5,7},{6,4},{7,5},{8,10},{9,11},{10,... | collective-permute-start | bytes 1572872 | tf_op jit(solution)/shard_map/ppermute | solution.py:473
  61.6 4.5 %collective-permute-done.7.refs_2_.refs_10_ = f32[272,128]{1,0:T(8,128)S(1)} collective-permute-done((f32[272,128]{1,0:T(8,128)S(1)}, f32[272,128]{1,0:T(8,128)S(1)}, u32[]{:S(2)}, u32[]{:S(2)}) %collective-permute-start.7) | collective-permute-done | bytes 139296 | tf_op jit(solution)/shard_map/ppermute | solution.py:470
  66.2 2.9 %lead.1 = (bf16[1024,256]{1,0:T(8,128)(2,1)S(1)}, bf16[4,1536,256]{2,1,0:T(8,128)(2,1)S(1)}) custom-call(s32[8]{0:T(128)S(1)} %bitcast.9, s32[3]{0:T(128)S(1)} %pad_add_fusion.place, f32[272,128]{1,0:T(8,128)S(1)} %series.1.refs_0_.refs_8_, f32[272,128]{1,0:T(8,128)S(1)} %collective-permute-done.6.refs_1_.refs_9_, ...), custom_call_target="tpu_custom_call" | custom-call | tf_op jit(solution)/shard_map/lead/pallas_call | solution.py:287
  69.0 6.0 %apply.1 = (f32[2,1024,512]{2,1,0:T(8,128)}, bf16[1024,256]{1,0:T(8,128)(2,1)S(1)}) custom-call(s32[8]{0:T(128)S(1)} %bitcast.10, bf16[4,1536,256]{2,1,0:T(8,128)(2,1)S(1)} %get-tuple-element.34.factors, f32[2,1024,512]{2,1,0:T(8,128)S(1)} %get-tuple-element.33.refs_4_.update, f32[2,1024,512]{2,1,0:T(8,128)S(1)} %copy-done), custom_call_target="tpu_custom_call" | custom-call | tf_op jit(solution)/shard_map/apply/pallas_call | solution.py:331
  75.7 3.1 %collective-permute-done.12.refs_1_ = bf16[128,2048]{1,0:T(8,128)(2,1)} collective-permute-done((bf16[128,2048]{1,0:T(8,128)(2,1)}, bf16[128,2048]{1,0:T(8,128)(2,1)}, u32[]{:S(2)}, u32[]{:S(2)}) %collective-permute-start.12) | collective-permute-done | bytes 524320 | tf_op jit(solution)/shard_map/ppermute | solution.py:473
  78.8 1.5 %collective-permute-start.18 = (bf16[1024,256]{1,0:T(8,128)(2,1)S(1)}, bf16[1024,256]{1,0:T(8,128)(2,1)S(1)}, u32[]{:S(2)}, u32[]{:S(2)}) collective-permute-start(bf16[1024,256]{1,0:T(8,128)(2,1)S(1)} %get-tuple-element.46.refs_0_), channel_id=1, source_target_pairs={{0,4},{4,0},{8,12},{12,8},{16,20},{20,16},{24,28},{28,24},{1,5},{5... | collective-permute-start | bytes 1572872 | tf_op jit(solution)/shard_map/ppermute | solution.py:470
  80.4 0.8 copy-done.1
  82.4 1.0 copy-done.2
  83.4 4.1 %normalise.1.normed = bf16[4,256,2048]{2,1,0:T(8,128)(2,1)S(1)} custom-call(s32[3]{0:T(128)S(1)} %pad_add_fusion.place, bf16[128,2048]{1,0:T(8,128)(2,1)S(1)} %collective-permute-done.9.refs_0_, bf16[128,2048]{1,0:T(8,128)(2,1)} %collective-permute-done.12.refs_1_, bf16[128,2048]{1,0:T(8,128)(2,1)S(1)} %copy-done.2, ...), custom_call_target="tpu_custom_call" | custom-call | tf_op jit(solution)/shard_map/normalise/pallas_call | solution.py:374
  87.5 6.1 %collective-permute-done.18.refs_1_ = bf16[1024,256]{1,0:T(8,128)(2,1)S(1)} collective-permute-done((bf16[1024,256]{1,0:T(8,128)(2,1)S(1)}, bf16[1024,256]{1,0:T(8,128)(2,1)S(1)}, u32[]{:S(2)}, u32[]{:S(2)}) %collective-permute-start.18) | collective-permute-done | bytes 524320 | tf_op jit(solution)/shard_map/ppermute | solution.py:470
  93.6 2.0 %project.2 = (f32[256,256]{1,0:T(8,128)S(1)}, s16[272,256]{1,0:T(8,128)(2,1)S(1)}, s16[272,256]{1,0:T(8,128)(2,1)S(1)}, s16[272,256]{1,0:T(8,128)(2,1)S(1)}) custom-call(s32[3]{0:T(128)S(1)} %pad_add_fusion.place, bf16[4,256,2048]{2,1,0:T(8,128)(2,1)S(1)} %normalise.1.normed, bf16[1024,256]{1,0:T(8,128)(2,1)S(1)} %get-tuple-element.46.refs_0_, ...), custom_call_target="tpu_custom_call" | custom-call | tf_op jit(solution)/shard_map/project/pallas_call | solution.py:440
  96.0 4.3 %collective-permute-start.20 = (s16[272,256]{1,0:T(8,128)(2,1)S(1)}, s16[272,256]{1,0:T(8,128)(2,1)S(1)}, u32[]{:S(2)}, u32[]{:S(2)}) collective-permute-start(s16[272,256]{1,0:T(8,128)(2,1)S(1)} %get-tuple-element.49), channel_id=1, source_target_pairs={{0,16},{4,20},{8,24},{12,28},{16,0},{20,4},{24,8},{28,12},{1,17},{... | collective-permute-start | bytes 417800 | tf_op jit(solution)/shard_map/ppermute | solution.py:470
  100.3 1.4 %collective-permute-start.21 = (s16[272,256]{1,0:T(8,128)(2,1)S(1)}, s16[272,256]{1,0:T(8,128)(2,1)S(1)}, u32[]{:S(2)}, u32[]{:S(2)}) collective-permute-start(s16[272,256]{1,0:T(8,128)(2,1)S(1)} %get-tuple-element.50), channel_id=1, source_target_pairs={{0,24},{4,28},{8,16},{12,20},{16,8},{20,12},{24,0},{28,4},{1,25},{... | collective-permute-start | bytes 417800 | tf_op jit(solution)/shard_map/ppermute | solution.py:470
  101.7 2.7 %collective-permute-done.22.refs_1_ = bf16[1024,256]{1,0:T(8,128)(2,1)S(1)} collective-permute-done((bf16[1024,256]{1,0:T(8,128)(2,1)S(1)}, bf16[1024,256]{1,0:T(8,128)(2,1)S(1)}, u32[]{:S(2)}, u32[]{:S(2)}) %collective-permute-start.22) | collective-permute-done | bytes 524320 | tf_op jit(solution)/shard_map/ppermute | solution.py:470
  104.4 2.0 %project.3 = (f32[256,256]{1,0:T(8,128)S(1)}, s16[272,256]{1,0:T(8,128)(2,1)S(1)}, s16[272,256]{1,0:T(8,128)(2,1)S(1)}, s16[272,256]{1,0:T(8,128)(2,1)S(1)}) custom-call(s32[3]{0:T(128)S(1)} %pad_add_fusion.place, bf16[4,256,2048]{2,1,0:T(8,128)(2,1)S(1)} %normalise.1.normed, bf16[1024,256]{1,0:T(8,128)(2,1)S(1)} %get-tuple-element.41.refs_0_, ...), custom_call_target="tpu_custom_call" | custom-call | tf_op jit(solution)/shard_map/project/pallas_call | solution.py:440
  106.8 4.2 %collective-permute-start.24 = (s16[272,256]{1,0:T(8,128)(2,1)S(1)}, s16[272,256]{1,0:T(8,128)(2,1)S(1)}, u32[]{:S(2)}, u32[]{:S(2)}) collective-permute-start(s16[272,256]{1,0:T(8,128)(2,1)S(1)} %get-tuple-element.53), channel_id=1, source_target_pairs={{0,16},{4,20},{8,24},{12,28},{16,0},{20,4},{24,8},{28,12},{1,17},{... | collective-permute-start | bytes 417800 | tf_op jit(solution)/shard_map/ppermute | solution.py:470
  111.0 1.0 collective-permute-start.25
  112.0 2.4 %collective-permute-done.23.refs_5_ = s16[272,256]{1,0:T(8,128)(2,1)S(1)} collective-permute-done((s16[272,256]{1,0:T(8,128)(2,1)S(1)}, s16[272,256]{1,0:T(8,128)(2,1)S(1)}, u32[]{:S(2)}, u32[]{:S(2)}) %collective-permute-start.23) | collective-permute-done | bytes 139296 | tf_op jit(solution)/shard_map/ppermute | solution.py:470
  114.4 8.0 %collective-permute-done.24.refs_6_ = s16[272,256]{1,0:T(8,128)(2,1)S(1)} collective-permute-done((s16[272,256]{1,0:T(8,128)(2,1)S(1)}, s16[272,256]{1,0:T(8,128)(2,1)S(1)}, u32[]{:S(2)}, u32[]{:S(2)}) %collective-permute-start.24) | collective-permute-done | bytes 139296 | tf_op jit(solution)/shard_map/ppermute | solution.py:470
  122.4 0.9 finish.1
  (45 shorter events, 6.8 us)
Async XLA Ops:
  1.9 21.2 %collective-permute-start.10 = (bf16[128,2048]{1,0:T(8,128)(2,1)S(1)}, bf16[128,2048]{1,0:T(8,128)(2,1)S(1)}, u32[]{:S(2)}, u32[]{:S(2)}) collective-permute-start(bf16[128,2048]{1,0:T(8,128)(2,1)S(1)} %get-tuple-element.55), channel_id=1, source_target_pairs={{0,2},{1,3},{2,0},{3,1},{4,6},{5,7},{6,4},{7,5},{8,10},{9,11},{10,... | collective-permute-start | bytes 1572872 | tf_op jit(solution)/shard_map/ppermute | solution.py:473
  5.0 0.7 copy-start.3
  5.7 16.8 %copy-start.4 = (bf16[256,2048]{1,0:T(8,128)(2,1)S(1)}, bf16[256,2048]{1,0:T(8,128)(2,1)}, u32[]{:S(2)}) copy-start(bf16[256,2048]{1,0:T(8,128)(2,1)} %param.10) | copy-start | bytes 3145732
  5.7 60.5 %copy-start = (f32[2,1024,512]{2,1,0:T(8,128)S(1)}, f32[2,1024,512]{2,1,0:T(8,128)}, u32[]{:S(2)}) copy-start(f32[2,1024,512]{2,1,0:T(8,128)} %master.1) | copy-start | bytes 12582916
  18.0 12.5 %collective-permute-start.2 = (f32[264,128]{1,0:T(8,128)S(1)}, f32[264,128]{1,0:T(8,128)S(1)}, u32[]{:S(2)}, u32[]{:S(2)}) collective-permute-start(f32[264,128]{1,0:T(8,128)S(1)} %get-tuple-element.32), channel_id=1, source_target_pairs={{0,24},{4,28},{8,16},{12,20},{16,8},{20,12},{24,0},{28,4},{1,25},{... | collective-permute-start | bytes 405512 | tf_op jit(solution)/shard_map/ppermute | solution.py:470
  21.6 23.3 %collective-permute-start.1 = (f32[264,128]{1,0:T(8,128)S(1)}, f32[264,128]{1,0:T(8,128)S(1)}, u32[]{:S(2)}, u32[]{:S(2)}) collective-permute-start(f32[264,128]{1,0:T(8,128)S(1)} %get-tuple-element.31), channel_id=1, source_target_pairs={{0,16},{4,20},{8,24},{12,28},{16,0},{20,4},{24,8},{28,12},{1,17},{... | collective-permute-start | bytes 405512 | tf_op jit(solution)/shard_map/ppermute | solution.py:470
  21.6 23.3 %collective-permute-start = (f32[264,128]{1,0:T(8,128)S(1)}, f32[264,128]{1,0:T(8,128)S(1)}, u32[]{:S(2)}, u32[]{:S(2)}) collective-permute-start(f32[264,128]{1,0:T(8,128)S(1)} %get-tuple-element.30), channel_id=1, source_target_pairs={{0,8},{4,12},{8,0},{12,4},{16,24},{20,28},{24,16},{28,20},{1,9},{5... | collective-permute-start | bytes 405512 | tf_op jit(solution)/shard_map/ppermute | solution.py:470
  22.7 3.6 %collective-permute-start.4 = (f32[256]{0:T(256)S(1)}, f32[256]{0:T(256)S(1)}, u32[]{:S(2)}, u32[]{:S(2)}) collective-permute-start(f32[256]{0:T(256)S(1)} %multiply_reduce_fusion), channel_id=1, source_target_pairs={{0,2},{1,3},{2,0},{3,1},{4,6},{5,7},{6,4},{7,5},{8,10},{9,11},{10,... | collective-permute-start | bytes 3080 | tf_op jit(solution)/shard_map/ppermute | solution.py:473
  23.1 31.4 %collective-permute-start.9 = (bf16[128,2048]{1,0:T(8,128)(2,1)S(1)}, bf16[128,2048]{1,0:T(8,128)(2,1)S(1)}, u32[]{:S(2)}, u32[]{:S(2)}) collective-permute-start(bf16[128,2048]{1,0:T(8,128)(2,1)S(1)} %get-tuple-element.37), channel_id=1, source_target_pairs={{0,0},{1,8},{2,16},{3,24},{4,4},{5,12},{6,20},{7,28},{8,1},{9,9},{... | collective-permute-start | bytes 1572872 | tf_op jit(solution)/shard_map/ppermute | solution.py:487
  26.4 32.5 %collective-permute-start.11 = (bf16[128,2048]{1,0:T(8,128)(2,1)S(1)}, bf16[128,2048]{1,0:T(8,128)(2,1)}, u32[]{:S(2)}, u32[]{:S(2)}) collective-permute-start(bf16[128,2048]{1,0:T(8,128)(2,1)S(1)} %collective-permute-done.10), channel_id=1, source_target_pairs={{0,18},{1,26},{2,2},{3,10},{4,22},{5,30},{6,6},{7,14},{8,19},{9,27... | collective-permute-start | bytes 1572872 | tf_op jit(solution)/shard_map/ppermute | solution.py:487
  30.6 16.0 %collective-permute-start.5 = (f32[256]{0:T(256)S(1)}, f32[256]{0:T(256)S(1)}, u32[]{:S(2)}, u32[]{:S(2)}) collective-permute-start(f32[256]{0:T(256)S(1)} %add.27), channel_id=1, source_target_pairs={{0,1},{1,0},{2,3},{3,2},{4,5},{5,4},{6,7},{7,6},{8,9},{9,8},{10,11... | collective-permute-start | bytes 3080 | tf_op jit(solution)/shard_map/ppermute | solution.py:473
  45.0 5.1 %collective-permute-start.3 = (f32[264,128]{1,0:T(8,128)S(1)}, f32[264,128]{1,0:T(8,128)S(1)}, u32[]{:S(2)}, u32[]{:S(2)}) collective-permute-start(f32[264,128]{1,0:T(8,128)S(1)} %add_add_fusion.refs_0_), channel_id=1, source_target_pairs={{0,4},{4,0},{8,12},{12,8},{16,20},{20,16},{24,28},{28,24},{1,5},{5... | collective-permute-start | bytes 405512 | tf_op jit(solution)/shard_map/ppermute | solution.py:470
  54.4 7.3 %collective-permute-start.6 = (f32[272,128]{1,0:T(8,128)S(1)}, f32[272,128]{1,0:T(8,128)S(1)}, u32[]{:S(2)}, u32[]{:S(2)}) collective-permute-start(f32[272,128]{1,0:T(8,128)S(1)} %series.1.refs_0_.refs_8_), channel_id=1, source_target_pairs={{0,8},{4,12},{8,0},{12,4},{16,24},{20,28},{24,16},{28,20},{1,9},{5... | collective-permute-start | bytes 417800 | tf_op jit(solution)/shard_map/ppermute | solution.py:470
  54.5 11.7 %collective-permute-start.7 = (f32[272,128]{1,0:T(8,128)S(1)}, f32[272,128]{1,0:T(8,128)S(1)}, u32[]{:S(2)}, u32[]{:S(2)}) collective-permute-start(f32[272,128]{1,0:T(8,128)S(1)} %series.1.refs_0_.refs_8_), channel_id=1, source_target_pairs={{0,16},{4,20},{8,24},{12,28},{16,0},{20,4},{24,8},{28,12},{1,17},{... | collective-permute-start | bytes 417800 | tf_op jit(solution)/shard_map/ppermute | solution.py:470
  54.5 20.6 %collective-permute-start.15 = (bf16[128,2048]{1,0:T(8,128)(2,1)S(1)}, bf16[128,2048]{1,0:T(8,128)(2,1)}, u32[]{:S(2)}, u32[]{:S(2)}) collective-permute-start(bf16[128,2048]{1,0:T(8,128)(2,1)S(1)} %collective-permute-done.9.refs_0_), channel_id=1, source_target_pairs={{0,2},{1,3},{2,0},{3,1},{4,6},{5,7},{6,4},{7,5},{8,10},{9,11},{10,... | collective-permute-start | bytes 1572872 | tf_op jit(solution)/shard_map/ppermute | solution.py:473
  58.5 7.7 %collective-permute-start.8 = (f32[272,128]{1,0:T(8,128)S(1)}, f32[272,128]{1,0:T(8,128)S(1)}, u32[]{:S(2)}, u32[]{:S(2)}) collective-permute-start(f32[272,128]{1,0:T(8,128)S(1)} %series.1.refs_0_.refs_8_), channel_id=1, source_target_pairs={{0,24},{4,28},{8,16},{12,20},{16,8},{20,12},{24,0},{28,4},{1,25},{... | collective-permute-start | bytes 417800 | tf_op jit(solution)/shard_map/ppermute | solution.py:470
  58.8 20.0 %collective-permute-start.12 = (bf16[128,2048]{1,0:T(8,128)(2,1)}, bf16[128,2048]{1,0:T(8,128)(2,1)}, u32[]{:S(2)}, u32[]{:S(2)}) collective-permute-start(bf16[128,2048]{1,0:T(8,128)(2,1)} %collective-permute-done.11.refs_5_), channel_id=1, source_target_pairs={{0,2},{1,3},{2,0},{3,1},{4,6},{5,7},{6,4},{7,5},{8,10},{9,11},{10,... | collective-permute-start | bytes 1572872 | tf_op jit(solution)/shard_map/ppermute | solution.py:473
  75.1 5.3 %collective-permute-start.13 = (bf16[128,2048]{1,0:T(8,128)(2,1)S(1)}, bf16[128,2048]{1,0:T(8,128)(2,1)S(1)}, u32[]{:S(2)}, u32[]{:S(2)}) collective-permute-start(bf16[128,2048]{1,0:T(8,128)(2,1)S(1)} %collective-permute-done.9.refs_0_), channel_id=1, source_target_pairs={{0,1},{1,0},{2,3},{3,2},{4,5},{5,4},{6,7},{7,6},{8,9},{9,8},{10,11... | collective-permute-start | bytes 1572872 | tf_op jit(solution)/shard_map/ppermute | solution.py:473
  75.1 7.2 %collective-permute-start.16 = (bf16[128,2048]{1,0:T(8,128)(2,1)}, bf16[128,2048]{1,0:T(8,128)(2,1)}, u32[]{:S(2)}, u32[]{:S(2)}) collective-permute-start(bf16[128,2048]{1,0:T(8,128)(2,1)} %collective-permute-done.15.refs_4_), channel_id=1, source_target_pairs={{0,1},{1,0},{2,3},{3,2},{4,5},{5,4},{6,7},{7,6},{8,9},{9,8},{10,11... | collective-permute-start | bytes 1572872 | tf_op jit(solution)/shard_map/ppermute | solution.py:473
  75.6 6.7 %collective-permute-start.17 = (bf16[128,2048]{1,0:T(8,128)(2,1)}, bf16[128,2048]{1,0:T(8,128)(2,1)}, u32[]{:S(2)}, u32[]{:S(2)}) collective-permute-start(bf16[128,2048]{1,0:T(8,128)(2,1)} %collective-permute-done.11.refs_5_), channel_id=1, source_target_pairs={{0,1},{1,0},{2,3},{3,2},{4,5},{5,4},{6,7},{7,6},{8,9},{9,8},{10,11... | collective-permute-start | bytes 1572872 | tf_op jit(solution)/shard_map/ppermute | solution.py:473
  78.8 3.5 %collective-permute-start.14 = (bf16[128,2048]{1,0:T(8,128)(2,1)}, bf16[128,2048]{1,0:T(8,128)(2,1)}, u32[]{:S(2)}, u32[]{:S(2)}) collective-permute-start(bf16[128,2048]{1,0:T(8,128)(2,1)} %collective-permute-done.12.refs_1_), channel_id=1, source_target_pairs={{0,1},{1,0},{2,3},{3,2},{4,5},{5,4},{6,7},{7,6},{8,9},{9,8},{10,11... | collective-permute-start | bytes 1572872 | tf_op jit(solution)/shard_map/ppermute | solution.py:473
  78.8 14.8 %collective-permute-start.18 = (bf16[1024,256]{1,0:T(8,128)(2,1)S(1)}, bf16[1024,256]{1,0:T(8,128)(2,1)S(1)}, u32[]{:S(2)}, u32[]{:S(2)}) collective-permute-start(bf16[1024,256]{1,0:T(8,128)(2,1)S(1)} %get-tuple-element.46.refs_0_), channel_id=1, source_target_pairs={{0,4},{4,0},{8,12},{12,8},{16,20},{20,16},{24,28},{28,24},{1,5},{5... | collective-permute-start | bytes 1572872 | tf_op jit(solution)/shard_map/ppermute | solution.py:470
  80.4 0.8 copy-start.1
  81.2 23.2 %collective-permute-start.22 = (bf16[1024,256]{1,0:T(8,128)(2,1)S(1)}, bf16[1024,256]{1,0:T(8,128)(2,1)S(1)}, u32[]{:S(2)}, u32[]{:S(2)}) collective-permute-start(bf16[1024,256]{1,0:T(8,128)(2,1)S(1)} %get-tuple-element.41.refs_0_), channel_id=1, source_target_pairs={{0,4},{4,0},{8,12},{12,8},{16,20},{20,16},{24,28},{28,24},{1,5},{5... | collective-permute-start | bytes 1572872 | tf_op jit(solution)/shard_map/ppermute | solution.py:470
  82.4 1.0 copy-start.2
  95.6 15.3 %collective-permute-start.19 = (s16[272,256]{1,0:T(8,128)(2,1)S(1)}, s16[272,256]{1,0:T(8,128)(2,1)S(1)}, u32[]{:S(2)}, u32[]{:S(2)}) collective-permute-start(s16[272,256]{1,0:T(8,128)(2,1)S(1)} %get-tuple-element.48), channel_id=1, source_target_pairs={{0,8},{4,12},{8,0},{12,4},{16,24},{20,28},{24,16},{28,20},{1,9},{5... | collective-permute-start | bytes 417800 | tf_op jit(solution)/shard_map/ppermute | solution.py:470
  96.0 16.0 %collective-permute-start.20 = (s16[272,256]{1,0:T(8,128)(2,1)S(1)}, s16[272,256]{1,0:T(8,128)(2,1)S(1)}, u32[]{:S(2)}, u32[]{:S(2)}) collective-permute-start(s16[272,256]{1,0:T(8,128)(2,1)S(1)} %get-tuple-element.49), channel_id=1, source_target_pairs={{0,16},{4,20},{8,24},{12,28},{16,0},{20,4},{24,8},{28,12},{1,17},{... | collective-permute-start | bytes 417800 | tf_op jit(solution)/shard_map/ppermute | solution.py:470
  100.3 11.7 %collective-permute-start.21 = (s16[272,256]{1,0:T(8,128)(2,1)S(1)}, s16[272,256]{1,0:T(8,128)(2,1)S(1)}, u32[]{:S(2)}, u32[]{:S(2)}) collective-permute-start(s16[272,256]{1,0:T(8,128)(2,1)S(1)} %get-tuple-element.50), channel_id=1, source_target_pairs={{0,24},{4,28},{8,16},{12,20},{16,8},{20,12},{24,0},{28,4},{1,25},{... | collective-permute-start | bytes 417800 | tf_op jit(solution)/shard_map/ppermute | solution.py:470
  106.4 8.0 %collective-permute-start.23 = (s16[272,256]{1,0:T(8,128)(2,1)S(1)}, s16[272,256]{1,0:T(8,128)(2,1)S(1)}, u32[]{:S(2)}, u32[]{:S(2)}) collective-permute-start(s16[272,256]{1,0:T(8,128)(2,1)S(1)} %get-tuple-element.52), channel_id=1, source_target_pairs={{0,8},{4,12},{8,0},{12,4},{16,24},{20,28},{24,16},{28,20},{1,9},{5... | collective-permute-start | bytes 417800 | tf_op jit(solution)/shard_map/ppermute | solution.py:470
  106.8 15.7 %collective-permute-start.24 = (s16[272,256]{1,0:T(8,128)(2,1)S(1)}, s16[272,256]{1,0:T(8,128)(2,1)S(1)}, u32[]{:S(2)}, u32[]{:S(2)}) collective-permute-start(s16[272,256]{1,0:T(8,128)(2,1)S(1)} %get-tuple-element.53), channel_id=1, source_target_pairs={{0,16},{4,20},{8,24},{12,28},{16,0},{20,4},{24,8},{28,12},{1,17},{... | collective-permute-start | bytes 417800 | tf_op jit(solution)/shard_map/ppermute | solution.py:470
  111.0 11.5 %collective-permute-start.25 = (s16[272,256]{1,0:T(8,128)(2,1)S(1)}, s16[272,256]{1,0:T(8,128)(2,1)S(1)}, u32[]{:S(2)}, u32[]{:S(2)}) collective-permute-start(s16[272,256]{1,0:T(8,128)(2,1)S(1)} %get-tuple-element.54), channel_id=1, source_target_pairs={{0,24},{4,28},{8,16},{12,20},{16,8},{20,12},{24,0},{28,4},{1,25},{... | collective-permute-start | bytes 417800 | tf_op jit(solution)/shard_map/ppermute | solution.py:470
where the time goes:
time: 124 us; the launch traced here: 123 us
  waiting for transfers between devices  46.5 us (38%)
  starting transfers between devices  36.7 us (30%)
  Pallas kernels  34.5 us (28%)
  local copies, waits for them, and re-layouts  4.47 us (4%)
    ppermute x15, waiting for transfers between devices, swap_dp(): return lax.ppermute(value, 'dp', [(i, i ^ bits) for i in range(dp)])  40.8 us
    ppermute x15, starting transfers between devices, swap_dp(): return lax.ppermute(value, 'dp', [(i, i ^ bits) for i in range(dp)])  20.2 us
    pallas_call x1, Pallas kernels, local_grams(): pl.pallas_call(functools.partial(gram_kernel, parts=parts, slots=slots),...  12.4 us
    ppermute x9, starting transfers between devices, swap_tensor(): return lax.ppermute(value, 'tensor', [(i, i ^ bits) for i in range(tp)])  11.7 us
    pallas_call x1, Pallas kernels, apply_update(): pl.pallas_call(functools.partial(apply_kernel, chunks=chunks), in_specs=[...  6.01 us
    ppermute x9, waiting for transfers between devices, swap_tensor(): return lax.ppermute(value, 'tensor', [(i, i ^ bits) for i in range(tp)])  5.71 us
    ppermute x2, starting transfers between devices, turn(): return lax.ppermute(value, ('dp', 'tensor'), pairs)  4.88 us
    pallas_call x1, Pallas kernels, series(): pl.pallas_call(functools.partial(series_kernel, step_scale=step_scale), i...  4.28 us
  transfers between devices with their start and end apart: 26, of which 10 were waited for; matrix products, arithmetic and copies ran while one was open for 1% of the time, Pallas kernels for 27%

commit v1 on v0

--- a/solution.py
+++ b/solution.py
@@ -30,6 +30,8 @@
 bf16 = jnp.bfloat16
 f32 = jnp.float32
 HIGHEST = lax.Precision.HIGHEST
+VM = pl.BlockSpec(memory_space=pltpu.VMEM)
+SM = pl.BlockSpec(memory_space=pltpu.SMEM)
 
 
 def head_of(table, place, count):
@@ -38,8 +40,8 @@
     upper = jnp.int32(0)
     for i in range(count):
         j = count - 1 - i
-        lower = jnp.where(table[j] == bucket, j, lower)
-        upper = jnp.where(table[i] == bucket, i, upper)
+        lower = jnp.where(table[0, j] == bucket, j, lower)
+        upper = jnp.where(table[0, i] == bucket, i, upper)
     return jnp.where(place % 2 == 0, lower, upper)
 
 
@@ -97,54 +99,59 @@
 def bucket_side(table, head):
     side = jnp.int32(0)
     for i in range(head):
-        side = jnp.where(table[i] == table[head], 1, side)
+        side = jnp.where(table[0, i] == table[0, head], 1, side)
     return side
 
 
-def gram_kernel(table, place, momentum, gradient, new_momentum, update, *rest, parts, slots):
+def gram_kernel(table, place, momentum, gradient, new_momentum, update, *rest, parts):
     outs = rest[:parts]
-    split, total = rest[parts:]
-    step = pl.program_id(0)
-    layers, height, _ = momentum.shape
+    held, slopes, split, total, arrive, leave = rest[parts:]
+    layers, height, width = update.shape
+    slots = width // HD
+    tall = split.shape[1]
     wide = 2 * HD
-    rows = pl.ds(pl.multiple_of(step * height, height), height)
-    for head in range(layers * slots):
-        layer = head // slots
-        cols = slice((head % slots) * HD, (head % slots + 1) * HD)
-        slope = gradient[layer, :, cols]
-        fresh = beta_momentum * momentum[layer, :, cols] + slope
-        new_momentum[layer, :, cols] = fresh
-        change = slope + beta_momentum * fresh
-        update[layer, rows, cols] = change
-        first = change.astype(bf16)
-        left = change - first.astype(f32)
-        second = left.astype(bf16)
-        third = (left - second.astype(f32)).astype(bf16)
-        side = bucket_side(table, head)
-        for k, plane in enumerate((first, second, third)):
-            start = pl.multiple_of(k * wide + side * HD, HD)
-            split[table[head], :, pl.ds(start, HD)] = plane
-
-    for bucket in range(parts):
-        planes = split[bucket]
-        one = planes[:, :wide]
-        two = planes[:, wide : 2 * wide]
-        mixed = dot_t(one, planes)
-        rough = mixed[:, :wide] + dot_t(two, two)
-        rough = rough + 2.0 * (mixed[:, wide : 2 * wide] + mixed[:, 2 * wide :])
-
-        @pl.when(step == 0)
-        def _():
-            total[bucket] = rough
-
-        @pl.when(step > 0)
-        def _():
-            total[bucket] = total[bucket] + rough
-
-    @pl.when(step == pl.num_programs(0) - 1)
-    def _():
+    blocks = [slice(low, low + tall) for low in range(0, height, tall)]
+    loads = []
+    for i, rows in enumerate(blocks):
+        loads.append(
+            (
+                pltpu.make_async_copy(momentum.at[:, rows, :], held.at[:, rows, :], arrive.at[0, i]),
+                pltpu.make_async_copy(gradient.at[:, rows, :], slopes.at[:, rows, :], arrive.at[1, i]),
+            )
+        )
+        for load in loads[-1]:
+            load.start()
+    stores = []
+    for i, rows in enumerate(blocks):
+        for load in loads[i]:
+            load.wait()
+        for head in range(layers * slots):
+            layer = head // slots
+            cols = slice((head % slots) * HD, (head % slots + 1) * HD)
+            slope = slopes[layer, rows, cols]
+            fresh = beta_momentum * held[layer, rows, cols] + slope
+            held[layer, rows, cols] = fresh
+            change = slope + beta_momentum * fresh
+            update[layer, rows, cols] = change
+            side = bucket_side(table, head)
+            for k, plane in enumerate(split_three(change)):
+                start = pl.multiple_of(k * wide + side * HD, HD)
+                split[table[0, head], :, pl.ds(start, HD)] = plane
+        stores.append(
+            pltpu.make_async_copy(held.at[:, rows, :], new_momentum.at[:, rows, :], leave.at[i])
+        )
+        stores[-1].start()
         for bucket in range(parts):
-            rough = total[bucket]
+            planes = split[bucket]
+            two = planes[:, wide : 2 * wide]
+            mixed = dot_t(planes[:, :wide], planes)
+            rough = mixed[:, :wide] + dot_t(two, two)
+            rough = rough + 2.0 * (mixed[:, wide : 2 * wide] + mixed[:, 2 * wide :])
+            if i > 0:
+                rough = total[bucket] + rough
+            if i + 1 < len(blocks):
+                total[bucket] = rough
+                continue
             mixed, side, diag = pack_symmetric(0.5 * (rough + rough.T))
             away = bucket ^ place[0]
             for k in range(parts):
@@ -155,31 +162,30 @@
                     outs[k][HD : 2 * HD, :] = side
                     outs[k][2 * HD : 2 * HD + 8, :] = diag
 
+    for store in stores:
+        store.wait()
+
 
 def local_grams(table, place, momentum, gradient, parts):
-    layers, height, width = momentum.shape
-    slots = width // HD
-    tall = min(height, ROWS)
-    block = pl.BlockSpec((layers, tall, width), lambda i, t, q: (0, i, 0))
+    shape = momentum.shape
+    tall = min(shape[1], ROWS)
+    blocks = shape[1] // tall
     packed = (2 * HD + 8, HD)
-    return pl.pallas_call(
-        functools.partial(gram_kernel, parts=parts, slots=slots),
-        grid_spec=pltpu.PrefetchScalarGridSpec(
-            num_scalar_prefetch=2,
-            grid=(height // tall,),
-            in_specs=[block, block],
-            out_specs=[block, pl.BlockSpec(memory_space=pltpu.VMEM)]
-            + [pl.BlockSpec(packed, lambda i, t, q: (0, 0))] * parts,
-            scratch_shapes=[
-                pltpu.VMEM((parts, tall, 6 * HD), bf16),
-                pltpu.VMEM((parts, 2 * HD, 2 * HD), f32),
-            ],
-        ),
-        out_shape=[
-            jax.ShapeDtypeStruct(momentum.shape, f32),
-            pltpu.VMEM(momentum.shape, f32),
-        ]
-        + [jax.ShapeDtypeStruct(packed, f32)] * parts,
+    anywhere = pl.BlockSpec(memory_space=pl.ANY)
+    return pl.pallas_call(
+        functools.partial(gram_kernel, parts=parts),
+        in_specs=[SM, SM, anywhere, anywhere],
+        out_specs=[anywhere] + [VM] * (parts + 1),
+        scratch_shapes=[
+            pltpu.VMEM(shape, f32),
+            pltpu.VMEM(shape, f32),
+            pltpu.VMEM((parts, tall, 6 * HD), bf16),
+            pltpu.VMEM((parts, 2 * HD, 2 * HD), f32),
+            pltpu.SemaphoreType.DMA((2, blocks)),
+            pltpu.SemaphoreType.DMA((blocks,)),
+        ],
+        out_shape=[jax.ShapeDtypeStruct(shape, f32), pltpu.VMEM(shape, f32)]
+        + [pltpu.VMEM(packed, f32)] * parts,
         compiler_params=pltpu.CompilerParams(vmem_limit_bytes=24 * MIB),
         name="grams",
     )(table, place, hbm(momentum), hbm(gradient))
@@ -218,10 +224,6 @@
     return pltpu.with_memory_space_constraint(value, pltpu.VMEM)
 
 
-VM = pl.BlockSpec(memory_space=pltpu.VMEM)
-SM = pl.BlockSpec(memory_space=pltpu.SMEM)
-
-
 def series(pieces, sums, step_scale):
     high, wide = pieces[0].shape
     return pl.pallas_call(
@@ -268,7 +270,7 @@
 
     tall = min(height, ROWS)
     for head in range(heads):
-        bucket = table[head]
+        bucket = table[0, head]
         start = pl.multiple_of(bucket_side(table, head) * HD, HD)
         factor = factors[bucket, :, pl.ds(start, HD)]
         spots = head_spots(table, bucket, slots, layers * slots)
@@ -343,45 +345,41 @@
     )(table, vmem(factors), vmem(update), vmem(master))
 
 
-def norm_kernel(place, *refs, parts, features):
-    halves = refs[: 2 * parts]
-    packed = refs[2 * parts : 3 * parts]
-    gain, out = refs[3 * parts :]
-    height, width = halves[0].shape
+def norm_kernel(place, *refs, parts, base, features):
+    pieces = refs[:parts]
+    packed = refs[parts : 2 * parts]
+    gain, out, sums = refs[2 * parts :]
+    height, width = pieces[0].shape
     high = packed[0].shape[0] - 8
     for k in range(parts):
-        inverse = lax.rsqrt(packed[k][high : high + 8, :] / features + rms_epsilon)
+        sums[k] = lax.rsqrt(packed[k][high : high + 8, :] / features + rms_epsilon)
+    for k in range(parts):
         away = k ^ place[0] ^ place[1]
-        for side in range(2):
-            for low in range(0, height, HD):
-                spot = (side * height + low) // HD
-                column = jnp.broadcast_to(inverse[spot : spot + 1, :], (HD, HD)).T
-                for i in range(parts):
-
-                    @pl.when(away == i)
-                    def _():
-                        for left in range(0, width, HD):
-                            cols = slice(left, left + HD)
-                            values = halves[2 * i + side][low : low + HD, cols].astype(f32)
-                            out[k, spot * HD : (spot + 1) * HD, cols] = (
-                                values * column * gain[:, cols]
-                            ).astype(bf16)
-
-
-def normalise(place, halves, packed, gain, features):
+        inverse = sums[away]
+        for low in range(0, height, HD):
+            spot = (base + low) // HD
+            column = jnp.broadcast_to(inverse[spot : spot + 1, :], (HD, HD)).T
+            for left in range(0, width, HD):
+                cols = slice(left, left + HD)
+                values = pieces[k][low : low + HD, cols].astype(f32)
+                out[away, low : low + HD, cols] = (values * column * gain[:, cols]).astype(bf16)
+
+
+def normalise(place, pieces, packed, gain, base, features):
     parts = len(packed)
-    height, width = halves[0].shape
-    return pl.pallas_call(
-        functools.partial(norm_kernel, parts=parts, features=features),
-        in_specs=[SM] + [VM] * (3 * parts + 1),
+    height, width = pieces[0].shape
+    return pl.pallas_call(
+        functools.partial(norm_kernel, parts=parts, base=base, features=features),
+        in_specs=[SM] + [VM] * (2 * parts + 1),
         out_specs=VM,
-        out_shape=pltpu.VMEM((parts, 2 * height, width), bf16),
+        out_shape=pltpu.VMEM((parts, height, width), bf16),
+        scratch_shapes=[pltpu.VMEM((parts, 8, HD), f32)],
         compiler_params=pltpu.CompilerParams(vmem_limit_bytes=8 * MIB),
         name="normalise",
-    )(place, *[vmem(h) for h in halves], *[vmem(p) for p in packed], vmem(gain))
-
-
-def project_kernel(place, normed, *refs, members, parts):
+    )(place, *[vmem(p) for p in pieces], *[vmem(p) for p in packed], vmem(gain))
+
+
+def project_kernel(place, near, far, *refs, members, parts):
     weights = refs[:members]
     outs = refs[members : members + parts]
     whole = refs[-1]
@@ -390,7 +388,8 @@
         start = pl.multiple_of((k ^ place[2]) * height, height)
         whole[pl.ds(start, height), :] = weights[k][...]
     for m in range(parts):
-        part = jnp.dot(normed[m], whole[...], preferred_element_type=f32)
+        both = [jnp.dot(half[m], whole[...], preferred_element_type=f32) for half in (near, far)]
+        part = jnp.concatenate(both, axis=0)
         if m == 0:
             outs[m][...] = part
         else:
@@ -433,19 +432,20 @@
     )(*[vmem(p) for piece in pieces for p in piece])
 
 
-def project(place, normed, weights):
-    parts, height, width = normed.shape
+def project(place, near, far, weights):
+    parts, height, width = near.shape
+    height *= 2
     cols = weights[0].shape[1]
     code = pltpu.VMEM((height + CODE_ROWS, cols), jnp.int16)
     return pl.pallas_call(
         functools.partial(project_kernel, members=len(weights), parts=parts),
-        in_specs=[SM] + [VM] * (1 + len(weights)),
+        in_specs=[SM] + [VM] * (2 + len(weights)),
         out_specs=[VM] * parts,
         out_shape=[pltpu.VMEM((height, cols), f32)] + [code] * (parts - 1),
         scratch_shapes=[pltpu.VMEM((width, cols), bf16)],
         compiler_params=pltpu.CompilerParams(vmem_limit_bytes=8 * MIB),
         name="project",
-    )(place, vmem(normed), *[vmem(w) for w in weights])
+    )(place, vmem(near), vmem(far), *[vmem(w) for w in weights])
 
 
 def after(value, other):
@@ -464,7 +464,7 @@
     column = lax.axis_index("tensor")
     row = mine // members
     place = jnp.stack([row, column, mine % members]).astype(jnp.int32)
-    table = bucket_table[0]
+    table = bucket_table
 
     def swap_dp(value, bits):
         return lax.ppermute(value, "dp", [(i, i ^ bits) for i in range(dp)])
@@ -511,24 +511,26 @@
     lead, factors = lead_weights(table, place, packed, update, master, CHUNKS)
     new_master, *others = apply_update(table, factors, update, master, CHUNKS)
 
-    held = {(0, 0): after(sent[0], own), (1, tp // 2): after(sent[1], own)}
-    bits = tp // 2
-    while bits:
-        fresh = {}
-        for (side, offset), value in held.items():
-            if bits < tp // 2:
-                value = after(value, others[0] if others else lead)
-            fresh[(side, offset ^ bits)] = swap_tensor(value, bits)
-        held.update(fresh)
-        bits //= 2
-    halves = [held[(side, offset)] for offset in range(parts) for side in range(2)]
     gain = lax.dynamic_slice_in_dim(norm_gain, row * share, share, 0)[None, :]
-    normed = normalise(place, halves, packed, gain, features)
+    normed = []
+    for side in range(2):
+        held = {side * (tp // 2): after(sent[side], own)}
+        bits = tp // 2
+        while bits:
+            fresh = {}
+            for offset, value in held.items():
+                if bits < tp // 2:
+                    value = after(value, others[0] if side and others else lead)
+                fresh[offset ^ bits] = swap_tensor(value, bits)
+            held.update(fresh)
+            bits //= 2
+        halves = [held[offset] for offset in range(parts)]
+        normed.append(normalise(place, halves, packed, gain, side * half, features))
 
     pieces = []
     for piece in [lead] + others:
         gathered = [piece] + [swap_dp(piece, k) for k in range(1, members)]
-        partial = project(place, normed, gathered)
+        partial = project(place, *normed, gathered)
         sums_of = [swap_dp(partial[k], k * members) for k in range(1, parts)]
         pieces.append([partial[0]] + sums_of)
     return (new_master, new_momentum, finish(pieces))

time: 124 us -> 123 us (level)
  waiting for transfers between devices: 46.5 us -> 47.9 us
    ppermute x15, waiting for transfers between devices: 40.8 us -> 46.4 us  [swap_dp(): return lax.ppermute(value, 'dp', [(i, i ^ bits) for i in range(dp)])]
    ppermute x9, waiting for transfers between devices: 5.71 us -> 1.51 us  [swap_tensor(): return lax.ppermute(value, 'tensor', [(i, i ^ bits) for i in range(tp)])]
    pallas_call x2 -> x3, Pallas kernels: 16.4 us -> 13.1 us  [the longest x1 9.3 us: local_grams(): pl.pallas_call(functools.partial(gram_kernel, parts=parts), in_specs=[SM,...]
    ppermute x9, starting transfers between devices: 11.7 us -> 8.57 us  [swap_tensor(): return lax.ppermute(value, 'tensor', [(i, i ^ bits) for i in range(tp)])]
    unnamed x10 -> x6, local copies, waits for them, and re-layouts: 2.5 us -> 0.66 us
    pallas_call x2, Pallas kernels: 3.94 us -> 5.62 us  [project(): pl.pallas_call(functools.partial(project_kernel, members=len(weights), pa...]
    ppermute x15, starting transfers between devices: 20.2 us -> 21.5 us  [swap_dp(): return lax.ppermute(value, 'dp', [(i, i ^ bits) for i in range(dp)])]
  transfers between devices with their start and end apart: 26 -> 26, of which waited for: 10 -> 9; matrix products, arithmetic and copies ran while one was open for 1% -> 1% of each run, Pallas kernels for 27% -> 27%
where the time goes in v1:
time: 123 us
  waiting for transfers between devices  47.9 us (39%)
  starting transfers between devices  36 us (29%)
  Pallas kernels  34.3 us (28%)
  local copies, waits for them, and re-layouts  3.45 us (3%)
    ppermute x15, waiting for transfers between devices, swap_dp(): return lax.ppermute(value, 'dp', [(i, i ^ bits) for i in range(dp)])  46.4 us
    ppermute x15, starting transfers between devices, swap_dp(): return lax.ppermute(value, 'dp', [(i, i ^ bits) for i in range(dp)])  21.5 us
    pallas_call x1, Pallas kernels, local_grams(): pl.pallas_call(functools.partial(gram_kernel, parts=parts), in_specs=[SM,...  9.3 us
    ppermute x9, starting transfers between devices, swap_tensor(): return lax.ppermute(value, 'tensor', [(i, i ^ bits) for i in range(tp)])  8.57 us
    pallas_call x1, Pallas kernels, apply_update(): pl.pallas_call(functools.partial(apply_kernel, chunks=chunks), in_specs=[...  6.72 us
    ppermute x2, starting transfers between devices, turn(): return lax.ppermute(value, ('dp', 'tensor'), pairs)  5.88 us
    pallas_call x2, Pallas kernels, project(): pl.pallas_call(functools.partial(project_kernel, members=len(weights), pa...  5.62 us
    pallas_call x1, Pallas kernels, series(): pl.pallas_call(functools.partial(series_kernel, step_scale=step_scale), i...  4.27 us
  transfers between devices with their start and end apart: 26, of which 9 were waited for; matrix products, arithmetic and copies ran while one was open for 1% of the time, Pallas kernels for 27%

profile of v1, /device:TPU:0, one launch (start us, length us, event | category | flops | bytes accessed | tf_op | source)
XLA Modules:
  0.0 122.8 jit_solution(5842176914798722004)
XLA Ops:
  0.6 2.1 %fusion = (bf16[128,2048]{1,0:T(8,128)(2,1)S(1)}, bf16[128,2048]{1,0:T(8,128)(2,1)}) fusion(bf16[256,2048]{1,0:T(8,128)(2,1)} %param.10), kind=kLoop, calls=%fused_computation.4 | loop fusion | bytes 2097152 | tf_op jit(solution)/shard_map/slice | solution.py:478
  2.7 3.0 %collective-permute-start.13 = (bf16[128,2048]{1,0:T(8,128)(2,1)S(1)}, bf16[128,2048]{1,0:T(8,128)(2,1)S(1)}, u32[]{:S(2)}, u32[]{:S(2)}) collective-permute-start(bf16[128,2048]{1,0:T(8,128)(2,1)S(1)} %get-tuple-element.55), channel_id=1, source_target_pairs={{0,2},{1,3},{2,0},{3,1},{4,6},{5,7},{6,4},{7,5},{8,10},{9,11},{10,... | collective-permute-start | bytes 1572872 | tf_op jit(solution)/shard_map/ppermute | solution.py:473
  6.4 9.3 %grams.1 = (f32[2,1024,512]{2,1,0:T(8,128)}, f32[2,1024,512]{2,1,0:T(8,128)S(1)}, f32[264,128]{1,0:T(8,128)S(1)}, f32[264,128]{1,0:T(8,128)S(1)}, f32[264,128]{1,0:T(8,128)S(1)}, /*index=5*/f32[264,128]{1,0:T(8,128)S(1)}) custom-call(s32[1,8]{1,0:T(1,128)S(1)} %copy-done.1, s32[3]{0:T(128)S(1)} %pad_add_fusion.place, f32[2,1024,512]{2,1,0:T(8,128)} %momentum.1, ...), custom_call_target="tpu_custom_call" | custom-call | tf_op jit(solution)/shard_map/grams/pallas_call | solution.py:175
  15.7 3.7 %collective-permute-start.2 = (f32[264,128]{1,0:T(8,128)S(1)}, f32[264,128]{1,0:T(8,128)S(1)}, u32[]{:S(2)}, u32[]{:S(2)}) collective-permute-start(f32[264,128]{1,0:T(8,128)S(1)} %get-tuple-element.32), channel_id=1, source_target_pairs={{0,24},{4,28},{8,16},{12,20},{16,8},{20,12},{24,0},{28,4},{1,25},{... | collective-permute-start | bytes 405512 | tf_op jit(solution)/shard_map/ppermute | solution.py:470
  20.9 1.7 %collective-permute-start.9 = (bf16[128,2048]{1,0:T(8,128)(2,1)}, bf16[128,2048]{1,0:T(8,128)(2,1)S(1)}, u32[]{:S(2)}, u32[]{:S(2)}) collective-permute-start(bf16[128,2048]{1,0:T(8,128)(2,1)} %get-tuple-element.37), channel_id=1, source_target_pairs={{0,0},{1,8},{2,16},{3,24},{4,4},{5,12},{6,20},{7,28},{8,1},{9,9},{... | collective-permute-start | bytes 1572872 | tf_op jit(solution)/shard_map/ppermute | solution.py:487
  22.6 1.5 %collective-permute-done.4 = f32[256]{0:T(256)S(1)} collective-permute-done((f32[256]{0:T(256)S(1)}, f32[256]{0:T(256)S(1)}, u32[]{:S(2)}, u32[]{:S(2)}) %collective-permute-start.4) | collective-permute-done | bytes 1056 | tf_op jit(solution)/shard_map/ppermute | solution.py:473
  24.1 4.2 %collective-permute-start.14 = (bf16[128,2048]{1,0:T(8,128)(2,1)S(1)}, bf16[128,2048]{1,0:T(8,128)(2,1)S(1)}, u32[]{:S(2)}, u32[]{:S(2)}) collective-permute-start(bf16[128,2048]{1,0:T(8,128)(2,1)S(1)} %collective-permute-done.13), channel_id=1, source_target_pairs={{0,18},{1,26},{2,2},{3,10},{4,22},{5,30},{6,6},{7,14},{8,19},{9,27... | collective-permute-start | bytes 1572872 | tf_op jit(solution)/shard_map/ppermute | solution.py:487
  28.3 1.6 %collective-permute-start.5 = (f32[256]{0:T(256)S(1)}, f32[256]{0:T(256)S(1)}, u32[]{:S(2)}, u32[]{:S(2)}) collective-permute-start(f32[256]{0:T(256)S(1)} %add.27), channel_id=1, source_target_pairs={{0,1},{1,0},{2,3},{3,2},{4,5},{5,4},{6,7},{7,6},{8,9},{9,8},{10,11... | collective-permute-start | bytes 3080 | tf_op jit(solution)/shard_map/ppermute | solution.py:473
  30.0 12.8 %collective-permute-done.1 = f32[264,128]{1,0:T(8,128)S(1)} collective-permute-done((f32[264,128]{1,0:T(8,128)S(1)}, f32[264,128]{1,0:T(8,128)S(1)}, u32[]{:S(2)}, u32[]{:S(2)}) %collective-permute-start.1) | collective-permute-done | bytes 135200 | tf_op jit(solution)/shard_map/ppermute | solution.py:470
  42.8 1.6 %collective-permute-start.3 = (f32[264,128]{1,0:T(8,128)S(1)}, f32[264,128]{1,0:T(8,128)S(1)}, u32[]{:S(2)}, u32[]{:S(2)}) collective-permute-start(f32[264,128]{1,0:T(8,128)S(1)} %add_add_fusion.refs_0_), channel_id=1, source_target_pairs={{0,4},{4,0},{8,12},{12,8},{16,20},{20,16},{24,28},{28,24},{1,5},{5... | collective-permute-start | bytes 405512 | tf_op jit(solution)/shard_map/ppermute | solution.py:470
  44.4 3.5 %collective-permute-done.3.refs_1_ = f32[264,128]{1,0:T(8,128)S(1)} collective-permute-done((f32[264,128]{1,0:T(8,128)S(1)}, f32[264,128]{1,0:T(8,128)S(1)}, u32[]{:S(2)}, u32[]{:S(2)}) %collective-permute-start.3) | collective-permute-done | bytes 135200 | tf_op jit(solution)/shard_map/ppermute | solution.py:470
  47.8 4.3 %series.1.refs_0_.refs_4_ = f32[272,128]{1,0:T(8,128)S(1)} custom-call(f32[264,128]{1,0:T(8,128)S(1)} %add_add_fusion.refs_0_, f32[264,128]{1,0:T(8,128)S(1)} %collective-permute-done.3.refs_1_, f32[2,128]{1,0:T(2,128)S(1)} %add_bitcast_fusion.refs_2_), custom_call_target="tpu_custom_call" | custom-call | tf_op jit(solution)/shard_map/series/pallas_call | solution.py:229
  52.1 2.4 %collective-permute-start.11 = (bf16[128,2048]{1,0:T(8,128)(2,1)S(1)}, bf16[128,2048]{1,0:T(8,128)(2,1)S(1)}, u32[]{:S(2)}, u32[]{:S(2)}) collective-permute-start(bf16[128,2048]{1,0:T(8,128)(2,1)S(1)} %collective-permute-done.9.refs_0_), channel_id=1, source_target_pairs={{0,2},{1,3},{2,0},{3,1},{4,6},{5,7},{6,4},{7,5},{8,10},{9,11},{10,... | collective-permute-start | bytes 1572872 | tf_op jit(solution)/shard_map/ppermute | solution.py:473
  54.6 1.7 %collective-permute-start.7 = (f32[272,128]{1,0:T(8,128)S(1)}, f32[272,128]{1,0:T(8,128)S(1)}, u32[]{:S(2)}, u32[]{:S(2)}) collective-permute-start(f32[272,128]{1,0:T(8,128)S(1)} %series.1.refs_0_.refs_4_), channel_id=1, source_target_pairs={{0,16},{4,20},{8,24},{12,28},{16,0},{20,4},{24,8},{28,12},{1,17},{... | collective-permute-start | bytes 417800 | tf_op jit(solution)/shard_map/ppermute | solution.py:470
  56.3 2.7 %collective-permute-start.8 = (f32[272,128]{1,0:T(8,128)S(1)}, f32[272,128]{1,0:T(8,128)S(1)}, u32[]{:S(2)}, u32[]{:S(2)}) collective-permute-start(f32[272,128]{1,0:T(8,128)S(1)} %series.1.refs_0_.refs_4_), channel_id=1, source_target_pairs={{0,24},{4,28},{8,16},{12,20},{16,8},{20,12},{24,0},{28,4},{1,25},{... | collective-permute-start | bytes 417800 | tf_op jit(solution)/shard_map/ppermute | solution.py:470
  59.8 7.0 %collective-permute-done.7.refs_2_.refs_6_ = f32[272,128]{1,0:T(8,128)S(1)} collective-permute-done((f32[272,128]{1,0:T(8,128)S(1)}, f32[272,128]{1,0:T(8,128)S(1)}, u32[]{:S(2)}, u32[]{:S(2)}) %collective-permute-start.7) | collective-permute-done | bytes 139296 | tf_op jit(solution)/shard_map/ppermute | solution.py:470
  66.8 3.7 %lead.1 = (bf16[1024,256]{1,0:T(8,128)(2,1)}, bf16[4,1536,256]{2,1,0:T(8,128)(2,1)S(1)}) custom-call(s32[1,8]{1,0:T(1,128)S(1)} %copy-done.1, s32[3]{0:T(128)S(1)} %pad_add_fusion.place, f32[272,128]{1,0:T(8,128)S(1)} %series.1.refs_0_.refs_4_, f32[272,128]{1,0:T(8,128)S(1)} %collective-permute-done.6.refs_1_.refs_5_, ...), custom_call_target="tpu_custom_call" | custom-call | tf_op jit(solution)/shard_map/lead/pallas_call | solution.py:289
  70.5 6.7 %apply.1 = (f32[2,1024,512]{2,1,0:T(8,128)}, bf16[1024,256]{1,0:T(8,128)(2,1)}) custom-call(s32[1,8]{1,0:T(1,128)S(1)} %copy-done.1, bf16[4,1536,256]{2,1,0:T(8,128)(2,1)S(1)} %get-tuple-element.34.factors, f32[2,1024,512]{2,1,0:T(8,128)S(1)} %get-tuple-element.33.refs_4_.update, f32[2,1024,512]{2,1,0:T(8,128)S(1)} %copy-done), custom_call_target="tpu_custom_call" | custom-call | tf_op jit(solution)/shard_map/apply/pallas_call | solution.py:333
  78.3 1.5 %collective-permute-start.18 = (bf16[1024,256]{1,0:T(8,128)(2,1)}, bf16[1024,256]{1,0:T(8,128)(2,1)}, u32[]{:S(2)}, u32[]{:S(2)}) collective-permute-start(bf16[1024,256]{1,0:T(8,128)(2,1)} %get-tuple-element.39.refs_0_), channel_id=1, source_target_pairs={{0,4},{4,0},{8,12},{12,8},{16,20},{20,16},{24,28},{28,24},{1,5},{5... | collective-permute-start | bytes 1572872 | tf_op jit(solution)/shard_map/ppermute | solution.py:470
  81.1 1.8 %normalise.2.near = bf16[4,128,2048]{2,1,0:T(8,128)(2,1)S(1)} custom-call(s32[3]{0:T(128)S(1)} %pad_add_fusion.place, bf16[128,2048]{1,0:T(8,128)(2,1)S(1)} %collective-permute-done.9.refs_0_, bf16[128,2048]{1,0:T(8,128)(2,1)S(1)} %collective-permute-done.10.refs_1_, bf16[128,2048]{1,0:T(8,128)(2,1)S(1)} %collective-permute-done.11.refs_2_, ...), custom_call_target="tpu_custom_call" | custom-call | tf_op jit(solution)/shard_map/normalise/pallas_call | solution.py:371
  82.9 2.0 %normalise.3.far = bf16[4,128,2048]{2,1,0:T(8,128)(2,1)S(1)} custom-call(s32[3]{0:T(128)S(1)} %pad_add_fusion.place, bf16[128,2048]{1,0:T(8,128)(2,1)S(1)} %collective-permute-done.15.refs_0_, bf16[128,2048]{1,0:T(8,128)(2,1)} %collective-permute-done.16.refs_1_, bf16[128,2048]{1,0:T(8,128)(2,1)S(1)} %collective-permute-done.14.refs_2_, ...), custom_call_target="tpu_custom_call" | custom-call | tf_op jit(solution)/shard_map/normalise/pallas_call | solution.py:371
  84.9 8.5 %collective-permute-done.18.refs_1_ = bf16[1024,256]{1,0:T(8,128)(2,1)} collective-permute-done((bf16[1024,256]{1,0:T(8,128)(2,1)}, bf16[1024,256]{1,0:T(8,128)(2,1)}, u32[]{:S(2)}, u32[]{:S(2)}) %collective-permute-start.18) | collective-permute-done | bytes 524320 | tf_op jit(solution)/shard_map/ppermute | solution.py:470
  93.4 3.0 %project.2 = (f32[256,256]{1,0:T(8,128)S(1)}, s16[272,256]{1,0:T(8,128)(2,1)S(1)}, s16[272,256]{1,0:T(8,128)(2,1)S(1)}, s16[272,256]{1,0:T(8,128)(2,1)S(1)}) custom-call(s32[3]{0:T(128)S(1)} %pad_add_fusion.place, bf16[4,128,2048]{2,1,0:T(8,128)(2,1)S(1)} %normalise.2.near, bf16[4,128,2048]{2,1,0:T(8,128)(2,1)S(1)} %normalise.3.far, ...), custom_call_target="tpu_custom_call" | custom-call | tf_op jit(solution)/shard_map/project/pallas_call | solution.py:440
  96.4 2.1 %collective-permute-start.19 = (s16[272,256]{1,0:T(8,128)(2,1)S(1)}, s16[272,256]{1,0:T(8,128)(2,1)S(1)}, u32[]{:S(2)}, u32[]{:S(2)}) collective-permute-start(s16[272,256]{1,0:T(8,128)(2,1)S(1)} %get-tuple-element.48), channel_id=1, source_target_pairs={{0,8},{4,12},{8,0},{12,4},{16,24},{20,28},{24,16},{28,20},{1,9},{5... | collective-permute-start | bytes 417800 | tf_op jit(solution)/shard_map/ppermute | solution.py:470
  98.5 1.1 collective-permute-start.20
  99.6 1.4 %collective-permute-start.21 = (s16[272,256]{1,0:T(8,128)(2,1)S(1)}, s16[272,256]{1,0:T(8,128)(2,1)S(1)}, u32[]{:S(2)}, u32[]{:S(2)}) collective-permute-start(s16[272,256]{1,0:T(8,128)(2,1)S(1)} %get-tuple-element.50), channel_id=1, source_target_pairs={{0,24},{4,28},{8,16},{12,20},{16,8},{20,12},{24,0},{28,4},{1,25},{... | collective-permute-start | bytes 417800 | tf_op jit(solution)/shard_map/ppermute | solution.py:470
  100.9 2.8 %collective-permute-done.22.refs_1_ = bf16[1024,256]{1,0:T(8,128)(2,1)} collective-permute-done((bf16[1024,256]{1,0:T(8,128)(2,1)}, bf16[1024,256]{1,0:T(8,128)(2,1)}, u32[]{:S(2)}, u32[]{:S(2)}) %collective-permute-start.22) | collective-permute-done | bytes 524320 | tf_op jit(solution)/shard_map/ppermute | solution.py:470
  103.8 2.7 %project.3 = (f32[256,256]{1,0:T(8,128)S(1)}, s16[272,256]{1,0:T(8,128)(2,1)S(1)}, s16[272,256]{1,0:T(8,128)(2,1)S(1)}, s16[272,256]{1,0:T(8,128)(2,1)S(1)}) custom-call(s32[3]{0:T(128)S(1)} %pad_add_fusion.place, bf16[4,128,2048]{2,1,0:T(8,128)(2,1)S(1)} %normalise.2.near, bf16[4,128,2048]{2,1,0:T(8,128)(2,1)S(1)} %normalise.3.far, ...), custom_call_target="tpu_custom_call" | custom-call | tf_op jit(solution)/shard_map/project/pallas_call | solution.py:440
  106.5 2.1 %collective-permute-start.23 = (s16[272,256]{1,0:T(8,128)(2,1)S(1)}, s16[272,256]{1,0:T(8,128)(2,1)S(1)}, u32[]{:S(2)}, u32[]{:S(2)}) collective-permute-start(s16[272,256]{1,0:T(8,128)(2,1)S(1)} %get-tuple-element.52), channel_id=1, source_target_pairs={{0,8},{4,12},{8,0},{12,4},{16,24},{20,28},{24,16},{28,20},{1,9},{5... | collective-permute-start | bytes 417800 | tf_op jit(solution)/shard_map/ppermute | solution.py:470
  109.6 1.4 %collective-permute-start.25 = (s16[272,256]{1,0:T(8,128)(2,1)S(1)}, s16[272,256]{1,0:T(8,128)(2,1)S(1)}, u32[]{:S(2)}, u32[]{:S(2)}) collective-permute-start(s16[272,256]{1,0:T(8,128)(2,1)S(1)} %get-tuple-element.54), channel_id=1, source_target_pairs={{0,24},{4,28},{8,16},{12,20},{16,8},{20,12},{24,0},{28,4},{1,25},{... | collective-permute-start | bytes 417800 | tf_op jit(solution)/shard_map/ppermute | solution.py:470
  111.0 2.6 %collective-permute-done.23.refs_5_ = s16[272,256]{1,0:T(8,128)(2,1)S(1)} collective-permute-done((s16[272,256]{1,0:T(8,128)(2,1)S(1)}, s16[272,256]{1,0:T(8,128)(2,1)S(1)}, u32[]{:S(2)}, u32[]{:S(2)}) %collective-permute-start.23) | collective-permute-done | bytes 139296 | tf_op jit(solution)/shard_map/ppermute | solution.py:470
  113.6 8.3 %collective-permute-done.24.refs_6_ = s16[272,256]{1,0:T(8,128)(2,1)S(1)} collective-permute-done((s16[272,256]{1,0:T(8,128)(2,1)S(1)}, s16[272,256]{1,0:T(8,128)(2,1)S(1)}, u32[]{:S(2)}, u32[]{:S(2)}) %collective-permute-start.24) | collective-permute-done | bytes 139296 | tf_op jit(solution)/shard_map/ppermute | solution.py:470
  (42 shorter events, 7.5 us)
Async XLA Ops:
  2.7 18.2 %collective-permute-start.13 = (bf16[128,2048]{1,0:T(8,128)(2,1)S(1)}, bf16[128,2048]{1,0:T(8,128)(2,1)S(1)}, u32[]{:S(2)}, u32[]{:S(2)}) collective-permute-start(bf16[128,2048]{1,0:T(8,128)(2,1)S(1)} %get-tuple-element.55), channel_id=1, source_target_pairs={{0,2},{1,3},{2,0},{3,1},{4,6},{5,7},{6,4},{7,5},{8,10},{9,11},{10,... | collective-permute-start | bytes 1572872 | tf_op jit(solution)/shard_map/ppermute | solution.py:473
  5.8 0.7 copy-start.1
  6.4 13.8 %copy-start.2 = (bf16[256,2048]{1,0:T(8,128)(2,1)S(1)}, bf16[256,2048]{1,0:T(8,128)(2,1)}, u32[]{:S(2)}) copy-start(bf16[256,2048]{1,0:T(8,128)(2,1)} %param.10) | copy-start | bytes 3145732
  6.4 60.4 %copy-start = (f32[2,1024,512]{2,1,0:T(8,128)S(1)}, f32[2,1024,512]{2,1,0:T(8,128)}, u32[]{:S(2)}) copy-start(f32[2,1024,512]{2,1,0:T(8,128)} %master.1) | copy-start | bytes 12582916
  15.7 12.6 %collective-permute-start.2 = (f32[264,128]{1,0:T(8,128)S(1)}, f32[264,128]{1,0:T(8,128)S(1)}, u32[]{:S(2)}, u32[]{:S(2)}) collective-permute-start(f32[264,128]{1,0:T(8,128)S(1)} %get-tuple-element.32), channel_id=1, source_target_pairs={{0,24},{4,28},{8,16},{12,20},{16,8},{20,12},{24,0},{28,4},{1,25},{... | collective-permute-start | bytes 405512 | tf_op jit(solution)/shard_map/ppermute | solution.py:470
  19.4 23.3 %collective-permute-start.1 = (f32[264,128]{1,0:T(8,128)S(1)}, f32[264,128]{1,0:T(8,128)S(1)}, u32[]{:S(2)}, u32[]{:S(2)}) collective-permute-start(f32[264,128]{1,0:T(8,128)S(1)} %get-tuple-element.31), channel_id=1, source_target_pairs={{0,16},{4,20},{8,24},{12,28},{16,0},{20,4},{24,8},{28,12},{1,17},{... | collective-permute-start | bytes 405512 | tf_op jit(solution)/shard_map/ppermute | solution.py:470
  19.4 23.3 %collective-permute-start = (f32[264,128]{1,0:T(8,128)S(1)}, f32[264,128]{1,0:T(8,128)S(1)}, u32[]{:S(2)}, u32[]{:S(2)}) collective-permute-start(f32[264,128]{1,0:T(8,128)S(1)} %get-tuple-element.30), channel_id=1, source_target_pairs={{0,8},{4,12},{8,0},{12,4},{16,24},{20,28},{24,16},{28,20},{1,9},{5... | collective-permute-start | bytes 405512 | tf_op jit(solution)/shard_map/ppermute | solution.py:470
  20.5 3.6 %collective-permute-start.4 = (f32[256]{0:T(256)S(1)}, f32[256]{0:T(256)S(1)}, u32[]{:S(2)}, u32[]{:S(2)}) collective-permute-start(f32[256]{0:T(256)S(1)} %multiply_reduce_fusion), channel_id=1, source_target_pairs={{0,2},{1,3},{2,0},{3,1},{4,6},{5,7},{6,4},{7,5},{8,10},{9,11},{10,... | collective-permute-start | bytes 3080 | tf_op jit(solution)/shard_map/ppermute | solution.py:473
  20.9 31.2 %collective-permute-start.9 = (bf16[128,2048]{1,0:T(8,128)(2,1)}, bf16[128,2048]{1,0:T(8,128)(2,1)S(1)}, u32[]{:S(2)}, u32[]{:S(2)}) collective-permute-start(bf16[128,2048]{1,0:T(8,128)(2,1)} %get-tuple-element.37), channel_id=1, source_target_pairs={{0,0},{1,8},{2,16},{3,24},{4,4},{5,12},{6,20},{7,28},{8,1},{9,9},{... | collective-permute-start | bytes 1572872 | tf_op jit(solution)/shard_map/ppermute | solution.py:487
  24.1 34.9 %collective-permute-start.14 = (bf16[128,2048]{1,0:T(8,128)(2,1)S(1)}, bf16[128,2048]{1,0:T(8,128)(2,1)S(1)}, u32[]{:S(2)}, u32[]{:S(2)}) collective-permute-start(bf16[128,2048]{1,0:T(8,128)(2,1)S(1)} %collective-permute-done.13), channel_id=1, source_target_pairs={{0,18},{1,26},{2,2},{3,10},{4,22},{5,30},{6,6},{7,14},{8,19},{9,27... | collective-permute-start | bytes 1572872 | tf_op jit(solution)/shard_map/ppermute | solution.py:487
  28.3 16.0 %collective-permute-start.5 = (f32[256]{0:T(256)S(1)}, f32[256]{0:T(256)S(1)}, u32[]{:S(2)}, u32[]{:S(2)}) collective-permute-start(f32[256]{0:T(256)S(1)} %add.27), channel_id=1, source_target_pairs={{0,1},{1,0},{2,3},{3,2},{4,5},{5,4},{6,7},{7,6},{8,9},{9,8},{10,11... | collective-permute-start | bytes 3080 | tf_op jit(solution)/shard_map/ppermute | solution.py:473
  42.8 5.1 %collective-permute-start.3 = (f32[264,128]{1,0:T(8,128)S(1)}, f32[264,128]{1,0:T(8,128)S(1)}, u32[]{:S(2)}, u32[]{:S(2)}) collective-permute-start(f32[264,128]{1,0:T(8,128)S(1)} %add_add_fusion.refs_0_), channel_id=1, source_target_pairs={{0,4},{4,0},{8,12},{12,8},{16,20},{20,16},{24,28},{28,24},{1,5},{5... | collective-permute-start | bytes 405512 | tf_op jit(solution)/shard_map/ppermute | solution.py:470
  52.1 25.1 %collective-permute-start.11 = (bf16[128,2048]{1,0:T(8,128)(2,1)S(1)}, bf16[128,2048]{1,0:T(8,128)(2,1)S(1)}, u32[]{:S(2)}, u32[]{:S(2)}) collective-permute-start(bf16[128,2048]{1,0:T(8,128)(2,1)S(1)} %collective-permute-done.9.refs_0_), channel_id=1, source_target_pairs={{0,2},{1,3},{2,0},{3,1},{4,6},{5,7},{6,4},{7,5},{8,10},{9,11},{10,... | collective-permute-start | bytes 1572872 | tf_op jit(solution)/shard_map/ppermute | solution.py:473
  54.6 5.3 %collective-permute-start.6 = (f32[272,128]{1,0:T(8,128)S(1)}, f32[272,128]{1,0:T(8,128)S(1)}, u32[]{:S(2)}, u32[]{:S(2)}) collective-permute-start(f32[272,128]{1,0:T(8,128)S(1)} %series.1.refs_0_.refs_4_), channel_id=1, source_target_pairs={{0,8},{4,12},{8,0},{12,4},{16,24},{20,28},{24,16},{28,20},{1,9},{5... | collective-permute-start | bytes 417800 | tf_op jit(solution)/shard_map/ppermute | solution.py:470
  54.6 12.3 %collective-permute-start.7 = (f32[272,128]{1,0:T(8,128)S(1)}, f32[272,128]{1,0:T(8,128)S(1)}, u32[]{:S(2)}, u32[]{:S(2)}) collective-permute-start(f32[272,128]{1,0:T(8,128)S(1)} %series.1.refs_0_.refs_4_), channel_id=1, source_target_pairs={{0,16},{4,20},{8,24},{12,28},{16,0},{20,4},{24,8},{28,12},{1,17},{... | collective-permute-start | bytes 417800 | tf_op jit(solution)/shard_map/ppermute | solution.py:470
  56.3 10.6 %collective-permute-start.8 = (f32[272,128]{1,0:T(8,128)S(1)}, f32[272,128]{1,0:T(8,128)S(1)}, u32[]{:S(2)}, u32[]{:S(2)}) collective-permute-start(f32[272,128]{1,0:T(8,128)S(1)} %series.1.refs_0_.refs_4_), channel_id=1, source_target_pairs={{0,24},{4,28},{8,16},{12,20},{16,8},{20,12},{24,0},{28,4},{1,25},{... | collective-permute-start | bytes 417800 | tf_op jit(solution)/shard_map/ppermute | solution.py:470
  59.0 18.9 %collective-permute-start.15 = (bf16[128,2048]{1,0:T(8,128)(2,1)S(1)}, bf16[128,2048]{1,0:T(8,128)(2,1)S(1)}, u32[]{:S(2)}, u32[]{:S(2)}) collective-permute-start(bf16[128,2048]{1,0:T(8,128)(2,1)S(1)} %collective-permute-done.14.refs_2_), channel_id=1, source_target_pairs={{0,2},{1,3},{2,0},{3,1},{4,6},{5,7},{6,4},{7,5},{8,10},{9,11},{10,... | collective-permute-start | bytes 1572872 | tf_op jit(solution)/shard_map/ppermute | solution.py:473
  70.5 9.3 %collective-permute-start.10 = (bf16[128,2048]{1,0:T(8,128)(2,1)S(1)}, bf16[128,2048]{1,0:T(8,128)(2,1)S(1)}, u32[]{:S(2)}, u32[]{:S(2)}) collective-permute-start(bf16[128,2048]{1,0:T(8,128)(2,1)S(1)} %collective-permute-done.9.refs_0_), channel_id=1, source_target_pairs={{0,1},{1,0},{2,3},{3,2},{4,5},{5,4},{6,7},{7,6},{8,9},{9,8},{10,11... | collective-permute-start | bytes 1572872 | tf_op jit(solution)/shard_map/ppermute | solution.py:473
  77.3 3.8 %collective-permute-start.12 = (bf16[128,2048]{1,0:T(8,128)(2,1)S(1)}, bf16[128,2048]{1,0:T(8,128)(2,1)}, u32[]{:S(2)}, u32[]{:S(2)}) collective-permute-start(bf16[128,2048]{1,0:T(8,128)(2,1)S(1)} %collective-permute-done.11.refs_2_), channel_id=1, source_target_pairs={{0,1},{1,0},{2,3},{3,2},{4,5},{5,4},{6,7},{7,6},{8,9},{9,8},{10,11... | collective-permute-start | bytes 1572872 | tf_op jit(solution)/shard_map/ppermute | solution.py:473
  77.8 5.1 %collective-permute-start.17 = (bf16[128,2048]{1,0:T(8,128)(2,1)S(1)}, bf16[128,2048]{1,0:T(8,128)(2,1)}, u32[]{:S(2)}, u32[]{:S(2)}) collective-permute-start(bf16[128,2048]{1,0:T(8,128)(2,1)S(1)} %collective-permute-done.14.refs_2_), channel_id=1, source_target_pairs={{0,1},{1,0},{2,3},{3,2},{4,5},{5,4},{6,7},{7,6},{8,9},{9,8},{10,11... | collective-permute-start | bytes 1572872 | tf_op jit(solution)/shard_map/ppermute | solution.py:473
  77.9 5.0 %collective-permute-start.16 = (bf16[128,2048]{1,0:T(8,128)(2,1)S(1)}, bf16[128,2048]{1,0:T(8,128)(2,1)}, u32[]{:S(2)}, u32[]{:S(2)}) collective-permute-start(bf16[128,2048]{1,0:T(8,128)(2,1)S(1)} %collective-permute-done.15.refs_0_), channel_id=1, source_target_pairs={{0,1},{1,0},{2,3},{3,2},{4,5},{5,4},{6,7},{7,6},{8,9},{9,8},{10,11... | collective-permute-start | bytes 1572872 | tf_op jit(solution)/shard_map/ppermute | solution.py:473
  78.3 15.1 %collective-permute-start.18 = (bf16[1024,256]{1,0:T(8,128)(2,1)}, bf16[1024,256]{1,0:T(8,128)(2,1)}, u32[]{:S(2)}, u32[]{:S(2)}) collective-permute-start(bf16[1024,256]{1,0:T(8,128)(2,1)} %get-tuple-element.39.refs_0_), channel_id=1, source_target_pairs={{0,4},{4,0},{8,12},{12,8},{16,20},{20,16},{24,28},{28,24},{1,5},{5... | collective-permute-start | bytes 1572872 | tf_op jit(solution)/shard_map/ppermute | solution.py:470
  79.9 23.9 %collective-permute-start.22 = (bf16[1024,256]{1,0:T(8,128)(2,1)}, bf16[1024,256]{1,0:T(8,128)(2,1)}, u32[]{:S(2)}, u32[]{:S(2)}) collective-permute-start(bf16[1024,256]{1,0:T(8,128)(2,1)} %get-tuple-element.44.refs_0_), channel_id=1, source_target_pairs={{0,4},{4,0},{8,12},{12,8},{16,20},{20,16},{24,28},{28,24},{1,5},{5... | collective-permute-start | bytes 1572872 | tf_op jit(solution)/shard_map/ppermute | solution.py:470
  96.4 13.2 %collective-permute-start.19 = (s16[272,256]{1,0:T(8,128)(2,1)S(1)}, s16[272,256]{1,0:T(8,128)(2,1)S(1)}, u32[]{:S(2)}, u32[]{:S(2)}) collective-permute-start(s16[272,256]{1,0:T(8,128)(2,1)S(1)} %get-tuple-element.48), channel_id=1, source_target_pairs={{0,8},{4,12},{8,0},{12,4},{16,24},{20,28},{24,16},{28,20},{1,9},{5... | collective-permute-start | bytes 417800 | tf_op jit(solution)/shard_map/ppermute | solution.py:470
  98.5 12.5 %collective-permute-start.20 = (s16[272,256]{1,0:T(8,128)(2,1)S(1)}, s16[272,256]{1,0:T(8,128)(2,1)S(1)}, u32[]{:S(2)}, u32[]{:S(2)}) collective-permute-start(s16[272,256]{1,0:T(8,128)(2,1)S(1)} %get-tuple-element.49), channel_id=1, source_target_pairs={{0,16},{4,20},{8,24},{12,28},{16,0},{20,4},{24,8},{28,12},{1,17},{... | collective-permute-start | bytes 417800 | tf_op jit(solution)/shard_map/ppermute | solution.py:470
  99.6 11.5 %collective-permute-start.21 = (s16[272,256]{1,0:T(8,128)(2,1)S(1)}, s16[272,256]{1,0:T(8,128)(2,1)S(1)}, u32[]{:S(2)}, u32[]{:S(2)}) collective-permute-start(s16[272,256]{1,0:T(8,128)(2,1)S(1)} %get-tuple-element.50), channel_id=1, source_target_pairs={{0,24},{4,28},{8,16},{12,20},{16,8},{20,12},{24,0},{28,4},{1,25},{... | collective-permute-start | bytes 417800 | tf_op jit(solution)/shard_map/ppermute | solution.py:470
  106.5 7.1 %collective-permute-start.23 = (s16[272,256]{1,0:T(8,128)(2,1)S(1)}, s16[272,256]{1,0:T(8,128)(2,1)S(1)}, u32[]{:S(2)}, u32[]{:S(2)}) collective-permute-start(s16[272,256]{1,0:T(8,128)(2,1)S(1)} %get-tuple-element.52), channel_id=1, source_target_pairs={{0,8},{4,12},{8,0},{12,4},{16,24},{20,28},{24,16},{28,20},{1,9},{5... | collective-permute-start | bytes 417800 | tf_op jit(solution)/shard_map/ppermute | solution.py:470
  108.6 13.3 %collective-permute-start.24 = (s16[272,256]{1,0:T(8,128)(2,1)S(1)}, s16[272,256]{1,0:T(8,128)(2,1)S(1)}, u32[]{:S(2)}, u32[]{:S(2)}) collective-permute-start(s16[272,256]{1,0:T(8,128)(2,1)S(1)} %get-tuple-element.53), channel_id=1, source_target_pairs={{0,16},{4,20},{8,24},{12,28},{16,0},{20,4},{24,8},{28,12},{1,17},{... | collective-permute-start | bytes 417800 | tf_op jit(solution)/shard_map/ppermute | solution.py:470
  109.6 12.3 %collective-permute-start.25 = (s16[272,256]{1,0:T(8,128)(2,1)S(1)}, s16[272,256]{1,0:T(8,128)(2,1)S(1)}, u32[]{:S(2)}, u32[]{:S(2)}) collective-permute-start(s16[272,256]{1,0:T(8,128)(2,1)S(1)} %get-tuple-element.54), channel_id=1, source_target_pairs={{0,24},{4,28},{8,16},{12,20},{16,8},{20,12},{24,0},{28,4},{1,25},{... | collective-permute-start | bytes 417800 | tf_op jit(solution)/shard_map/ppermute | solution.py:470

commit v2 on v1

--- a/solution.py
+++ b/solution.py
@@ -23,6 +23,7 @@
 CHUNKS = 2
 ROWS = 256
 MIB = 1 << 20
+PLACES = 3
 CODE_ROWS = 16
 CODE_BITS = 14.9
 LEAST = 2.0**-100
@@ -40,8 +41,8 @@
     upper = jnp.int32(0)
     for i in range(count):
         j = count - 1 - i
-        lower = jnp.where(table[0, j] == bucket, j, lower)
-        upper = jnp.where(table[0, i] == bucket, i, upper)
+        lower = jnp.where(table[PLACES + j] == bucket, j, lower)
+        upper = jnp.where(table[PLACES + i] == bucket, i, upper)
     return jnp.where(place % 2 == 0, lower, upper)
 
 
@@ -99,11 +100,11 @@
 def bucket_side(table, head):
     side = jnp.int32(0)
     for i in range(head):
-        side = jnp.where(table[0, i] == table[0, head], 1, side)
+        side = jnp.where(table[PLACES + i] == table[PLACES + head], 1, side)
     return side
 
 
-def gram_kernel(table, place, momentum, gradient, new_momentum, update, *rest, parts):
+def gram_kernel(place, momentum, gradient, new_momentum, update, *rest, parts):
     outs = rest[:parts]
     held, slopes, split, total, arrive, leave = rest[parts:]
     layers, height, width = update.shape
@@ -133,10 +134,10 @@
             held[layer, rows, cols] = fresh
             change = slope + beta_momentum * fresh
             update[layer, rows, cols] = change
-            side = bucket_side(table, head)
+            side = bucket_side(place, head)
             for k, plane in enumerate(split_three(change)):
                 start = pl.multiple_of(k * wide + side * HD, HD)
-                split[table[0, head], :, pl.ds(start, HD)] = plane
+                split[place[PLACES + head], :, pl.ds(start, HD)] = plane
         stores.append(
             pltpu.make_async_copy(held.at[:, rows, :], new_momentum.at[:, rows, :], leave.at[i])
         )
@@ -166,7 +167,7 @@
         store.wait()
 
 
-def local_grams(table, place, momentum, gradient, parts):
+def local_grams(place, momentum, gradient, parts):
     shape = momentum.shape
     tall = min(shape[1], ROWS)
     blocks = shape[1] // tall
@@ -174,7 +175,7 @@
     anywhere = pl.BlockSpec(memory_space=pl.ANY)
     return pl.pallas_call(
         functools.partial(gram_kernel, parts=parts),
-        in_specs=[SM, SM, anywhere, anywhere],
+        in_specs=[SM, anywhere, anywhere],
         out_specs=[anywhere] + [VM] * (parts + 1),
         scratch_shapes=[
             pltpu.VMEM(shape, f32),
@@ -186,9 +187,9 @@
         ],
         out_shape=[jax.ShapeDtypeStruct(shape, f32), pltpu.VMEM(shape, f32)]
         + [pltpu.VMEM(packed, f32)] * parts,
-        compiler_params=pltpu.CompilerParams(vmem_limit_bytes=24 * MIB),
+        compiler_params=pltpu.CompilerParams(vmem_limit_bytes=16 * MIB),
         name="grams",
-    )(table, place, hbm(momentum), hbm(gradient))
+    )(place, hbm(momentum), hbm(gradient))
 
 
 def series_kernel(*refs, step_scale):
@@ -231,7 +232,7 @@
         in_specs=[VM] * (len(pieces) + 1),
         out_specs=VM,
         out_shape=pltpu.VMEM((high + 8, wide), f32),
-        compiler_params=pltpu.CompilerParams(vmem_limit_bytes=8 * MIB),
+        compiler_params=pltpu.CompilerParams(vmem_limit_bytes=5 * MIB),
         name="series",
     )(*[vmem(p) for p in pieces], vmem(sums))
 
@@ -257,7 +258,7 @@
     return spots
 
 
-def lead_kernel(table, place, *refs, parts, slots, heads):
+def lead_kernel(place, *refs, parts, slots, heads):
     packed = refs[:parts]
     update, master, weights, factors = refs[parts:]
     layers, height, _ = master.shape
@@ -270,10 +271,10 @@
 
     tall = min(height, ROWS)
     for head in range(heads):
-        bucket = table[0, head]
-        start = pl.multiple_of(bucket_side(table, head) * HD, HD)
+        bucket = place[PLACES + head]
+        start = pl.multiple_of(bucket_side(place, head) * HD, HD)
         factor = factors[bucket, :, pl.ds(start, HD)]
-        spots = head_spots(table, bucket, slots, layers * slots)
+        spots = head_spots(place, bucket, slots, layers * slots)
         cols = slice(head * HD, (head + 1) * HD)
         for low in range(0, height, tall):
             rows = slice(low, low + tall)
@@ -282,21 +283,21 @@
             weights[rows, cols] = (master[0, rows, cols] - ortho).astype(bf16)
 
 
-def lead_weights(table, place, packed, update, master, chunks):
+def lead_weights(place, packed, update, master, chunks):
     _, height, width = master.shape
     parts = len(packed)
     slots = width // HD
     return pl.pallas_call(
         functools.partial(lead_kernel, parts=parts, slots=slots, heads=slots // chunks),
-        in_specs=[SM, SM] + [VM] * (parts + 2),
+        in_specs=[SM] + [VM] * (parts + 2),
         out_specs=[VM, VM],
         out_shape=[
             pltpu.VMEM((height, width // chunks), bf16),
             pltpu.VMEM((parts, 12 * HD, 2 * HD), bf16),
         ],
-        compiler_params=pltpu.CompilerParams(vmem_limit_bytes=12 * MIB),
+        compiler_params=pltpu.CompilerParams(vmem_limit_bytes=9 * MIB),
         name="lead",
-    )(table, place, *[vmem(p) for p in packed], vmem(update), vmem(master))
+    )(place, *[vmem(p) for p in packed], vmem(update), vmem(master))
 
 
 def apply_kernel(table, factors, update, master, new_master, *refs, chunks):
@@ -340,7 +341,7 @@
         ],
         out_shape=[jax.ShapeDtypeStruct(master.shape, f32)]
         + [pltpu.VMEM((height, width // chunks), bf16)] * (chunks - 1),
-        compiler_params=pltpu.CompilerParams(vmem_limit_bytes=12 * MIB),
+        compiler_params=pltpu.CompilerParams(vmem_limit_bytes=9 * MIB),
         name="apply",
     )(table, vmem(factors), vmem(update), vmem(master))
 
@@ -374,7 +375,7 @@
         out_specs=VM,
         out_shape=pltpu.VMEM((parts, height, width), bf16),
         scratch_shapes=[pltpu.VMEM((parts, 8, HD), f32)],
-        compiler_params=pltpu.CompilerParams(vmem_limit_bytes=8 * MIB),
+        compiler_params=pltpu.CompilerParams(vmem_limit_bytes=5 * MIB),
         name="normalise",
     )(place, *[vmem(p) for p in pieces], *[vmem(p) for p in packed], vmem(gain))
 
@@ -388,8 +389,8 @@
         start = pl.multiple_of((k ^ place[2]) * height, height)
         whole[pl.ds(start, height), :] = weights[k][...]
     for m in range(parts):
-        both = [jnp.dot(half[m], whole[...], preferred_element_type=f32) for half in (near, far)]
-        part = jnp.concatenate(both, axis=0)
+        both = jnp.concatenate([near[m], far[m]], axis=0)
+        part = jnp.dot(both, whole[...], preferred_element_type=f32)
         if m == 0:
             outs[m][...] = part
         else:
@@ -427,7 +428,7 @@
         functools.partial(finish_kernel, chunks=chunks, parts=parts),
         in_specs=[VM] * (chunks * parts),
         out_shape=jax.ShapeDtypeStruct((height, chunks * width), bf16),
-        compiler_params=pltpu.CompilerParams(vmem_limit_bytes=8 * MIB),
+        compiler_params=pltpu.CompilerParams(vmem_limit_bytes=5 * MIB),
         name="finish",
     )(*[vmem(p) for piece in pieces for p in piece])
 
@@ -443,7 +444,7 @@
         out_specs=[VM] * parts,
         out_shape=[pltpu.VMEM((height, cols), f32)] + [code] * (parts - 1),
         scratch_shapes=[pltpu.VMEM((width, cols), bf16)],
-        compiler_params=pltpu.CompilerParams(vmem_limit_bytes=8 * MIB),
+        compiler_params=pltpu.CompilerParams(vmem_limit_bytes=5 * MIB),
         name="project",
     )(place, vmem(near), vmem(far), *[vmem(w) for w in weights])
 
@@ -463,8 +464,8 @@
     mine = lax.axis_index("dp")
     column = lax.axis_index("tensor")
     row = mine // members
-    place = jnp.stack([row, column, mine % members]).astype(jnp.int32)
-    table = bucket_table
+    spot = jnp.stack([row, column, mine % members]).astype(jnp.int32)
+    place = jnp.concatenate([spot, bucket_table[0]])
 
     def swap_dp(value, bits):
         return lax.ppermute(value, "dp", [(i, i ^ bits) for i in range(dp)])
@@ -474,7 +475,6 @@
 
     half = tokens.shape[0] // 2
     flips = (0, tp // 2)
-    near = lax.slice_in_dim(tokens, 0, half, axis=0)
     far = swap_tensor(lax.slice_in_dim(tokens, half, 2 * half, axis=0), tp // 2)
 
     def turn(value, flip):
@@ -486,7 +486,7 @@
                     pairs.append(((q * members + r) * tp + j, target))
         return lax.ppermute(value, ("dp", "tensor"), pairs)
 
-    new_momentum, update, *grams = local_grams(table, place, momentum, gradient, parts)
+    new_momentum, update, *grams = local_grams(place, momentum, gradient, parts)
 
     local_f = tokens.astype(f32)
     sums = jnp.sum(local_f * local_f, axis=1)
@@ -495,7 +495,8 @@
         sums = sums + swap_tensor(sums, bits)
         bits //= 2
 
-    sent = [turn(after(value, grams[0]), flip) for value, flip in zip((near, far), flips)]
+    near = lax.slice_in_dim(after(tokens, grams[0]), 0, half, axis=0)
+    sent = [turn(near, flips[0]), turn(after(far, grams[0]), flips[1])]
     total = grams[0]
     for k in range(1, parts):
         total = total + swap_dp(grams[k], k * members)
@@ -508,24 +509,26 @@
     own = series(pieces, sums.reshape(-1, HD), step_scale)
 
     packed = [own] + [swap_dp(own, k * members) for k in range(1, parts)]
-    lead, factors = lead_weights(table, place, packed, update, master, CHUNKS)
-    new_master, *others = apply_update(table, factors, update, master, CHUNKS)
-
+    lead, factors = lead_weights(place, packed, update, master, CHUNKS)
     gain = lax.dynamic_slice_in_dim(norm_gain, row * share, share, 0)[None, :]
-    normed = []
-    for side in range(2):
+
+    def shared(side, start):
         held = {side * (tp // 2): after(sent[side], own)}
         bits = tp // 2
         while bits:
             fresh = {}
             for offset, value in held.items():
                 if bits < tp // 2:
-                    value = after(value, others[0] if side and others else lead)
+                    value = after(value, start)
                 fresh[offset ^ bits] = swap_tensor(value, bits)
             held.update(fresh)
             bits //= 2
         halves = [held[offset] for offset in range(parts)]
-        normed.append(normalise(place, halves, packed, gain, side * half, features))
+        return normalise(place, halves, packed, gain, side * half, features)
+
+    near_normed = shared(0, lead)
+    new_master, *others = apply_update(place, factors, update, master, CHUNKS)
+    normed = (near_normed, shared(1, others[0] if others else lead))
 
     pieces = []
     for piece in [lead] + others:

time: 123 us -> 122 us (level)
  local copies, waits for them, and re-layouts: 3.45 us -> 1.82 us
where the time goes in v2:
time: 122 us; the launch traced here: 121 us
  waiting for transfers between devices  48.7 us (40%)
  starting transfers between devices  35.1 us (29%)
  Pallas kernels  34 us (28%)
  local copies, waits for them, and re-layouts  1.82 us (1%)
    ppermute x15, waiting for transfers between devices, swap_dp(): return lax.ppermute(value, 'dp', [(i, i ^ bits) for i in range(dp)])  46.3 us
    ppermute x15, starting transfers between devices, swap_dp(): return lax.ppermute(value, 'dp', [(i, i ^ bits) for i in range(dp)])  21.6 us
    pallas_call x1, Pallas kernels, local_grams(): pl.pallas_call(functools.partial(gram_kernel, parts=parts), in_specs=[SM,...  9.28 us
    ppermute x9, starting transfers between devices, swap_tensor(): return lax.ppermute(value, 'tensor', [(i, i ^ bits) for i in range(tp)])  8.63 us
    pallas_call x1, Pallas kernels, apply_update(): pl.pallas_call(functools.partial(apply_kernel, chunks=chunks), in_specs=[...  6.79 us
    pallas_call x2, Pallas kernels, project(): pl.pallas_call(functools.partial(project_kernel, members=len(weights), pa...  5.27 us
    ppermute x2, starting transfers between devices, turn(): return lax.ppermute(value, ('dp', 'tensor'), pairs)  4.88 us
    pallas_call x1, Pallas kernels, series(): pl.pallas_call(functools.partial(series_kernel, step_scale=step_scale), i...  4.28 us
  transfers between devices with their start and end apart: 26, of which 9 were waited for; matrix products, arithmetic and copies ran while one was open for 1% of the time, Pallas kernels for 27%

profile of v2, /device:TPU:0, one launch (start us, length us, event | category | flops | bytes accessed | tf_op | source)
XLA Modules:
  0.0 121.5 jit_solution(12206464234819951728)
XLA Ops:
  0.6 1.1 slice.7
  1.7 3.0 %collective-permute-start.13 = (bf16[128,2048]{1,0:T(8,128)(2,1)S(1)}, bf16[128,2048]{1,0:T(8,128)(2,1)S(1)}, u32[]{:S(2)}, u32[]{:S(2)}) collective-permute-start(bf16[128,2048]{1,0:T(8,128)(2,1)S(1)} %slice.7), channel_id=1, source_target_pairs={{0,2},{1,3},{2,0},{3,1},{4,6},{5,7},{6,4},{7,5},{8,10},{9,11},{10,... | collective-permute-start | bytes 1572872 | tf_op jit(solution)/shard_map/ppermute | solution.py:474
  5.5 9.3 %grams.1 = (f32[2,1024,512]{2,1,0:T(8,128)}, f32[2,1024,512]{2,1,0:T(8,128)S(1)}, f32[264,128]{1,0:T(8,128)S(1)}, f32[264,128]{1,0:T(8,128)S(1)}, f32[264,128]{1,0:T(8,128)S(1)}, /*index=5*/f32[264,128]{1,0:T(8,128)S(1)}) custom-call(s32[11]{0:T(128)S(1)} %pad_add_fusion.place.table, f32[2,1024,512]{2,1,0:T(8,128)} %momentum.1, f32[2,1024,512]{2,1,0:T(8,128)} %gradient.1), custom_call_target="tpu_custom_call" | custom-call | tf_op jit(solution)/shard_map/grams/pallas_call | solution.py:176
  14.8 3.7 %collective-permute-start.2 = (f32[264,128]{1,0:T(8,128)S(1)}, f32[264,128]{1,0:T(8,128)S(1)}, u32[]{:S(2)}, u32[]{:S(2)}) collective-permute-start(f32[264,128]{1,0:T(8,128)S(1)} %get-tuple-element.32), channel_id=1, source_target_pairs={{0,24},{4,28},{8,16},{12,20},{16,8},{20,12},{24,0},{28,4},{1,25},{... | collective-permute-start | bytes 405512 | tf_op jit(solution)/shard_map/ppermute | solution.py:471
  20.7 2.4 %collective-permute-done.4 = f32[256]{0:T(256)S(1)} collective-permute-done((f32[256]{0:T(256)S(1)}, f32[256]{0:T(256)S(1)}, u32[]{:S(2)}, u32[]{:S(2)}) %collective-permute-start.4) | collective-permute-done | bytes 1056 | tf_op jit(solution)/shard_map/ppermute | solution.py:474
  23.1 4.2 %collective-permute-start.14 = (bf16[128,2048]{1,0:T(8,128)(2,1)S(1)}, bf16[128,2048]{1,0:T(8,128)(2,1)S(1)}, u32[]{:S(2)}, u32[]{:S(2)}) collective-permute-start(bf16[128,2048]{1,0:T(8,128)(2,1)S(1)} %collective-permute-done.13), channel_id=1, source_target_pairs={{0,18},{1,26},{2,2},{3,10},{4,22},{5,30},{6,6},{7,14},{8,19},{9,27... | collective-permute-start | bytes 1572872 | tf_op jit(solution)/shard_map/ppermute | solution.py:487
  27.4 1.6 %collective-permute-start.5 = (f32[256]{0:T(256)S(1)}, f32[256]{0:T(256)S(1)}, u32[]{:S(2)}, u32[]{:S(2)}) collective-permute-start(f32[256]{0:T(256)S(1)} %add.27), channel_id=1, source_target_pairs={{0,1},{1,0},{2,3},{3,2},{4,5},{5,4},{6,7},{7,6},{8,9},{9,8},{10,11... | collective-permute-start | bytes 3080 | tf_op jit(solution)/shard_map/ppermute | solution.py:474
  29.0 12.8 %collective-permute-done.1 = f32[264,128]{1,0:T(8,128)S(1)} collective-permute-done((f32[264,128]{1,0:T(8,128)S(1)}, f32[264,128]{1,0:T(8,128)S(1)}, u32[]{:S(2)}, u32[]{:S(2)}) %collective-permute-start.1) | collective-permute-done | bytes 135200 | tf_op jit(solution)/shard_map/ppermute | solution.py:471
  41.8 1.6 %collective-permute-start.3 = (f32[264,128]{1,0:T(8,128)S(1)}, f32[264,128]{1,0:T(8,128)S(1)}, u32[]{:S(2)}, u32[]{:S(2)}) collective-permute-start(f32[264,128]{1,0:T(8,128)S(1)} %add_add_fusion.refs_0_), channel_id=1, source_target_pairs={{0,4},{4,0},{8,12},{12,8},{16,20},{20,16},{24,28},{28,24},{1,5},{5... | collective-permute-start | bytes 405512 | tf_op jit(solution)/shard_map/ppermute | solution.py:471
  43.4 3.5 %collective-permute-done.3.refs_1_ = f32[264,128]{1,0:T(8,128)S(1)} collective-permute-done((f32[264,128]{1,0:T(8,128)S(1)}, f32[264,128]{1,0:T(8,128)S(1)}, u32[]{:S(2)}, u32[]{:S(2)}) %collective-permute-start.3) | collective-permute-done | bytes 135200 | tf_op jit(solution)/shard_map/ppermute | solution.py:471
  46.9 4.3 %series.1.refs_0_.refs_4_ = f32[272,128]{1,0:T(8,128)S(1)} custom-call(f32[264,128]{1,0:T(8,128)S(1)} %add_add_fusion.refs_0_, f32[264,128]{1,0:T(8,128)S(1)} %collective-permute-done.3.refs_1_, f32[2,128]{1,0:T(2,128)S(1)} %add_bitcast_fusion.refs_2_), custom_call_target="tpu_custom_call" | custom-call | tf_op jit(solution)/shard_map/series/pallas_call | solution.py:230
  51.2 2.4 %collective-permute-start.11 = (bf16[128,2048]{1,0:T(8,128)(2,1)S(1)}, bf16[128,2048]{1,0:T(8,128)(2,1)S(1)}, u32[]{:S(2)}, u32[]{:S(2)}) collective-permute-start(bf16[128,2048]{1,0:T(8,128)(2,1)S(1)} %collective-permute-done.9.refs_0_), channel_id=1, source_target_pairs={{0,2},{1,3},{2,0},{3,1},{4,6},{5,7},{6,4},{7,5},{8,10},{9,11},{10,... | collective-permute-start | bytes 1572872 | tf_op jit(solution)/shard_map/ppermute | solution.py:474
  53.6 1.7 %collective-permute-start.7 = (f32[272,128]{1,0:T(8,128)S(1)}, f32[272,128]{1,0:T(8,128)S(1)}, u32[]{:S(2)}, u32[]{:S(2)}) collective-permute-start(f32[272,128]{1,0:T(8,128)S(1)} %series.1.refs_0_.refs_4_), channel_id=1, source_target_pairs={{0,16},{4,20},{8,24},{12,28},{16,0},{20,4},{24,8},{28,12},{1,17},{... | collective-permute-start | bytes 417800 | tf_op jit(solution)/shard_map/ppermute | solution.py:471
  55.3 2.7 %collective-permute-start.8 = (f32[272,128]{1,0:T(8,128)S(1)}, f32[272,128]{1,0:T(8,128)S(1)}, u32[]{:S(2)}, u32[]{:S(2)}) collective-permute-start(f32[272,128]{1,0:T(8,128)S(1)} %series.1.refs_0_.refs_4_), channel_id=1, source_target_pairs={{0,24},{4,28},{8,16},{12,20},{16,8},{20,12},{24,0},{28,4},{1,25},{... | collective-permute-start | bytes 417800 | tf_op jit(solution)/shard_map/ppermute | solution.py:471
  58.9 7.0 %collective-permute-done.7.refs_2_.refs_6_ = f32[272,128]{1,0:T(8,128)S(1)} collective-permute-done((f32[272,128]{1,0:T(8,128)S(1)}, f32[272,128]{1,0:T(8,128)S(1)}, u32[]{:S(2)}, u32[]{:S(2)}) %collective-permute-start.7) | collective-permute-done | bytes 139296 | tf_op jit(solution)/shard_map/ppermute | solution.py:471
  65.9 3.7 %lead.1 = (bf16[1024,256]{1,0:T(8,128)(2,1)}, bf16[4,1536,256]{2,1,0:T(8,128)(2,1)S(1)}) custom-call(s32[11]{0:T(128)S(1)} %pad_add_fusion.place.table, f32[272,128]{1,0:T(8,128)S(1)} %series.1.refs_0_.refs_4_, f32[272,128]{1,0:T(8,128)S(1)} %collective-permute-done.6.refs_1_.refs_5_, f32[272,128]{1,0:T(8,128)S(1)} %collective-permute-done.7.refs_2_.refs_6_, ...), custom_call_target="tpu_custom_call" | custom-call | tf_op jit(solution)/shard_map/lead/pallas_call | solution.py:290
  69.5 6.8 %apply.1 = (f32[2,1024,512]{2,1,0:T(8,128)}, bf16[1024,256]{1,0:T(8,128)(2,1)}) custom-call(s32[11]{0:T(128)S(1)} %pad_add_fusion.place.table, bf16[4,1536,256]{2,1,0:T(8,128)(2,1)S(1)} %get-tuple-element.34.factors, f32[2,1024,512]{2,1,0:T(8,128)S(1)} %get-tuple-element.33.refs_4_.update, f32[2,1024,512]{2,1,0:T(8,128)S(1)} %copy-done), custom_call_target="tpu_custom_call" | custom-call | tf_op jit(solution)/shard_map/apply/pallas_call | solution.py:334
  77.4 1.5 %collective-permute-start.18 = (bf16[1024,256]{1,0:T(8,128)(2,1)}, bf16[1024,256]{1,0:T(8,128)(2,1)}, u32[]{:S(2)}, u32[]{:S(2)}) collective-permute-start(bf16[1024,256]{1,0:T(8,128)(2,1)} %get-tuple-element.39.refs_0_), channel_id=1, source_target_pairs={{0,4},{4,0},{8,12},{12,8},{16,20},{20,16},{24,28},{28,24},{1,5},{5... | collective-permute-start | bytes 1572872 | tf_op jit(solution)/shard_map/ppermute | solution.py:471
  80.2 1.8 %normalise.2.near = bf16[4,128,2048]{2,1,0:T(8,128)(2,1)S(1)} custom-call(s32[11]{0:T(128)S(1)} %pad_add_fusion.place.table, bf16[128,2048]{1,0:T(8,128)(2,1)S(1)} %collective-permute-done.9.refs_0_, bf16[128,2048]{1,0:T(8,128)(2,1)S(1)} %collective-permute-done.10.refs_1_, bf16[128,2048]{1,0:T(8,128)(2,1)S(1)} %collective-permute-done.11.refs_2_, ...), custom_call_target="tpu_custom_call" | custom-call | tf_op jit(solution)/shard_map/normalise/pallas_call | solution.py:372
  82.0 2.0 %normalise.3.far = bf16[4,128,2048]{2,1,0:T(8,128)(2,1)S(1)} custom-call(s32[11]{0:T(128)S(1)} %pad_add_fusion.place.table, bf16[128,2048]{1,0:T(8,128)(2,1)S(1)} %collective-permute-done.15.refs_0_, bf16[128,2048]{1,0:T(8,128)(2,1)} %collective-permute-done.16.refs_1_, bf16[128,2048]{1,0:T(8,128)(2,1)S(1)} %collective-permute-done.14.refs_2_, ...), custom_call_target="tpu_custom_call" | custom-call | tf_op jit(solution)/shard_map/normalise/pallas_call | solution.py:372
  84.0 8.5 %collective-permute-done.18.refs_1_ = bf16[1024,256]{1,0:T(8,128)(2,1)} collective-permute-done((bf16[1024,256]{1,0:T(8,128)(2,1)}, bf16[1024,256]{1,0:T(8,128)(2,1)}, u32[]{:S(2)}, u32[]{:S(2)}) %collective-permute-start.18) | collective-permute-done | bytes 524320 | tf_op jit(solution)/shard_map/ppermute | solution.py:471
  92.5 2.6 %project.2 = (f32[256,256]{1,0:T(8,128)S(1)}, s16[272,256]{1,0:T(8,128)(2,1)S(1)}, s16[272,256]{1,0:T(8,128)(2,1)S(1)}, s16[272,256]{1,0:T(8,128)(2,1)S(1)}) custom-call(s32[11]{0:T(128)S(1)} %pad_add_fusion.place.table, bf16[4,128,2048]{2,1,0:T(8,128)(2,1)S(1)} %normalise.2.near, bf16[4,128,2048]{2,1,0:T(8,128)(2,1)S(1)} %normalise.3.far, ...), custom_call_target="tpu_custom_call" | custom-call | tf_op jit(solution)/shard_map/project/pallas_call | solution.py:441
  95.2 2.1 %collective-permute-start.19 = (s16[272,256]{1,0:T(8,128)(2,1)S(1)}, s16[272,256]{1,0:T(8,128)(2,1)S(1)}, u32[]{:S(2)}, u32[]{:S(2)}) collective-permute-start(s16[272,256]{1,0:T(8,128)(2,1)S(1)} %get-tuple-element.48), channel_id=1, source_target_pairs={{0,8},{4,12},{8,0},{12,4},{16,24},{20,28},{24,16},{28,20},{1,9},{5... | collective-permute-start | bytes 417800 | tf_op jit(solution)/shard_map/ppermute | solution.py:471
  97.3 1.1 collective-permute-start.20
  98.3 1.4 %collective-permute-start.21 = (s16[272,256]{1,0:T(8,128)(2,1)S(1)}, s16[272,256]{1,0:T(8,128)(2,1)S(1)}, u32[]{:S(2)}, u32[]{:S(2)}) collective-permute-start(s16[272,256]{1,0:T(8,128)(2,1)S(1)} %get-tuple-element.50), channel_id=1, source_target_pairs={{0,24},{4,28},{8,16},{12,20},{16,8},{20,12},{24,0},{28,4},{1,25},{... | collective-permute-start | bytes 417800 | tf_op jit(solution)/shard_map/ppermute | solution.py:471
  99.7 3.1 %collective-permute-done.22.refs_1_ = bf16[1024,256]{1,0:T(8,128)(2,1)} collective-permute-done((bf16[1024,256]{1,0:T(8,128)(2,1)}, bf16[1024,256]{1,0:T(8,128)(2,1)}, u32[]{:S(2)}, u32[]{:S(2)}) %collective-permute-start.22) | collective-permute-done | bytes 524320 | tf_op jit(solution)/shard_map/ppermute | solution.py:471
  102.9 2.6 %project.3 = (f32[256,256]{1,0:T(8,128)S(1)}, s16[272,256]{1,0:T(8,128)(2,1)S(1)}, s16[272,256]{1,0:T(8,128)(2,1)S(1)}, s16[272,256]{1,0:T(8,128)(2,1)S(1)}) custom-call(s32[11]{0:T(128)S(1)} %pad_add_fusion.place.table, bf16[4,128,2048]{2,1,0:T(8,128)(2,1)S(1)} %normalise.2.near, bf16[4,128,2048]{2,1,0:T(8,128)(2,1)S(1)} %normalise.3.far, ...), custom_call_target="tpu_custom_call" | custom-call | tf_op jit(solution)/shard_map/project/pallas_call | solution.py:441
  105.5 2.1 %collective-permute-start.23 = (s16[272,256]{1,0:T(8,128)(2,1)S(1)}, s16[272,256]{1,0:T(8,128)(2,1)S(1)}, u32[]{:S(2)}, u32[]{:S(2)}) collective-permute-start(s16[272,256]{1,0:T(8,128)(2,1)S(1)} %get-tuple-element.52), channel_id=1, source_target_pairs={{0,8},{4,12},{8,0},{12,4},{16,24},{20,28},{24,16},{28,20},{1,9},{5... | collective-permute-start | bytes 417800 | tf_op jit(solution)/shard_map/ppermute | solution.py:471
  107.6 1.1 collective-permute-start.24
  108.7 1.4 %collective-permute-start.25 = (s16[272,256]{1,0:T(8,128)(2,1)S(1)}, s16[272,256]{1,0:T(8,128)(2,1)S(1)}, u32[]{:S(2)}, u32[]{:S(2)}) collective-permute-start(s16[272,256]{1,0:T(8,128)(2,1)S(1)} %get-tuple-element.54), channel_id=1, source_target_pairs={{0,24},{4,28},{8,16},{12,20},{16,8},{20,12},{24,0},{28,4},{1,25},{... | collective-permute-start | bytes 417800 | tf_op jit(solution)/shard_map/ppermute | solution.py:471
  110.1 2.5 %collective-permute-done.23.refs_5_ = s16[272,256]{1,0:T(8,128)(2,1)S(1)} collective-permute-done((s16[272,256]{1,0:T(8,128)(2,1)S(1)}, s16[272,256]{1,0:T(8,128)(2,1)S(1)}, u32[]{:S(2)}, u32[]{:S(2)}) %collective-permute-start.23) | collective-permute-done | bytes 139296 | tf_op jit(solution)/shard_map/ppermute | solution.py:471
  112.6 8.0 %collective-permute-done.24.refs_6_ = s16[272,256]{1,0:T(8,128)(2,1)S(1)} collective-permute-done((s16[272,256]{1,0:T(8,128)(2,1)S(1)}, s16[272,256]{1,0:T(8,128)(2,1)S(1)}, u32[]{:S(2)}, u32[]{:S(2)}) %collective-permute-start.24) | collective-permute-done | bytes 139296 | tf_op jit(solution)/shard_map/ppermute | solution.py:471
  (41 shorter events, 7.2 us)
Async XLA Ops:
  1.7 18.3 %collective-permute-start.13 = (bf16[128,2048]{1,0:T(8,128)(2,1)S(1)}, bf16[128,2048]{1,0:T(8,128)(2,1)S(1)}, u32[]{:S(2)}, u32[]{:S(2)}) collective-permute-start(bf16[128,2048]{1,0:T(8,128)(2,1)S(1)} %slice.7), channel_id=1, source_target_pairs={{0,2},{1,3},{2,0},{3,1},{4,6},{5,7},{6,4},{7,5},{8,10},{9,11},{10,... | collective-permute-start | bytes 1572872 | tf_op jit(solution)/shard_map/ppermute | solution.py:474
  5.5 13.7 %copy-start.1 = (bf16[256,2048]{1,0:T(8,128)(2,1)S(1)}, bf16[256,2048]{1,0:T(8,128)(2,1)}, u32[]{:S(2)}) copy-start(bf16[256,2048]{1,0:T(8,128)(2,1)} %param.10) | copy-start | bytes 3145732
  5.5 60.4 %copy-start = (f32[2,1024,512]{2,1,0:T(8,128)S(1)}, f32[2,1024,512]{2,1,0:T(8,128)}, u32[]{:S(2)}) copy-start(f32[2,1024,512]{2,1,0:T(8,128)} %master.1) | copy-start | bytes 12582916
  14.8 12.6 %collective-permute-start.2 = (f32[264,128]{1,0:T(8,128)S(1)}, f32[264,128]{1,0:T(8,128)S(1)}, u32[]{:S(2)}, u32[]{:S(2)}) collective-permute-start(f32[264,128]{1,0:T(8,128)S(1)} %get-tuple-element.32), channel_id=1, source_target_pairs={{0,24},{4,28},{8,16},{12,20},{16,8},{20,12},{24,0},{28,4},{1,25},{... | collective-permute-start | bytes 405512 | tf_op jit(solution)/shard_map/ppermute | solution.py:471
  18.4 23.3 %collective-permute-start.1 = (f32[264,128]{1,0:T(8,128)S(1)}, f32[264,128]{1,0:T(8,128)S(1)}, u32[]{:S(2)}, u32[]{:S(2)}) collective-permute-start(f32[264,128]{1,0:T(8,128)S(1)} %get-tuple-element.31), channel_id=1, source_target_pairs={{0,16},{4,20},{8,24},{12,28},{16,0},{20,4},{24,8},{28,12},{1,17},{... | collective-permute-start | bytes 405512 | tf_op jit(solution)/shard_map/ppermute | solution.py:471
  18.4 23.3 %collective-permute-start = (f32[264,128]{1,0:T(8,128)S(1)}, f32[264,128]{1,0:T(8,128)S(1)}, u32[]{:S(2)}, u32[]{:S(2)}) collective-permute-start(f32[264,128]{1,0:T(8,128)S(1)} %get-tuple-element.30), channel_id=1, source_target_pairs={{0,8},{4,12},{8,0},{12,4},{16,24},{20,28},{24,16},{28,20},{1,9},{5... | collective-permute-start | bytes 405512 | tf_op jit(solution)/shard_map/ppermute | solution.py:471
  19.5 3.6 %collective-permute-start.4 = (f32[256]{0:T(256)S(1)}, f32[256]{0:T(256)S(1)}, u32[]{:S(2)}, u32[]{:S(2)}) collective-permute-start(f32[256]{0:T(256)S(1)} %multiply_reduce_fusion), channel_id=1, source_target_pairs={{0,2},{1,3},{2,0},{3,1},{4,6},{5,7},{6,4},{7,5},{8,10},{9,11},{10,... | collective-permute-start | bytes 3080 | tf_op jit(solution)/shard_map/ppermute | solution.py:474
  20.0 31.2 %collective-permute-start.9 = (bf16[128,2048]{1,0:T(8,128)(2,1)S(1)}, bf16[128,2048]{1,0:T(8,128)(2,1)S(1)}, u32[]{:S(2)}, u32[]{:S(2)}) collective-permute-start(bf16[128,2048]{1,0:T(8,128)(2,1)S(1)} %slice.6), channel_id=1, source_target_pairs={{0,0},{1,8},{2,16},{3,24},{4,4},{5,12},{6,20},{7,28},{8,1},{9,9},{... | collective-permute-start | bytes 1572872 | tf_op jit(solution)/shard_map/ppermute | solution.py:487
  23.1 34.9 %collective-permute-start.14 = (bf16[128,2048]{1,0:T(8,128)(2,1)S(1)}, bf16[128,2048]{1,0:T(8,128)(2,1)S(1)}, u32[]{:S(2)}, u32[]{:S(2)}) collective-permute-start(bf16[128,2048]{1,0:T(8,128)(2,1)S(1)} %collective-permute-done.13), channel_id=1, source_target_pairs={{0,18},{1,26},{2,2},{3,10},{4,22},{5,30},{6,6},{7,14},{8,19},{9,27... | collective-permute-start | bytes 1572872 | tf_op jit(solution)/shard_map/ppermute | solution.py:487
  27.4 16.0 %collective-permute-start.5 = (f32[256]{0:T(256)S(1)}, f32[256]{0:T(256)S(1)}, u32[]{:S(2)}, u32[]{:S(2)}) collective-permute-start(f32[256]{0:T(256)S(1)} %add.27), channel_id=1, source_target_pairs={{0,1},{1,0},{2,3},{3,2},{4,5},{5,4},{6,7},{7,6},{8,9},{9,8},{10,11... | collective-permute-start | bytes 3080 | tf_op jit(solution)/shard_map/ppermute | solution.py:474
  41.8 5.1 %collective-permute-start.3 = (f32[264,128]{1,0:T(8,128)S(1)}, f32[264,128]{1,0:T(8,128)S(1)}, u32[]{:S(2)}, u32[]{:S(2)}) collective-permute-start(f32[264,128]{1,0:T(8,128)S(1)} %add_add_fusion.refs_0_), channel_id=1, source_target_pairs={{0,4},{4,0},{8,12},{12,8},{16,20},{20,16},{24,28},{28,24},{1,5},{5... | collective-permute-start | bytes 405512 | tf_op jit(solution)/shard_map/ppermute | solution.py:471
  51.2 25.2 %collective-permute-start.11 = (bf16[128,2048]{1,0:T(8,128)(2,1)S(1)}, bf16[128,2048]{1,0:T(8,128)(2,1)S(1)}, u32[]{:S(2)}, u32[]{:S(2)}) collective-permute-start(bf16[128,2048]{1,0:T(8,128)(2,1)S(1)} %collective-permute-done.9.refs_0_), channel_id=1, source_target_pairs={{0,2},{1,3},{2,0},{3,1},{4,6},{5,7},{6,4},{7,5},{8,10},{9,11},{10,... | collective-permute-start | bytes 1572872 | tf_op jit(solution)/shard_map/ppermute | solution.py:474
  53.6 5.3 %collective-permute-start.6 = (f32[272,128]{1,0:T(8,128)S(1)}, f32[272,128]{1,0:T(8,128)S(1)}, u32[]{:S(2)}, u32[]{:S(2)}) collective-permute-start(f32[272,128]{1,0:T(8,128)S(1)} %series.1.refs_0_.refs_4_), channel_id=1, source_target_pairs={{0,8},{4,12},{8,0},{12,4},{16,24},{20,28},{24,16},{28,20},{1,9},{5... | collective-permute-start | bytes 417800 | tf_op jit(solution)/shard_map/ppermute | solution.py:471
  53.6 12.3 %collective-permute-start.7 = (f32[272,128]{1,0:T(8,128)S(1)}, f32[272,128]{1,0:T(8,128)S(1)}, u32[]{:S(2)}, u32[]{:S(2)}) collective-permute-start(f32[272,128]{1,0:T(8,128)S(1)} %series.1.refs_0_.refs_4_), channel_id=1, source_target_pairs={{0,16},{4,20},{8,24},{12,28},{16,0},{20,4},{24,8},{28,12},{1,17},{... | collective-permute-start | bytes 417800 | tf_op jit(solution)/shard_map/ppermute | solution.py:471
  55.3 10.6 %collective-permute-start.8 = (f32[272,128]{1,0:T(8,128)S(1)}, f32[272,128]{1,0:T(8,128)S(1)}, u32[]{:S(2)}, u32[]{:S(2)}) collective-permute-start(f32[272,128]{1,0:T(8,128)S(1)} %series.1.refs_0_.refs_4_), channel_id=1, source_target_pairs={{0,24},{4,28},{8,16},{12,20},{16,8},{20,12},{24,0},{28,4},{1,25},{... | collective-permute-start | bytes 417800 | tf_op jit(solution)/shard_map/ppermute | solution.py:471
  58.0 19.0 %collective-permute-start.15 = (bf16[128,2048]{1,0:T(8,128)(2,1)S(1)}, bf16[128,2048]{1,0:T(8,128)(2,1)S(1)}, u32[]{:S(2)}, u32[]{:S(2)}) collective-permute-start(bf16[128,2048]{1,0:T(8,128)(2,1)S(1)} %collective-permute-done.14.refs_2_), channel_id=1, source_target_pairs={{0,2},{1,3},{2,0},{3,1},{4,6},{5,7},{6,4},{7,5},{8,10},{9,11},{10,... | collective-permute-start | bytes 1572872 | tf_op jit(solution)/shard_map/ppermute | solution.py:474
  69.5 9.4 %collective-permute-start.10 = (bf16[128,2048]{1,0:T(8,128)(2,1)S(1)}, bf16[128,2048]{1,0:T(8,128)(2,1)S(1)}, u32[]{:S(2)}, u32[]{:S(2)}) collective-permute-start(bf16[128,2048]{1,0:T(8,128)(2,1)S(1)} %collective-permute-done.9.refs_0_), channel_id=1, source_target_pairs={{0,1},{1,0},{2,3},{3,2},{4,5},{5,4},{6,7},{7,6},{8,9},{9,8},{10,11... | collective-permute-start | bytes 1572872 | tf_op jit(solution)/shard_map/ppermute | solution.py:474
  76.3 3.8 %collective-permute-start.12 = (bf16[128,2048]{1,0:T(8,128)(2,1)S(1)}, bf16[128,2048]{1,0:T(8,128)(2,1)}, u32[]{:S(2)}, u32[]{:S(2)}) collective-permute-start(bf16[128,2048]{1,0:T(8,128)(2,1)S(1)} %collective-permute-done.11.refs_2_), channel_id=1, source_target_pairs={{0,1},{1,0},{2,3},{3,2},{4,5},{5,4},{6,7},{7,6},{8,9},{9,8},{10,11... | collective-permute-start | bytes 1572872 | tf_op jit(solution)/shard_map/ppermute | solution.py:474
  76.9 5.1 %collective-permute-start.17 = (bf16[128,2048]{1,0:T(8,128)(2,1)S(1)}, bf16[128,2048]{1,0:T(8,128)(2,1)}, u32[]{:S(2)}, u32[]{:S(2)}) collective-permute-start(bf16[128,2048]{1,0:T(8,128)(2,1)S(1)} %collective-permute-done.14.refs_2_), channel_id=1, source_target_pairs={{0,1},{1,0},{2,3},{3,2},{4,5},{5,4},{6,7},{7,6},{8,9},{9,8},{10,11... | collective-permute-start | bytes 1572872 | tf_op jit(solution)/shard_map/ppermute | solution.py:474
  77.0 5.0 %collective-permute-start.16 = (bf16[128,2048]{1,0:T(8,128)(2,1)S(1)}, bf16[128,2048]{1,0:T(8,128)(2,1)}, u32[]{:S(2)}, u32[]{:S(2)}) collective-permute-start(bf16[128,2048]{1,0:T(8,128)(2,1)S(1)} %collective-permute-done.15.refs_0_), channel_id=1, source_target_pairs={{0,1},{1,0},{2,3},{3,2},{4,5},{5,4},{6,7},{7,6},{8,9},{9,8},{10,11... | collective-permute-start | bytes 1572872 | tf_op jit(solution)/shard_map/ppermute | solution.py:474
  77.4 15.1 %collective-permute-start.18 = (bf16[1024,256]{1,0:T(8,128)(2,1)}, bf16[1024,256]{1,0:T(8,128)(2,1)}, u32[]{:S(2)}, u32[]{:S(2)}) collective-permute-start(bf16[1024,256]{1,0:T(8,128)(2,1)} %get-tuple-element.39.refs_0_), channel_id=1, source_target_pairs={{0,4},{4,0},{8,12},{12,8},{16,20},{20,16},{24,28},{28,24},{1,5},{5... | collective-permute-start | bytes 1572872 | tf_op jit(solution)/shard_map/ppermute | solution.py:471
  78.9 23.9 %collective-permute-start.22 = (bf16[1024,256]{1,0:T(8,128)(2,1)}, bf16[1024,256]{1,0:T(8,128)(2,1)}, u32[]{:S(2)}, u32[]{:S(2)}) collective-permute-start(bf16[1024,256]{1,0:T(8,128)(2,1)} %get-tuple-element.44.refs_0_), channel_id=1, source_target_pairs={{0,4},{4,0},{8,12},{12,8},{16,20},{20,16},{24,28},{28,24},{1,5},{5... | collective-permute-start | bytes 1572872 | tf_op jit(solution)/shard_map/ppermute | solution.py:471
  95.2 13.5 %collective-permute-start.19 = (s16[272,256]{1,0:T(8,128)(2,1)S(1)}, s16[272,256]{1,0:T(8,128)(2,1)S(1)}, u32[]{:S(2)}, u32[]{:S(2)}) collective-permute-start(s16[272,256]{1,0:T(8,128)(2,1)S(1)} %get-tuple-element.48), channel_id=1, source_target_pairs={{0,8},{4,12},{8,0},{12,4},{16,24},{20,28},{24,16},{28,20},{1,9},{5... | collective-permute-start | bytes 417800 | tf_op jit(solution)/shard_map/ppermute | solution.py:471
  97.3 12.8 %collective-permute-start.20 = (s16[272,256]{1,0:T(8,128)(2,1)S(1)}, s16[272,256]{1,0:T(8,128)(2,1)S(1)}, u32[]{:S(2)}, u32[]{:S(2)}) collective-permute-start(s16[272,256]{1,0:T(8,128)(2,1)S(1)} %get-tuple-element.49), channel_id=1, source_target_pairs={{0,16},{4,20},{8,24},{12,28},{16,0},{20,4},{24,8},{28,12},{1,17},{... | collective-permute-start | bytes 417800 | tf_op jit(solution)/shard_map/ppermute | solution.py:471
  98.3 11.7 %collective-permute-start.21 = (s16[272,256]{1,0:T(8,128)(2,1)S(1)}, s16[272,256]{1,0:T(8,128)(2,1)S(1)}, u32[]{:S(2)}, u32[]{:S(2)}) collective-permute-start(s16[272,256]{1,0:T(8,128)(2,1)S(1)} %get-tuple-element.50), channel_id=1, source_target_pairs={{0,24},{4,28},{8,16},{12,20},{16,8},{20,12},{24,0},{28,4},{1,25},{... | collective-permute-start | bytes 417800 | tf_op jit(solution)/shard_map/ppermute | solution.py:471
  105.5 7.1 %collective-permute-start.23 = (s16[272,256]{1,0:T(8,128)(2,1)S(1)}, s16[272,256]{1,0:T(8,128)(2,1)S(1)}, u32[]{:S(2)}, u32[]{:S(2)}) collective-permute-start(s16[272,256]{1,0:T(8,128)(2,1)S(1)} %get-tuple-element.52), channel_id=1, source_target_pairs={{0,8},{4,12},{8,0},{12,4},{16,24},{20,28},{24,16},{28,20},{1,9},{5... | collective-permute-start | bytes 417800 | tf_op jit(solution)/shard_map/ppermute | solution.py:471
  107.6 12.9 %collective-permute-start.24 = (s16[272,256]{1,0:T(8,128)(2,1)S(1)}, s16[272,256]{1,0:T(8,128)(2,1)S(1)}, u32[]{:S(2)}, u32[]{:S(2)}) collective-permute-start(s16[272,256]{1,0:T(8,128)(2,1)S(1)} %get-tuple-element.53), channel_id=1, source_target_pairs={{0,16},{4,20},{8,24},{12,28},{16,0},{20,4},{24,8},{28,12},{1,17},{... | collective-permute-start | bytes 417800 | tf_op jit(solution)/shard_map/ppermute | solution.py:471
  108.7 11.9 %collective-permute-start.25 = (s16[272,256]{1,0:T(8,128)(2,1)S(1)}, s16[272,256]{1,0:T(8,128)(2,1)S(1)}, u32[]{:S(2)}, u32[]{:S(2)}) collective-permute-start(s16[272,256]{1,0:T(8,128)(2,1)S(1)} %get-tuple-element.54), channel_id=1, source_target_pairs={{0,24},{4,28},{8,16},{12,20},{16,8},{20,12},{24,0},{28,4},{1,25},{... | collective-permute-start | bytes 417800 | tf_op jit(solution)/shard_map/ppermute | solution.py:471

commit v3 on v2

--- a/solution.py
+++ b/solution.py
@@ -24,7 +24,7 @@
 ROWS = 256
 MIB = 1 << 20
 PLACES = 3
-CODE_ROWS = 16
+CODE_ROWS = 8
 CODE_BITS = 14.9
 LEAST = 2.0**-100
 
@@ -212,9 +212,8 @@
         if iteration + 1 < NS_ITERS:
             gram = dot_full(dot_full(gram, factor), factor)
     store_packed(out, product * (scale * step_scale))
-    high = pieces[0].shape[0]
-    out[high : high + 8, :] = jnp.zeros((8, HD), f32)
-    out[high : high + sums.shape[0], :] = sums[...]
+    first = pieces[0].shape[0] - 7
+    out[first : first + sums.shape[0], :] = sums[...]
 
 
 def hbm(value):
@@ -231,7 +230,7 @@
         functools.partial(series_kernel, step_scale=step_scale),
         in_specs=[VM] * (len(pieces) + 1),
         out_specs=VM,
-        out_shape=pltpu.VMEM((high + 8, wide), f32),
+        out_shape=pltpu.VMEM((high, wide), f32),
         compiler_params=pltpu.CompilerParams(vmem_limit_bytes=5 * MIB),
         name="series",
     )(*[vmem(p) for p in pieces], vmem(sums))
@@ -261,7 +260,6 @@
 def lead_kernel(place, *refs, parts, slots, heads):
     packed = refs[:parts]
     update, master, weights, factors = refs[parts:]
-    layers, height, _ = master.shape
     wide = 2 * HD
     for k in range(parts):
         planes = split_three(unpack_symmetric(packed[k][0 : 2 * HD + 8, :]))
@@ -269,8 +267,13 @@
         for spot, plane in enumerate((0, 1, 2, 0, 1, 0)):
             factors[away, spot * wide : (spot + 1) * wide, :] = planes[plane]
 
+    store_weights(place, factors, update, master, weights, slots, range(heads))
+
+
+def store_weights(place, factors, update, master, weights, slots, heads):
+    layers, height, _ = master.shape
     tall = min(height, ROWS)
-    for head in range(heads):
+    for spot, head in enumerate(heads):
         bucket = place[PLACES + head]
         start = pl.multiple_of(bucket_side(place, head) * HD, HD)
         factor = factors[bucket, :, pl.ds(start, HD)]
@@ -280,7 +283,8 @@
             rows = slice(low, low + tall)
             value = head_pair(update, rows, spots)
             ortho = jnp.dot(value, factor, preferred_element_type=f32)
-            weights[rows, cols] = (master[0, rows, cols] - ortho).astype(bf16)
+            rounded = (master[0, rows, cols] - ortho).astype(bf16)
+            weights[rows, spot * HD : (spot + 1) * HD] = rounded
 
 
 def lead_weights(place, packed, update, master, chunks):
@@ -300,50 +304,77 @@
     )(place, *[vmem(p) for p in packed], vmem(update), vmem(master))
 
 
-def apply_kernel(table, factors, update, master, new_master, *refs, chunks):
-    weights = refs[: chunks - 1]
-    fresh, sems = refs[chunks - 1 :]
+def next_kernel(place, factors, update, master, weights, *, slots, heads):
+    store_weights(place, factors, update, master, weights, slots, heads)
+
+
+def next_weights(place, factors, update, master, chunks, chunk):
+    _, height, width = master.shape
+    slots = width // HD
+    share = slots // chunks
+    heads = range(chunk * share, (chunk + 1) * share)
+    return pl.pallas_call(
+        functools.partial(next_kernel, slots=slots, heads=heads),
+        in_specs=[SM] + [VM] * 3,
+        out_specs=VM,
+        out_shape=pltpu.VMEM((height, width // chunks), bf16),
+        compiler_params=pltpu.CompilerParams(vmem_limit_bytes=9 * MIB),
+        name="next",
+    )(place, vmem(factors), vmem(update), vmem(master))
+
+
+def apply_kernel(place, factors, update, master, new_master, changes, fresh, arrive, leave):
     layers, height, width = master.shape
     slots = width // HD
     tall = min(height, ROWS)
-    piece = width // chunks
     parts = factors.shape[0]
-    spots = [head_spots(table, bucket, slots, layers * slots) for bucket in range(parts)]
-    copies = []
-    for i in range(height // tall):
-        rows = slice(i * tall, (i + 1) * tall)
+    blocks = [slice(low, low + tall) for low in range(0, height, tall)]
+    loads = []
+    for i, rows in enumerate(blocks):
+        loads.append(
+            (
+                pltpu.make_async_copy(update.at[:, rows, :], changes.at[:, rows, :], arrive.at[0, i]),
+                pltpu.make_async_copy(master.at[:, rows, :], fresh.at[:, rows, :], arrive.at[1, i]),
+            )
+        )
+        for load in loads[-1]:
+            load.start()
+    spots = [head_spots(place, bucket, slots, layers * slots) for bucket in range(parts)]
+    stores = []
+    for i, rows in enumerate(blocks):
+        for load in loads[i]:
+            load.wait()
         for bucket in range(parts):
-            value = head_pair(update, rows, spots[bucket])
+            value = head_pair(changes, rows, spots[bucket])
             ortho = jnp.dot(value, factors[bucket], preferred_element_type=f32)
             for side, (layer, cols) in enumerate(spots[bucket]):
                 part = ortho[:, side * HD : (side + 1) * HD]
-                fresh[layer, rows, cols] = master[layer, rows, cols] - part
-        copies.append(
-            pltpu.make_async_copy(fresh.at[:, rows, :], new_master.at[:, rows, :], sems.at[i])
+                fresh[layer, rows, cols] = fresh[layer, rows, cols] - part
+        stores.append(
+            pltpu.make_async_copy(fresh.at[:, rows, :], new_master.at[:, rows, :], leave.at[i])
         )
-        copies[-1].start()
-        for c in range(1, chunks):
-            cols = slice(c * piece, (c + 1) * piece)
-            weights[c - 1][rows, :] = fresh[0, rows, cols].astype(bf16)
-    for copy in copies:
-        copy.wait()
-
-
-def apply_update(table, factors, update, master, chunks):
-    _, height, width = master.shape
-    return pl.pallas_call(
-        functools.partial(apply_kernel, chunks=chunks),
-        in_specs=[SM] + [VM] * 3,
-        out_specs=[pl.BlockSpec(memory_space=pl.ANY)] + [VM] * (chunks - 1),
+        stores[-1].start()
+    for store in stores:
+        store.wait()
+
+
+def apply_update(place, factors, update, master):
+    blocks = master.shape[1] // min(master.shape[1], ROWS)
+    anywhere = pl.BlockSpec(memory_space=pl.ANY)
+    return pl.pallas_call(
+        apply_kernel,
+        in_specs=[SM, VM, anywhere, anywhere],
+        out_specs=anywhere,
         scratch_shapes=[
             pltpu.VMEM(master.shape, f32),
-            pltpu.SemaphoreType.DMA((height // min(height, ROWS),)),
+            pltpu.VMEM(master.shape, f32),
+            pltpu.SemaphoreType.DMA((2, blocks)),
+            pltpu.SemaphoreType.DMA((blocks,)),
         ],
-        out_shape=[jax.ShapeDtypeStruct(master.shape, f32)]
-        + [pltpu.VMEM((height, width // chunks), bf16)] * (chunks - 1),
-        compiler_params=pltpu.CompilerParams(vmem_limit_bytes=9 * MIB),
+        out_shape=jax.ShapeDtypeStruct(master.shape, f32),
+        compiler_params=pltpu.CompilerParams(vmem_limit_bytes=13 * MIB),
         name="apply",
-    )(table, vmem(factors), vmem(update), vmem(master))
+    )(place, vmem(factors), hbm(update), hbm(master))
 
 
 def norm_kernel(place, *refs, parts, base, features):
@@ -358,12 +389,13 @@
         away = k ^ place[0] ^ place[1]
         inverse = sums[away]
         for low in range(0, height, HD):
-            spot = (base + low) // HD
+            spot = 1 + (base + low) // HD
             column = jnp.broadcast_to(inverse[spot : spot + 1, :], (HD, HD)).T
             for left in range(0, width, HD):
                 cols = slice(left, left + HD)
+                own = pl.ds(pl.multiple_of(place[0] * width + left, HD), HD)
                 values = pieces[k][low : low + HD, cols].astype(f32)
-                out[away, low : low + HD, cols] = (values * column * gain[:, cols]).astype(bf16)
+                out[away, low : low + HD, cols] = (values * column * gain[:, own]).astype(bf16)
 
 
 def normalise(place, pieces, packed, gain, base, features):
@@ -510,7 +542,7 @@
 
     packed = [own] + [swap_dp(own, k * members) for k in range(1, parts)]
     lead, factors = lead_weights(place, packed, update, master, CHUNKS)
-    gain = lax.dynamic_slice_in_dim(norm_gain, row * share, share, 0)[None, :]
+    gain = norm_gain[None, :]
 
     def shared(side, start):
         held = {side * (tp // 2): after(sent[side], own)}
@@ -526,9 +558,9 @@
         halves = [held[offset] for offset in range(parts)]
         return normalise(place, halves, packed, gain, side * half, features)
 
-    near_normed = shared(0, lead)
-    new_master, *others = apply_update(place, factors, update, master, CHUNKS)
-    normed = (near_normed, shared(1, others[0] if others else lead))
+    others = [next_weights(place, factors, update, master, CHUNKS, c) for c in range(1, CHUNKS)]
+    near_normed = shared(0, (others or [lead])[-1])
+    normed = (near_normed, shared(1, near_normed))
 
     pieces = []
     for piece in [lead] + others:
@@ -536,6 +568,7 @@
         partial = project(place, *normed, gathered)
         sums_of = [swap_dp(partial[k], k * members) for k in range(1, parts)]
         pieces.append([partial[0]] + sums_of)
+    new_master = apply_update(place, factors, update, master)
     return (new_master, new_momentum, finish(pieces))
 
 

time: 122 us -> 151 us (1.24)
  starting transfers between devices: 35.1 us -> 51.3 us
  waiting for transfers between devices: 48.7 us -> 63.7 us
  local copies, waits for them, and re-layouts: 1.82 us -> 0.09 us
    ppermute x9, starting transfers between devices: 8.63 us -> 20 us  [swap_tensor(): return lax.ppermute(value, 'tensor', [(i, i ^ bits) for i in range(tp)])]
    ppermute x9, waiting for transfers between devices: 2.45 us -> 12.1 us  [swap_tensor(): return lax.ppermute(value, 'tensor', [(i, i ^ bits) for i in range(tp)])]
    ppermute x15, starting transfers between devices: 21.6 us -> 28.5 us  [swap_dp(): return lax.ppermute(value, 'dp', [(i, i ^ bits) for i in range(dp)])]
    ppermute x2, waiting for transfers between devices: 0.01 us -> 4.3 us  [turn(): return lax.ppermute(value, ('dp', 'tensor'), pairs)]
    pallas_call x1 -> x2, Pallas kernels: 6.79 us -> 10.2 us  [the longest x1 7.83 us: apply_update(): pl.pallas_call(apply_kernel, in_specs=[SM, VM, anywhere, anywhere], out_s...]
    ppermute x2, starting transfers between devices: 4.88 us -> 2.78 us  [turn(): return lax.ppermute(value, ('dp', 'tensor'), pairs)]
  transfers between devices with their start and end apart: 26 -> 26, of which waited for: 9 -> 12; matrix products, arithmetic and copies ran while one was open for 1% -> 0% of each run, Pallas kernels for 27% -> 16%
where the time goes in v3:
time: 151 us
  waiting for transfers between devices  63.7 us (42%)
  starting transfers between devices  51.3 us (34%)
  Pallas kernels  33.9 us (22%)
    ppermute x15, waiting for transfers between devices, swap_dp(): return lax.ppermute(value, 'dp', [(i, i ^ bits) for i in range(dp)])  47.3 us
    ppermute x15, starting transfers between devices, swap_dp(): return lax.ppermute(value, 'dp', [(i, i ^ bits) for i in range(dp)])  28.5 us
    ppermute x9, starting transfers between devices, swap_tensor(): return lax.ppermute(value, 'tensor', [(i, i ^ bits) for i in range(tp)])  20 us
    ppermute x9, waiting for transfers between devices, swap_tensor(): return lax.ppermute(value, 'tensor', [(i, i ^ bits) for i in range(tp)])  12.1 us
    pallas_call x1, Pallas kernels, local_grams(): pl.pallas_call(functools.partial(gram_kernel, parts=parts), in_specs=[SM,...  9.02 us
    pallas_call x1, Pallas kernels, apply_update(): pl.pallas_call(apply_kernel, in_specs=[SM, VM, anywhere, anywhere], out_s...  7.83 us
    ppermute x2, waiting for transfers between devices, turn(): return lax.ppermute(value, ('dp', 'tensor'), pairs)  4.3 us
    pallas_call x1, Pallas kernels, series(): pl.pallas_call(functools.partial(series_kernel, step_scale=step_scale), i...  4.27 us
  transfers between devices with their start and end apart: 26, of which 12 were waited for; matrix products, arithmetic and copies ran while one was open for 0% of the time, Pallas kernels for 16%

profile of v3, /device:TPU:0, one launch (start us, length us, event | category | flops | bytes accessed | tf_op | source)
XLA Modules:
  0.0 150.9 jit_solution(5689904693248712191)
XLA Ops:
  1.4 9.0 %grams.1 = (f32[2,1024,512]{2,1,0:T(8,128)}, f32[2,1024,512]{2,1,0:T(8,128)S(1)}, f32[264,128]{1,0:T(8,128)S(1)}, f32[264,128]{1,0:T(8,128)S(1)}, f32[264,128]{1,0:T(8,128)S(1)}, /*index=5*/f32[264,128]{1,0:T(8,128)S(1)}) custom-call(s32[11]{0:T(128)S(1)} %pad_add_fusion.place, f32[2,1024,512]{2,1,0:T(8,128)} %momentum.1, f32[2,1024,512]{2,1,0:T(8,128)} %gradient.1), custom_call_target="tpu_custom_call" | custom-call | tf_op jit(solution)/shard_map/grams/pallas_call | solution.py:176
  10.4 5.1 %collective-permute-start.2 = (f32[264,128]{1,0:T(8,128)S(1)}, f32[264,128]{1,0:T(8,128)S(1)}, u32[]{:S(2)}, u32[]{:S(2)}) collective-permute-start(f32[264,128]{1,0:T(8,128)S(1)} %get-tuple-element.30), channel_id=1, source_target_pairs={{0,24},{4,28},{8,16},{12,20},{16,8},{20,12},{24,0},{28,4},{1,25},{... | collective-permute-start | bytes 405512 | tf_op jit(solution)/shard_map/ppermute | solution.py:503
  16.5 1.7 %collective-permute-start.4 = (f32[256]{0:T(256)S(1)}, f32[256]{0:T(256)S(1)}, u32[]{:S(2)}, u32[]{:S(2)}) collective-permute-start(f32[256]{0:T(256)S(1)} %multiply_reduce_fusion), channel_id=1, source_target_pairs={{0,2},{1,3},{2,0},{3,1},{4,6},{5,7},{6,4},{7,5},{8,10},{9,11},{10,... | collective-permute-start | bytes 3080 | tf_op jit(solution)/shard_map/ppermute | solution.py:506
  20.1 3.7 %collective-permute-start.13 = (bf16[128,2048]{1,0:T(8,128)(2,1)S(1)}, bf16[128,2048]{1,0:T(8,128)(2,1)S(1)}, u32[]{:S(2)}, u32[]{:S(2)}) collective-permute-start(bf16[128,2048]{1,0:T(8,128)(2,1)S(1)} %slice.7), channel_id=1, source_target_pairs={{0,2},{1,3},{2,0},{3,1},{4,6},{5,7},{6,4},{7,5},{8,10},{9,11},{10,... | collective-permute-start | bytes 1572872 | tf_op jit(solution)/shard_map/ppermute | solution.py:506
  25.2 14.0 %collective-permute-done.1 = f32[264,128]{1,0:T(8,128)S(1)} collective-permute-done((f32[264,128]{1,0:T(8,128)S(1)}, f32[264,128]{1,0:T(8,128)S(1)}, u32[]{:S(2)}, u32[]{:S(2)}) %collective-permute-start.1) | collective-permute-done | bytes 135200 | tf_op jit(solution)/shard_map/ppermute | solution.py:503
  39.2 1.6 %collective-permute-start.3 = (f32[264,128]{1,0:T(8,128)S(1)}, f32[264,128]{1,0:T(8,128)S(1)}, u32[]{:S(2)}, u32[]{:S(2)}) collective-permute-start(f32[264,128]{1,0:T(8,128)S(1)} %add_add_fusion.refs_0_), channel_id=1, source_target_pairs={{0,4},{4,0},{8,12},{12,8},{16,20},{20,16},{24,28},{28,24},{1,5},{5... | collective-permute-start | bytes 405512 | tf_op jit(solution)/shard_map/ppermute | solution.py:503
  40.8 3.5 %collective-permute-done.3.refs_1_ = f32[264,128]{1,0:T(8,128)S(1)} collective-permute-done((f32[264,128]{1,0:T(8,128)S(1)}, f32[264,128]{1,0:T(8,128)S(1)}, u32[]{:S(2)}, u32[]{:S(2)}) %collective-permute-start.3) | collective-permute-done | bytes 135200 | tf_op jit(solution)/shard_map/ppermute | solution.py:503
  44.3 4.3 %series.1.refs_0_.refs_4_ = f32[264,128]{1,0:T(8,128)S(1)} custom-call(f32[264,128]{1,0:T(8,128)S(1)} %add_add_fusion.refs_0_, f32[264,128]{1,0:T(8,128)S(1)} %collective-permute-done.3.refs_1_, f32[2,128]{1,0:T(2,128)S(1)} %add_bitcast_fusion.refs_2_), custom_call_target="tpu_custom_call" | custom-call | tf_op jit(solution)/shard_map/series/pallas_call | solution.py:229
  48.6 2.4 %collective-permute-start.11 = (bf16[128,2048]{1,0:T(8,128)(2,1)S(1)}, bf16[128,2048]{1,0:T(8,128)(2,1)S(1)}, u32[]{:S(2)}, u32[]{:S(2)}) collective-permute-start(bf16[128,2048]{1,0:T(8,128)(2,1)S(1)} %collective-permute-done.9.refs_0_), channel_id=1, source_target_pairs={{0,2},{1,3},{2,0},{3,1},{4,6},{5,7},{6,4},{7,5},{8,10},{9,11},{10,... | collective-permute-start | bytes 1572872 | tf_op jit(solution)/shard_map/ppermute | solution.py:506
  51.0 2.1 %collective-permute-start.14 = (bf16[128,2048]{1,0:T(8,128)(2,1)S(1)}, bf16[128,2048]{1,0:T(8,128)(2,1)S(1)}, u32[]{:S(2)}, u32[]{:S(2)}) collective-permute-start(bf16[128,2048]{1,0:T(8,128)(2,1)S(1)} %collective-permute-done.13), channel_id=1, source_target_pairs={{0,18},{1,26},{2,2},{3,10},{4,22},{5,30},{6,6},{7,14},{8,19},{9,27... | collective-permute-start | bytes 1572872 | tf_op jit(solution)/shard_map/ppermute | solution.py:519
  53.1 2.2 %collective-permute-start.6 = (f32[264,128]{1,0:T(8,128)S(1)}, f32[264,128]{1,0:T(8,128)S(1)}, u32[]{:S(2)}, u32[]{:S(2)}) collective-permute-start(f32[264,128]{1,0:T(8,128)S(1)} %series.1.refs_0_.refs_4_), channel_id=1, source_target_pairs={{0,8},{4,12},{8,0},{12,4},{16,24},{20,28},{24,16},{28,20},{1,9},{5... | collective-permute-start | bytes 405512 | tf_op jit(solution)/shard_map/ppermute | solution.py:503
  55.6 2.2 %collective-permute-start.8 = (f32[264,128]{1,0:T(8,128)S(1)}, f32[264,128]{1,0:T(8,128)S(1)}, u32[]{:S(2)}, u32[]{:S(2)}) collective-permute-start(f32[264,128]{1,0:T(8,128)S(1)} %series.1.refs_0_.refs_4_), channel_id=1, source_target_pairs={{0,24},{4,28},{8,16},{12,20},{16,8},{20,12},{24,0},{28,4},{1,25},{... | collective-permute-start | bytes 405512 | tf_op jit(solution)/shard_map/ppermute | solution.py:503
  57.8 9.7 %collective-permute-done.6.refs_1_.refs_5_ = f32[264,128]{1,0:T(8,128)S(1)} collective-permute-done((f32[264,128]{1,0:T(8,128)S(1)}, f32[264,128]{1,0:T(8,128)S(1)}, u32[]{:S(2)}, u32[]{:S(2)}) %collective-permute-start.6) | collective-permute-done | bytes 135200 | tf_op jit(solution)/shard_map/ppermute | solution.py:503
  67.5 2.9 %collective-permute-done.7.refs_2_.refs_6_ = f32[264,128]{1,0:T(8,128)S(1)} collective-permute-done((f32[264,128]{1,0:T(8,128)S(1)}, f32[264,128]{1,0:T(8,128)S(1)}, u32[]{:S(2)}, u32[]{:S(2)}) %collective-permute-start.7) | collective-permute-done | bytes 135200 | tf_op jit(solution)/shard_map/ppermute | solution.py:503
  70.4 2.9 %collective-permute-done.8.refs_3_.refs_7_ = f32[264,128]{1,0:T(8,128)S(1)} collective-permute-done((f32[264,128]{1,0:T(8,128)S(1)}, f32[264,128]{1,0:T(8,128)S(1)}, u32[]{:S(2)}, u32[]{:S(2)}) %collective-permute-start.8) | collective-permute-done | bytes 135200 | tf_op jit(solution)/shard_map/ppermute | solution.py:503
  73.3 2.8 %lead.1 = (bf16[1024,256]{1,0:T(8,128)(2,1)S(1)}, bf16[4,1536,256]{2,1,0:T(8,128)(2,1)S(1)}) custom-call(s32[11]{0:T(128)S(1)} %pad_add_fusion.place, f32[264,128]{1,0:T(8,128)S(1)} %series.1.refs_0_.refs_4_, f32[264,128]{1,0:T(8,128)S(1)} %collective-permute-done.6.refs_1_.refs_5_, f32[264,128]{1,0:T(8,128)S(1)} %collective-permute-done.7.refs_2_.refs_6_, ...), custom_call_target="tpu_custom_call" | custom-call | tf_op jit(solution)/shard_map/lead/pallas_call | solution.py:294
  76.2 2.4 %next.1.refs_0_ = bf16[1024,256]{1,0:T(8,128)(2,1)S(1)} custom-call(s32[11]{0:T(128)S(1)} %pad_add_fusion.place, bf16[4,1536,256]{2,1,0:T(8,128)(2,1)S(1)} %get-tuple-element.32.factors, f32[2,1024,512]{2,1,0:T(8,128)S(1)} %get-tuple-element.31.refs_4_.update, f32[2,1024,512]{2,1,0:T(8,128)S(1)} %copy-done), custom_call_target="tpu_custom_call" | custom-call | tf_op jit(solution)/shard_map/next/pallas_call | solution.py:316
  79.6 4.3 %collective-permute-done.14.refs_2_ = bf16[128,2048]{1,0:T(8,128)(2,1)S(1)} collective-permute-done((bf16[128,2048]{1,0:T(8,128)(2,1)S(1)}, bf16[128,2048]{1,0:T(8,128)(2,1)S(1)}, u32[]{:S(2)}, u32[]{:S(2)}) %collective-permute-start.14) | collective-permute-done | bytes 524320 | tf_op jit(solution)/shard_map/ppermute | solution.py:519
  83.9 9.3 %collective-permute-start.15 = (bf16[128,2048]{1,0:T(8,128)(2,1)S(1)}, bf16[128,2048]{1,0:T(8,128)(2,1)S(1)}, u32[]{:S(2)}, u32[]{:S(2)}) collective-permute-start(bf16[128,2048]{1,0:T(8,128)(2,1)S(1)} %collective-permute-done.14.refs_2_), channel_id=1, source_target_pairs={{0,2},{1,3},{2,0},{3,1},{4,6},{5,7},{6,4},{7,5},{8,10},{9,11},{10,... | collective-permute-start | bytes 1572872 | tf_op jit(solution)/shard_map/ppermute | solution.py:506
  94.6 10.8 %collective-permute-done.15.refs_0_ = bf16[128,2048]{1,0:T(8,128)(2,1)S(1)} collective-permute-done((bf16[128,2048]{1,0:T(8,128)(2,1)S(1)}, bf16[128,2048]{1,0:T(8,128)(2,1)S(1)}, u32[]{:S(2)}, u32[]{:S(2)}) %collective-permute-start.15) | collective-permute-done | bytes 524320 | tf_op jit(solution)/shard_map/ppermute | solution.py:506
  105.9 1.5 %collective-permute-start.18 = (bf16[1024,256]{1,0:T(8,128)(2,1)S(1)}, bf16[1024,256]{1,0:T(8,128)(2,1)S(1)}, u32[]{:S(2)}, u32[]{:S(2)}) collective-permute-start(bf16[1024,256]{1,0:T(8,128)(2,1)S(1)} %get-tuple-element.42.refs_0_), channel_id=1, source_target_pairs={{0,4},{4,0},{8,12},{12,8},{16,20},{20,16},{24,28},{28,24},{1,5},{5... | collective-permute-start | bytes 1572872 | tf_op jit(solution)/shard_map/ppermute | solution.py:503
  109.4 11.3 %collective-permute-done.18.refs_1_ = bf16[1024,256]{1,0:T(8,128)(2,1)S(1)} collective-permute-done((bf16[1024,256]{1,0:T(8,128)(2,1)S(1)}, bf16[1024,256]{1,0:T(8,128)(2,1)S(1)}, u32[]{:S(2)}, u32[]{:S(2)}) %collective-permute-start.18) | collective-permute-done | bytes 524320 | tf_op jit(solution)/shard_map/ppermute | solution.py:503
  120.7 1.9 %project.2 = (f32[256,256]{1,0:T(8,128)S(1)}, s16[264,256]{1,0:T(8,128)(2,1)S(1)}, s16[264,256]{1,0:T(8,128)(2,1)S(1)}, s16[264,256]{1,0:T(8,128)(2,1)S(1)}) custom-call(s32[11]{0:T(128)S(1)} %pad_add_fusion.place, bf16[4,128,2048]{2,1,0:T(8,128)(2,1)S(1)} %normalise.2.near, bf16[4,128,2048]{2,1,0:T(8,128)(2,1)S(1)} %normalise.3.far, ...), custom_call_target="tpu_custom_call" | custom-call | tf_op jit(solution)/shard_map/project/pallas_call | solution.py:473
  122.7 3.9 %collective-permute-start.19 = (s16[264,256]{1,0:T(8,128)(2,1)S(1)}, s16[264,256]{1,0:T(8,128)(2,1)S(1)}, u32[]{:S(2)}, u32[]{:S(2)}) collective-permute-start(s16[264,256]{1,0:T(8,128)(2,1)S(1)} %get-tuple-element.44), channel_id=1, source_target_pairs={{0,8},{4,12},{8,0},{12,4},{16,24},{20,28},{24,16},{28,20},{1,9},{5... | collective-permute-start | bytes 405512 | tf_op jit(solution)/shard_map/ppermute | solution.py:503
  126.5 2.0 %collective-permute-start.20 = (s16[264,256]{1,0:T(8,128)(2,1)S(1)}, s16[264,256]{1,0:T(8,128)(2,1)S(1)}, u32[]{:S(2)}, u32[]{:S(2)}) collective-permute-start(s16[264,256]{1,0:T(8,128)(2,1)S(1)} %get-tuple-element.45), channel_id=1, source_target_pairs={{0,16},{4,20},{8,24},{12,28},{16,0},{20,4},{24,8},{28,12},{1,17},{... | collective-permute-start | bytes 405512 | tf_op jit(solution)/shard_map/ppermute | solution.py:503
  128.5 1.4 collective-permute-start.21
  131.0 1.9 %project.3 = (f32[256,256]{1,0:T(8,128)S(1)}, s16[264,256]{1,0:T(8,128)(2,1)S(1)}, s16[264,256]{1,0:T(8,128)(2,1)S(1)}, s16[264,256]{1,0:T(8,128)(2,1)S(1)}) custom-call(s32[11]{0:T(128)S(1)} %pad_add_fusion.place, bf16[4,128,2048]{2,1,0:T(8,128)(2,1)S(1)} %normalise.2.near, bf16[4,128,2048]{2,1,0:T(8,128)(2,1)S(1)} %normalise.3.far, ...), custom_call_target="tpu_custom_call" | custom-call | tf_op jit(solution)/shard_map/project/pallas_call | solution.py:473
  132.9 3.9 %collective-permute-start.23 = (s16[264,256]{1,0:T(8,128)(2,1)S(1)}, s16[264,256]{1,0:T(8,128)(2,1)S(1)}, u32[]{:S(2)}, u32[]{:S(2)}) collective-permute-start(s16[264,256]{1,0:T(8,128)(2,1)S(1)} %get-tuple-element.48), channel_id=1, source_target_pairs={{0,8},{4,12},{8,0},{12,4},{16,24},{20,28},{24,16},{28,20},{1,9},{5... | collective-permute-start | bytes 405512 | tf_op jit(solution)/shard_map/ppermute | solution.py:503
  136.8 2.0 %collective-permute-start.24 = (s16[264,256]{1,0:T(8,128)(2,1)S(1)}, s16[264,256]{1,0:T(8,128)(2,1)S(1)}, u32[]{:S(2)}, u32[]{:S(2)}) collective-permute-start(s16[264,256]{1,0:T(8,128)(2,1)S(1)} %get-tuple-element.49), channel_id=1, source_target_pairs={{0,16},{4,20},{8,24},{12,28},{16,0},{20,4},{24,8},{28,12},{1,17},{... | collective-permute-start | bytes 405512 | tf_op jit(solution)/shard_map/ppermute | solution.py:503
  138.8 1.4 collective-permute-start.25
  140.2 7.8 %apply.1 = f32[2,1024,512]{2,1,0:T(8,128)} custom-call(s32[11]{0:T(128)S(1)} %pad_add_fusion.place, bf16[4,1536,256]{2,1,0:T(8,128)(2,1)S(1)} %get-tuple-element.32.factors, f32[2,1024,512]{2,1,0:T(8,128)} %copy-done.1, f32[2,1024,512]{2,1,0:T(8,128)} %master.3), custom_call_target="tpu_custom_call" | custom-call | tf_op jit(solution)/shard_map/apply/pallas_call | solution.py:364
  148.0 2.0 %collective-permute-done.24.refs_6_ = s16[264,256]{1,0:T(8,128)(2,1)S(1)} collective-permute-done((s16[264,256]{1,0:T(8,128)(2,1)S(1)}, s16[264,256]{1,0:T(8,128)(2,1)S(1)}, u32[]{:S(2)}, u32[]{:S(2)}) %collective-permute-start.24) | collective-permute-done | bytes 135200 | tf_op jit(solution)/shard_map/ppermute | solution.py:503
  (45 shorter events, 12.1 us)
Async XLA Ops:
  1.4 14.8 %copy-start.3 = (bf16[256,2048]{1,0:T(8,128)(2,1)S(1)}, bf16[256,2048]{1,0:T(8,128)(2,1)}, u32[]{:S(2)}) copy-start(bf16[256,2048]{1,0:T(8,128)(2,1)} %param.10) | copy-start | bytes 3145732
  10.4 65.8 %copy-start.1 = (f32[2,1024,512]{2,1,0:T(8,128)}, f32[2,1024,512]{2,1,0:T(8,128)S(1)}, u32[]{:S(2)}) copy-start(f32[2,1024,512]{2,1,0:T(8,128)S(1)} %get-tuple-element.31.refs_4_.update) | copy-start | bytes 12582916
  10.4 62.9 %copy-start = (f32[2,1024,512]{2,1,0:T(8,128)S(1)}, f32[2,1024,512]{2,1,0:T(8,128)}, u32[]{:S(2)}) copy-start(f32[2,1024,512]{2,1,0:T(8,128)} %master.3) | copy-start | bytes 12582916
  10.4 13.5 %collective-permute-start.2 = (f32[264,128]{1,0:T(8,128)S(1)}, f32[264,128]{1,0:T(8,128)S(1)}, u32[]{:S(2)}, u32[]{:S(2)}) collective-permute-start(f32[264,128]{1,0:T(8,128)S(1)} %get-tuple-element.30), channel_id=1, source_target_pairs={{0,24},{4,28},{8,16},{12,20},{16,8},{20,12},{24,0},{28,4},{1,25},{... | collective-permute-start | bytes 405512 | tf_op jit(solution)/shard_map/ppermute | solution.py:503
  15.6 23.6 %collective-permute-start.1 = (f32[264,128]{1,0:T(8,128)S(1)}, f32[264,128]{1,0:T(8,128)S(1)}, u32[]{:S(2)}, u32[]{:S(2)}) collective-permute-start(f32[264,128]{1,0:T(8,128)S(1)} %get-tuple-element.29), channel_id=1, source_target_pairs={{0,16},{4,20},{8,24},{12,28},{16,0},{20,4},{24,8},{28,12},{1,17},{... | collective-permute-start | bytes 405512 | tf_op jit(solution)/shard_map/ppermute | solution.py:503
  15.6 23.6 %collective-permute-start = (f32[264,128]{1,0:T(8,128)S(1)}, f32[264,128]{1,0:T(8,128)S(1)}, u32[]{:S(2)}, u32[]{:S(2)}) collective-permute-start(f32[264,128]{1,0:T(8,128)S(1)} %get-tuple-element.28), channel_id=1, source_target_pairs={{0,8},{4,12},{8,0},{12,4},{16,24},{20,28},{24,16},{28,20},{1,9},{5... | collective-permute-start | bytes 405512 | tf_op jit(solution)/shard_map/ppermute | solution.py:503
  16.5 3.6 %collective-permute-start.4 = (f32[256]{0:T(256)S(1)}, f32[256]{0:T(256)S(1)}, u32[]{:S(2)}, u32[]{:S(2)}) collective-permute-start(f32[256]{0:T(256)S(1)} %multiply_reduce_fusion), channel_id=1, source_target_pairs={{0,2},{1,3},{2,0},{3,1},{4,6},{5,7},{6,4},{7,5},{8,10},{9,11},{10,... | collective-permute-start | bytes 3080 | tf_op jit(solution)/shard_map/ppermute | solution.py:506
  18.2 30.3 %collective-permute-start.9 = (bf16[128,2048]{1,0:T(8,128)(2,1)S(1)}, bf16[128,2048]{1,0:T(8,128)(2,1)S(1)}, u32[]{:S(2)}, u32[]{:S(2)}) collective-permute-start(bf16[128,2048]{1,0:T(8,128)(2,1)S(1)} %slice.6), channel_id=1, source_target_pairs={{0,0},{1,8},{2,16},{3,24},{4,4},{5,12},{6,20},{7,28},{8,1},{9,9},{... | collective-permute-start | bytes 1572872 | tf_op jit(solution)/shard_map/ppermute | solution.py:519
  20.1 30.9 %collective-permute-start.13 = (bf16[128,2048]{1,0:T(8,128)(2,1)S(1)}, bf16[128,2048]{1,0:T(8,128)(2,1)S(1)}, u32[]{:S(2)}, u32[]{:S(2)}) collective-permute-start(bf16[128,2048]{1,0:T(8,128)(2,1)S(1)} %slice.7), channel_id=1, source_target_pairs={{0,2},{1,3},{2,0},{3,1},{4,6},{5,7},{6,4},{7,5},{8,10},{9,11},{10,... | collective-permute-start | bytes 1572872 | tf_op jit(solution)/shard_map/ppermute | solution.py:506
  23.9 16.9 %collective-permute-start.5 = (f32[256]{0:T(256)S(1)}, f32[256]{0:T(256)S(1)}, u32[]{:S(2)}, u32[]{:S(2)}) collective-permute-start(f32[256]{0:T(256)S(1)} %add.24), channel_id=1, source_target_pairs={{0,1},{1,0},{2,3},{3,2},{4,5},{5,4},{6,7},{7,6},{8,9},{9,8},{10,11... | collective-permute-start | bytes 3080 | tf_op jit(solution)/shard_map/ppermute | solution.py:506
  39.2 5.1 %collective-permute-start.3 = (f32[264,128]{1,0:T(8,128)S(1)}, f32[264,128]{1,0:T(8,128)S(1)}, u32[]{:S(2)}, u32[]{:S(2)}) collective-permute-start(f32[264,128]{1,0:T(8,128)S(1)} %add_add_fusion.refs_0_), channel_id=1, source_target_pairs={{0,4},{4,0},{8,12},{12,8},{16,20},{20,16},{24,28},{28,24},{1,5},{5... | collective-permute-start | bytes 405512 | tf_op jit(solution)/shard_map/ppermute | solution.py:503
  48.6 30.9 %collective-permute-start.11 = (bf16[128,2048]{1,0:T(8,128)(2,1)S(1)}, bf16[128,2048]{1,0:T(8,128)(2,1)S(1)}, u32[]{:S(2)}, u32[]{:S(2)}) collective-permute-start(bf16[128,2048]{1,0:T(8,128)(2,1)S(1)} %collective-permute-done.9.refs_0_), channel_id=1, source_target_pairs={{0,2},{1,3},{2,0},{3,1},{4,6},{5,7},{6,4},{7,5},{8,10},{9,11},{10,... | collective-permute-start | bytes 1572872 | tf_op jit(solution)/shard_map/ppermute | solution.py:506
  51.0 32.9 %collective-permute-start.14 = (bf16[128,2048]{1,0:T(8,128)(2,1)S(1)}, bf16[128,2048]{1,0:T(8,128)(2,1)S(1)}, u32[]{:S(2)}, u32[]{:S(2)}) collective-permute-start(bf16[128,2048]{1,0:T(8,128)(2,1)S(1)} %collective-permute-done.13), channel_id=1, source_target_pairs={{0,18},{1,26},{2,2},{3,10},{4,22},{5,30},{6,6},{7,14},{8,19},{9,27... | collective-permute-start | bytes 1572872 | tf_op jit(solution)/shard_map/ppermute | solution.py:519
  53.1 14.3 %collective-permute-start.6 = (f32[264,128]{1,0:T(8,128)S(1)}, f32[264,128]{1,0:T(8,128)S(1)}, u32[]{:S(2)}, u32[]{:S(2)}) collective-permute-start(f32[264,128]{1,0:T(8,128)S(1)} %series.1.refs_0_.refs_4_), channel_id=1, source_target_pairs={{0,8},{4,12},{8,0},{12,4},{16,24},{20,28},{24,16},{28,20},{1,9},{5... | collective-permute-start | bytes 405512 | tf_op jit(solution)/shard_map/ppermute | solution.py:503
  55.4 15.1 %collective-permute-start.7 = (f32[264,128]{1,0:T(8,128)S(1)}, f32[264,128]{1,0:T(8,128)S(1)}, u32[]{:S(2)}, u32[]{:S(2)}) collective-permute-start(f32[264,128]{1,0:T(8,128)S(1)} %series.1.refs_0_.refs_4_), channel_id=1, source_target_pairs={{0,16},{4,20},{8,24},{12,28},{16,0},{20,4},{24,8},{28,12},{1,17},{... | collective-permute-start | bytes 405512 | tf_op jit(solution)/shard_map/ppermute | solution.py:503
  55.6 17.7 %collective-permute-start.8 = (f32[264,128]{1,0:T(8,128)S(1)}, f32[264,128]{1,0:T(8,128)S(1)}, u32[]{:S(2)}, u32[]{:S(2)}) collective-permute-start(f32[264,128]{1,0:T(8,128)S(1)} %series.1.refs_0_.refs_4_), channel_id=1, source_target_pairs={{0,24},{4,28},{8,16},{12,20},{16,8},{20,12},{24,0},{28,4},{1,25},{... | collective-permute-start | bytes 405512 | tf_op jit(solution)/shard_map/ppermute | solution.py:503
  76.2 17.1 %copy-start.2 = (f32[8192]{0:T(1024)S(1)}, f32[8192]{0:T(1024)}, u32[]{:S(2)}) copy-start(f32[8192]{0:T(1024)} %param.11) | copy-start | bytes 98308
  78.6 14.6 %collective-permute-start.10 = (bf16[128,2048]{1,0:T(8,128)(2,1)S(1)}, bf16[128,2048]{1,0:T(8,128)(2,1)S(1)}, u32[]{:S(2)}, u32[]{:S(2)}) collective-permute-start(bf16[128,2048]{1,0:T(8,128)(2,1)S(1)} %collective-permute-done.9.refs_0_), channel_id=1, source_target_pairs={{0,1},{1,0},{2,3},{3,2},{4,5},{5,4},{6,7},{7,6},{8,9},{9,8},{10,11... | collective-permute-start | bytes 1572872 | tf_op jit(solution)/shard_map/ppermute | solution.py:506
  79.5 13.7 %collective-permute-start.12 = (bf16[128,2048]{1,0:T(8,128)(2,1)S(1)}, bf16[128,2048]{1,0:T(8,128)(2,1)S(1)}, u32[]{:S(2)}, u32[]{:S(2)}) collective-permute-start(bf16[128,2048]{1,0:T(8,128)(2,1)S(1)} %collective-permute-done.11.refs_2_), channel_id=1, source_target_pairs={{0,1},{1,0},{2,3},{3,2},{4,5},{5,4},{6,7},{7,6},{8,9},{9,8},{10,11... | collective-permute-start | bytes 1572872 | tf_op jit(solution)/shard_map/ppermute | solution.py:506
  83.9 21.5 %collective-permute-start.15 = (bf16[128,2048]{1,0:T(8,128)(2,1)S(1)}, bf16[128,2048]{1,0:T(8,128)(2,1)S(1)}, u32[]{:S(2)}, u32[]{:S(2)}) collective-permute-start(bf16[128,2048]{1,0:T(8,128)(2,1)S(1)} %collective-permute-done.14.refs_2_), channel_id=1, source_target_pairs={{0,2},{1,3},{2,0},{3,1},{4,6},{5,7},{6,4},{7,5},{8,10},{9,11},{10,... | collective-permute-start | bytes 1572872 | tf_op jit(solution)/shard_map/ppermute | solution.py:506
  105.4 2.5 %collective-permute-start.16 = (bf16[128,2048]{1,0:T(8,128)(2,1)S(1)}, bf16[128,2048]{1,0:T(8,128)(2,1)S(1)}, u32[]{:S(2)}, u32[]{:S(2)}) collective-permute-start(bf16[128,2048]{1,0:T(8,128)(2,1)S(1)} %collective-permute-done.15.refs_0_), channel_id=1, source_target_pairs={{0,1},{1,0},{2,3},{3,2},{4,5},{5,4},{6,7},{7,6},{8,9},{9,8},{10,11... | collective-permute-start | bytes 1572872 | tf_op jit(solution)/shard_map/ppermute | solution.py:506
  105.4 2.7 %collective-permute-start.17 = (bf16[128,2048]{1,0:T(8,128)(2,1)S(1)}, bf16[128,2048]{1,0:T(8,128)(2,1)S(1)}, u32[]{:S(2)}, u32[]{:S(2)}) collective-permute-start(bf16[128,2048]{1,0:T(8,128)(2,1)S(1)} %collective-permute-done.14.refs_2_), channel_id=1, source_target_pairs={{0,1},{1,0},{2,3},{3,2},{4,5},{5,4},{6,7},{7,6},{8,9},{9,8},{10,11... | collective-permute-start | bytes 1572872 | tf_op jit(solution)/shard_map/ppermute | solution.py:506
  105.9 14.8 %collective-permute-start.18 = (bf16[1024,256]{1,0:T(8,128)(2,1)S(1)}, bf16[1024,256]{1,0:T(8,128)(2,1)S(1)}, u32[]{:S(2)}, u32[]{:S(2)}) collective-permute-start(bf16[1024,256]{1,0:T(8,128)(2,1)S(1)} %get-tuple-element.42.refs_0_), channel_id=1, source_target_pairs={{0,4},{4,0},{8,12},{12,8},{16,20},{20,16},{24,28},{28,24},{1,5},{5... | collective-permute-start | bytes 1572872 | tf_op jit(solution)/shard_map/ppermute | solution.py:503
  107.4 23.5 %collective-permute-start.22 = (bf16[1024,256]{1,0:T(8,128)(2,1)S(1)}, bf16[1024,256]{1,0:T(8,128)(2,1)S(1)}, u32[]{:S(2)}, u32[]{:S(2)}) collective-permute-start(bf16[1024,256]{1,0:T(8,128)(2,1)S(1)} %next.1.refs_0_), channel_id=1, source_target_pairs={{0,4},{4,0},{8,12},{12,8},{16,20},{20,16},{24,28},{28,24},{1,5},{5... | collective-permute-start | bytes 1572872 | tf_op jit(solution)/shard_map/ppermute | solution.py:503
  122.7 16.1 %collective-permute-start.19 = (s16[264,256]{1,0:T(8,128)(2,1)S(1)}, s16[264,256]{1,0:T(8,128)(2,1)S(1)}, u32[]{:S(2)}, u32[]{:S(2)}) collective-permute-start(s16[264,256]{1,0:T(8,128)(2,1)S(1)} %get-tuple-element.44), channel_id=1, source_target_pairs={{0,8},{4,12},{8,0},{12,4},{16,24},{20,28},{24,16},{28,20},{1,9},{5... | collective-permute-start | bytes 405512 | tf_op jit(solution)/shard_map/ppermute | solution.py:503
  126.5 21.5 %collective-permute-start.20 = (s16[264,256]{1,0:T(8,128)(2,1)S(1)}, s16[264,256]{1,0:T(8,128)(2,1)S(1)}, u32[]{:S(2)}, u32[]{:S(2)}) collective-permute-start(s16[264,256]{1,0:T(8,128)(2,1)S(1)} %get-tuple-element.45), channel_id=1, source_target_pairs={{0,16},{4,20},{8,24},{12,28},{16,0},{20,4},{24,8},{28,12},{1,17},{... | collective-permute-start | bytes 405512 | tf_op jit(solution)/shard_map/ppermute | solution.py:503
  128.5 19.5 %collective-permute-start.21 = (s16[264,256]{1,0:T(8,128)(2,1)S(1)}, s16[264,256]{1,0:T(8,128)(2,1)S(1)}, u32[]{:S(2)}, u32[]{:S(2)}) collective-permute-start(s16[264,256]{1,0:T(8,128)(2,1)S(1)} %get-tuple-element.46), channel_id=1, source_target_pairs={{0,24},{4,28},{8,16},{12,20},{16,8},{20,12},{24,0},{28,4},{1,25},{... | collective-permute-start | bytes 405512 | tf_op jit(solution)/shard_map/ppermute | solution.py:503
  132.9 15.1 %collective-permute-start.23 = (s16[264,256]{1,0:T(8,128)(2,1)S(1)}, s16[264,256]{1,0:T(8,128)(2,1)S(1)}, u32[]{:S(2)}, u32[]{:S(2)}) collective-permute-start(s16[264,256]{1,0:T(8,128)(2,1)S(1)} %get-tuple-element.48), channel_id=1, source_target_pairs={{0,8},{4,12},{8,0},{12,4},{16,24},{20,28},{24,16},{28,20},{1,9},{5... | collective-permute-start | bytes 405512 | tf_op jit(solution)/shard_map/ppermute | solution.py:503
  136.8 13.2 %collective-permute-start.24 = (s16[264,256]{1,0:T(8,128)(2,1)S(1)}, s16[264,256]{1,0:T(8,128)(2,1)S(1)}, u32[]{:S(2)}, u32[]{:S(2)}) collective-permute-start(s16[264,256]{1,0:T(8,128)(2,1)S(1)} %get-tuple-element.49), channel_id=1, source_target_pairs={{0,16},{4,20},{8,24},{12,28},{16,0},{20,4},{24,8},{28,12},{1,17},{... | collective-permute-start | bytes 405512 | tf_op jit(solution)/shard_map/ppermute | solution.py:503
  138.8 11.2 %collective-permute-start.25 = (s16[264,256]{1,0:T(8,128)(2,1)S(1)}, s16[264,256]{1,0:T(8,128)(2,1)S(1)}, u32[]{:S(2)}, u32[]{:S(2)}) collective-permute-start(s16[264,256]{1,0:T(8,128)(2,1)S(1)} %get-tuple-element.50), channel_id=1, source_target_pairs={{0,24},{4,28},{8,16},{12,20},{16,8},{20,12},{24,0},{28,4},{1,25},{... | collective-permute-start | bytes 405512 | tf_op jit(solution)/shard_map/ppermute | solution.py:503

commit v4 on v3

--- a/solution.py
+++ b/solution.py
@@ -551,7 +551,7 @@
             fresh = {}
             for offset, value in held.items():
                 if bits < tp // 2:
-                    value = after(value, start)
+                    value = after(value, last if offset == side * (tp // 2) else start)
                 fresh[offset ^ bits] = swap_tensor(value, bits)
             held.update(fresh)
             bits //= 2
@@ -559,7 +559,8 @@
         return normalise(place, halves, packed, gain, side * half, features)
 
     others = [next_weights(place, factors, update, master, CHUNKS, c) for c in range(1, CHUNKS)]
-    near_normed = shared(0, (others or [lead])[-1])
+    last = (others or [lead])[-1]
+    near_normed = shared(0, last)
     normed = (near_normed, shared(1, near_normed))
 
     pieces = []

time: 151 us -> 151 us (level)
  transfers between devices with their start and end apart: 26 -> 26, of which waited for: 12 -> 11; matrix products, arithmetic and copies ran while one was open for 0% -> 0% of each run, Pallas kernels for 16% -> 16%
where the time goes in v4:
time: 151 us
  waiting for transfers between devices  64.5 us (43%)
  starting transfers between devices  50.8 us (34%)
  Pallas kernels  33.9 us (22%)
    ppermute x15, waiting for transfers between devices, swap_dp(): return lax.ppermute(value, 'dp', [(i, i ^ bits) for i in range(dp)])  48.2 us
    ppermute x15, starting transfers between devices, swap_dp(): return lax.ppermute(value, 'dp', [(i, i ^ bits) for i in range(dp)])  28.5 us
    ppermute x9, starting transfers between devices, swap_tensor(): return lax.ppermute(value, 'tensor', [(i, i ^ bits) for i in range(tp)])  19.5 us
    ppermute x9, waiting for transfers between devices, swap_tensor(): return lax.ppermute(value, 'tensor', [(i, i ^ bits) for i in range(tp)])  12 us
    pallas_call x1, Pallas kernels, local_grams(): pl.pallas_call(functools.partial(gram_kernel, parts=parts), in_specs=[SM,...  9.02 us
    pallas_call x1, Pallas kernels, apply_update(): pl.pallas_call(apply_kernel, in_specs=[SM, VM, anywhere, anywhere], out_s...  7.83 us
    ppermute x2, waiting for transfers between devices, turn(): return lax.ppermute(value, ('dp', 'tensor'), pairs)  4.3 us
    pallas_call x1, Pallas kernels, series(): pl.pallas_call(functools.partial(series_kernel, step_scale=step_scale), i...  4.27 us
  transfers between devices with their start and end apart: 26, of which 11 were waited for; matrix products, arithmetic and copies ran while one was open for 0% of the time, Pallas kernels for 16%

profile of v4, /device:TPU:0, one launch (start us, length us, event | category | flops | bytes accessed | tf_op | source)
XLA Modules:
  0.0 151.2 jit_solution(5339292202668565660)
XLA Ops:
  1.4 9.0 %grams.1 = (f32[2,1024,512]{2,1,0:T(8,128)}, f32[2,1024,512]{2,1,0:T(8,128)S(1)}, f32[264,128]{1,0:T(8,128)S(1)}, f32[264,128]{1,0:T(8,128)S(1)}, f32[264,128]{1,0:T(8,128)S(1)}, /*index=5*/f32[264,128]{1,0:T(8,128)S(1)}) custom-call(s32[11]{0:T(128)S(1)} %pad_add_fusion.place, f32[2,1024,512]{2,1,0:T(8,128)} %momentum.1, f32[2,1024,512]{2,1,0:T(8,128)} %gradient.1), custom_call_target="tpu_custom_call" | custom-call | tf_op jit(solution)/shard_map/grams/pallas_call | solution.py:176
  10.4 5.1 %collective-permute-start.2 = (f32[264,128]{1,0:T(8,128)S(1)}, f32[264,128]{1,0:T(8,128)S(1)}, u32[]{:S(2)}, u32[]{:S(2)}) collective-permute-start(f32[264,128]{1,0:T(8,128)S(1)} %get-tuple-element.30), channel_id=1, source_target_pairs={{0,24},{4,28},{8,16},{12,20},{16,8},{20,12},{24,0},{28,4},{1,25},{... | collective-permute-start | bytes 405512 | tf_op jit(solution)/shard_map/ppermute | solution.py:503
  16.5 1.7 %collective-permute-start.4 = (f32[256]{0:T(256)S(1)}, f32[256]{0:T(256)S(1)}, u32[]{:S(2)}, u32[]{:S(2)}) collective-permute-start(f32[256]{0:T(256)S(1)} %multiply_reduce_fusion), channel_id=1, source_target_pairs={{0,2},{1,3},{2,0},{3,1},{4,6},{5,7},{6,4},{7,5},{8,10},{9,11},{10,... | collective-permute-start | bytes 3080 | tf_op jit(solution)/shard_map/ppermute | solution.py:506
  20.1 3.7 %collective-permute-start.13 = (bf16[128,2048]{1,0:T(8,128)(2,1)S(1)}, bf16[128,2048]{1,0:T(8,128)(2,1)S(1)}, u32[]{:S(2)}, u32[]{:S(2)}) collective-permute-start(bf16[128,2048]{1,0:T(8,128)(2,1)S(1)} %slice.7), channel_id=1, source_target_pairs={{0,2},{1,3},{2,0},{3,1},{4,6},{5,7},{6,4},{7,5},{8,10},{9,11},{10,... | collective-permute-start | bytes 1572872 | tf_op jit(solution)/shard_map/ppermute | solution.py:506
  25.2 14.0 %collective-permute-done.1 = f32[264,128]{1,0:T(8,128)S(1)} collective-permute-done((f32[264,128]{1,0:T(8,128)S(1)}, f32[264,128]{1,0:T(8,128)S(1)}, u32[]{:S(2)}, u32[]{:S(2)}) %collective-permute-start.1) | collective-permute-done | bytes 135200 | tf_op jit(solution)/shard_map/ppermute | solution.py:503
  39.2 1.6 %collective-permute-start.3 = (f32[264,128]{1,0:T(8,128)S(1)}, f32[264,128]{1,0:T(8,128)S(1)}, u32[]{:S(2)}, u32[]{:S(2)}) collective-permute-start(f32[264,128]{1,0:T(8,128)S(1)} %add_add_fusion.refs_0_), channel_id=1, source_target_pairs={{0,4},{4,0},{8,12},{12,8},{16,20},{20,16},{24,28},{28,24},{1,5},{5... | collective-permute-start | bytes 405512 | tf_op jit(solution)/shard_map/ppermute | solution.py:503
  40.8 3.5 %collective-permute-done.3.refs_1_ = f32[264,128]{1,0:T(8,128)S(1)} collective-permute-done((f32[264,128]{1,0:T(8,128)S(1)}, f32[264,128]{1,0:T(8,128)S(1)}, u32[]{:S(2)}, u32[]{:S(2)}) %collective-permute-start.3) | collective-permute-done | bytes 135200 | tf_op jit(solution)/shard_map/ppermute | solution.py:503
  44.3 4.3 %series.1.refs_0_.refs_4_ = f32[264,128]{1,0:T(8,128)S(1)} custom-call(f32[264,128]{1,0:T(8,128)S(1)} %add_add_fusion.refs_0_, f32[264,128]{1,0:T(8,128)S(1)} %collective-permute-done.3.refs_1_, f32[2,128]{1,0:T(2,128)S(1)} %add_bitcast_fusion.refs_2_), custom_call_target="tpu_custom_call" | custom-call | tf_op jit(solution)/shard_map/series/pallas_call | solution.py:229
  48.6 2.4 %collective-permute-start.11 = (bf16[128,2048]{1,0:T(8,128)(2,1)S(1)}, bf16[128,2048]{1,0:T(8,128)(2,1)S(1)}, u32[]{:S(2)}, u32[]{:S(2)}) collective-permute-start(bf16[128,2048]{1,0:T(8,128)(2,1)S(1)} %collective-permute-done.9.refs_0_), channel_id=1, source_target_pairs={{0,2},{1,3},{2,0},{3,1},{4,6},{5,7},{6,4},{7,5},{8,10},{9,11},{10,... | collective-permute-start | bytes 1572872 | tf_op jit(solution)/shard_map/ppermute | solution.py:506
  51.0 2.1 %collective-permute-start.14 = (bf16[128,2048]{1,0:T(8,128)(2,1)S(1)}, bf16[128,2048]{1,0:T(8,128)(2,1)S(1)}, u32[]{:S(2)}, u32[]{:S(2)}) collective-permute-start(bf16[128,2048]{1,0:T(8,128)(2,1)S(1)} %collective-permute-done.13), channel_id=1, source_target_pairs={{0,18},{1,26},{2,2},{3,10},{4,22},{5,30},{6,6},{7,14},{8,19},{9,27... | collective-permute-start | bytes 1572872 | tf_op jit(solution)/shard_map/ppermute | solution.py:519
  53.1 2.2 %collective-permute-start.6 = (f32[264,128]{1,0:T(8,128)S(1)}, f32[264,128]{1,0:T(8,128)S(1)}, u32[]{:S(2)}, u32[]{:S(2)}) collective-permute-start(f32[264,128]{1,0:T(8,128)S(1)} %series.1.refs_0_.refs_4_), channel_id=1, source_target_pairs={{0,8},{4,12},{8,0},{12,4},{16,24},{20,28},{24,16},{28,20},{1,9},{5... | collective-permute-start | bytes 405512 | tf_op jit(solution)/shard_map/ppermute | solution.py:503
  55.6 2.2 %collective-permute-start.8 = (f32[264,128]{1,0:T(8,128)S(1)}, f32[264,128]{1,0:T(8,128)S(1)}, u32[]{:S(2)}, u32[]{:S(2)}) collective-permute-start(f32[264,128]{1,0:T(8,128)S(1)} %series.1.refs_0_.refs_4_), channel_id=1, source_target_pairs={{0,24},{4,28},{8,16},{12,20},{16,8},{20,12},{24,0},{28,4},{1,25},{... | collective-permute-start | bytes 405512 | tf_op jit(solution)/shard_map/ppermute | solution.py:503
  57.8 9.7 %collective-permute-done.6.refs_1_.refs_5_ = f32[264,128]{1,0:T(8,128)S(1)} collective-permute-done((f32[264,128]{1,0:T(8,128)S(1)}, f32[264,128]{1,0:T(8,128)S(1)}, u32[]{:S(2)}, u32[]{:S(2)}) %collective-permute-start.6) | collective-permute-done | bytes 135200 | tf_op jit(solution)/shard_map/ppermute | solution.py:503
  67.5 2.9 %collective-permute-done.7.refs_2_.refs_6_ = f32[264,128]{1,0:T(8,128)S(1)} collective-permute-done((f32[264,128]{1,0:T(8,128)S(1)}, f32[264,128]{1,0:T(8,128)S(1)}, u32[]{:S(2)}, u32[]{:S(2)}) %collective-permute-start.7) | collective-permute-done | bytes 135200 | tf_op jit(solution)/shard_map/ppermute | solution.py:503
  70.4 2.9 %collective-permute-done.8.refs_3_.refs_7_ = f32[264,128]{1,0:T(8,128)S(1)} collective-permute-done((f32[264,128]{1,0:T(8,128)S(1)}, f32[264,128]{1,0:T(8,128)S(1)}, u32[]{:S(2)}, u32[]{:S(2)}) %collective-permute-start.8) | collective-permute-done | bytes 135200 | tf_op jit(solution)/shard_map/ppermute | solution.py:503
  73.3 2.8 %lead.1 = (bf16[1024,256]{1,0:T(8,128)(2,1)S(1)}, bf16[4,1536,256]{2,1,0:T(8,128)(2,1)S(1)}) custom-call(s32[11]{0:T(128)S(1)} %pad_add_fusion.place, f32[264,128]{1,0:T(8,128)S(1)} %series.1.refs_0_.refs_4_, f32[264,128]{1,0:T(8,128)S(1)} %collective-permute-done.6.refs_1_.refs_5_, f32[264,128]{1,0:T(8,128)S(1)} %collective-permute-done.7.refs_2_.refs_6_, ...), custom_call_target="tpu_custom_call" | custom-call | tf_op jit(solution)/shard_map/lead/pallas_call | solution.py:294
  76.2 2.4 %next.1.refs_0_ = bf16[1024,256]{1,0:T(8,128)(2,1)S(1)} custom-call(s32[11]{0:T(128)S(1)} %pad_add_fusion.place, bf16[4,1536,256]{2,1,0:T(8,128)(2,1)S(1)} %get-tuple-element.32.factors, f32[2,1024,512]{2,1,0:T(8,128)S(1)} %get-tuple-element.31.refs_4_.update, f32[2,1024,512]{2,1,0:T(8,128)S(1)} %copy-done), custom_call_target="tpu_custom_call" | custom-call | tf_op jit(solution)/shard_map/next/pallas_call | solution.py:316
  79.6 4.3 %collective-permute-done.14.refs_2_ = bf16[128,2048]{1,0:T(8,128)(2,1)S(1)} collective-permute-done((bf16[128,2048]{1,0:T(8,128)(2,1)S(1)}, bf16[128,2048]{1,0:T(8,128)(2,1)S(1)}, u32[]{:S(2)}, u32[]{:S(2)}) %collective-permute-start.14) | collective-permute-done | bytes 524320 | tf_op jit(solution)/shard_map/ppermute | solution.py:519
  83.9 9.3 %collective-permute-start.15 = (bf16[128,2048]{1,0:T(8,128)(2,1)S(1)}, bf16[128,2048]{1,0:T(8,128)(2,1)S(1)}, u32[]{:S(2)}, u32[]{:S(2)}) collective-permute-start(bf16[128,2048]{1,0:T(8,128)(2,1)S(1)} %collective-permute-done.14.refs_2_), channel_id=1, source_target_pairs={{0,2},{1,3},{2,0},{3,1},{4,6},{5,7},{6,4},{7,5},{8,10},{9,11},{10,... | collective-permute-start | bytes 1572872 | tf_op jit(solution)/shard_map/ppermute | solution.py:506
  94.6 10.8 %collective-permute-done.15.refs_0_ = bf16[128,2048]{1,0:T(8,128)(2,1)S(1)} collective-permute-done((bf16[128,2048]{1,0:T(8,128)(2,1)S(1)}, bf16[128,2048]{1,0:T(8,128)(2,1)S(1)}, u32[]{:S(2)}, u32[]{:S(2)}) %collective-permute-start.15) | collective-permute-done | bytes 524320 | tf_op jit(solution)/shard_map/ppermute | solution.py:506
  105.4 1.5 %collective-permute-start.18 = (bf16[1024,256]{1,0:T(8,128)(2,1)S(1)}, bf16[1024,256]{1,0:T(8,128)(2,1)S(1)}, u32[]{:S(2)}, u32[]{:S(2)}) collective-permute-start(bf16[1024,256]{1,0:T(8,128)(2,1)S(1)} %get-tuple-element.42.refs_0_), channel_id=1, source_target_pairs={{0,4},{4,0},{8,12},{12,8},{16,20},{20,16},{24,28},{28,24},{1,5},{5... | collective-permute-start | bytes 1572872 | tf_op jit(solution)/shard_map/ppermute | solution.py:503
  108.8 11.4 %collective-permute-done.18.refs_1_ = bf16[1024,256]{1,0:T(8,128)(2,1)S(1)} collective-permute-done((bf16[1024,256]{1,0:T(8,128)(2,1)S(1)}, bf16[1024,256]{1,0:T(8,128)(2,1)S(1)}, u32[]{:S(2)}, u32[]{:S(2)}) %collective-permute-start.18) | collective-permute-done | bytes 524320 | tf_op jit(solution)/shard_map/ppermute | solution.py:503
  120.2 2.0 %project.2 = (f32[256,256]{1,0:T(8,128)S(1)}, s16[264,256]{1,0:T(8,128)(2,1)S(1)}, s16[264,256]{1,0:T(8,128)(2,1)S(1)}, s16[264,256]{1,0:T(8,128)(2,1)S(1)}) custom-call(s32[11]{0:T(128)S(1)} %pad_add_fusion.place, bf16[4,128,2048]{2,1,0:T(8,128)(2,1)S(1)} %normalise.2.near, bf16[4,128,2048]{2,1,0:T(8,128)(2,1)S(1)} %normalise.3.far, ...), custom_call_target="tpu_custom_call" | custom-call | tf_op jit(solution)/shard_map/project/pallas_call | solution.py:473
  122.2 3.9 %collective-permute-start.19 = (s16[264,256]{1,0:T(8,128)(2,1)S(1)}, s16[264,256]{1,0:T(8,128)(2,1)S(1)}, u32[]{:S(2)}, u32[]{:S(2)}) collective-permute-start(s16[264,256]{1,0:T(8,128)(2,1)S(1)} %get-tuple-element.44), channel_id=1, source_target_pairs={{0,8},{4,12},{8,0},{12,4},{16,24},{20,28},{24,16},{28,20},{1,9},{5... | collective-permute-start | bytes 405512 | tf_op jit(solution)/shard_map/ppermute | solution.py:503
  126.0 2.0 %collective-permute-start.20 = (s16[264,256]{1,0:T(8,128)(2,1)S(1)}, s16[264,256]{1,0:T(8,128)(2,1)S(1)}, u32[]{:S(2)}, u32[]{:S(2)}) collective-permute-start(s16[264,256]{1,0:T(8,128)(2,1)S(1)} %get-tuple-element.45), channel_id=1, source_target_pairs={{0,16},{4,20},{8,24},{12,28},{16,0},{20,4},{24,8},{28,12},{1,17},{... | collective-permute-start | bytes 405512 | tf_op jit(solution)/shard_map/ppermute | solution.py:503
  129.4 1.6 %collective-permute-done.22.refs_1_ = bf16[1024,256]{1,0:T(8,128)(2,1)S(1)} collective-permute-done((bf16[1024,256]{1,0:T(8,128)(2,1)S(1)}, bf16[1024,256]{1,0:T(8,128)(2,1)S(1)}, u32[]{:S(2)}, u32[]{:S(2)}) %collective-permute-start.22) | collective-permute-done | bytes 524320 | tf_op jit(solution)/shard_map/ppermute | solution.py:503
  131.0 1.9 %project.3 = (f32[256,256]{1,0:T(8,128)S(1)}, s16[264,256]{1,0:T(8,128)(2,1)S(1)}, s16[264,256]{1,0:T(8,128)(2,1)S(1)}, s16[264,256]{1,0:T(8,128)(2,1)S(1)}) custom-call(s32[11]{0:T(128)S(1)} %pad_add_fusion.place, bf16[4,128,2048]{2,1,0:T(8,128)(2,1)S(1)} %normalise.2.near, bf16[4,128,2048]{2,1,0:T(8,128)(2,1)S(1)} %normalise.3.far, ...), custom_call_target="tpu_custom_call" | custom-call | tf_op jit(solution)/shard_map/project/pallas_call | solution.py:473
  132.9 3.9 %collective-permute-start.23 = (s16[264,256]{1,0:T(8,128)(2,1)S(1)}, s16[264,256]{1,0:T(8,128)(2,1)S(1)}, u32[]{:S(2)}, u32[]{:S(2)}) collective-permute-start(s16[264,256]{1,0:T(8,128)(2,1)S(1)} %get-tuple-element.48), channel_id=1, source_target_pairs={{0,8},{4,12},{8,0},{12,4},{16,24},{20,28},{24,16},{28,20},{1,9},{5... | collective-permute-start | bytes 405512 | tf_op jit(solution)/shard_map/ppermute | solution.py:503
  136.8 2.0 %collective-permute-start.24 = (s16[264,256]{1,0:T(8,128)(2,1)S(1)}, s16[264,256]{1,0:T(8,128)(2,1)S(1)}, u32[]{:S(2)}, u32[]{:S(2)}) collective-permute-start(s16[264,256]{1,0:T(8,128)(2,1)S(1)} %get-tuple-element.49), channel_id=1, source_target_pairs={{0,16},{4,20},{8,24},{12,28},{16,0},{20,4},{24,8},{28,12},{1,17},{... | collective-permute-start | bytes 405512 | tf_op jit(solution)/shard_map/ppermute | solution.py:503
  138.8 1.4 collective-permute-start.25
  140.2 7.8 %apply.1 = f32[2,1024,512]{2,1,0:T(8,128)} custom-call(s32[11]{0:T(128)S(1)} %pad_add_fusion.place, bf16[4,1536,256]{2,1,0:T(8,128)(2,1)S(1)} %get-tuple-element.32.factors, f32[2,1024,512]{2,1,0:T(8,128)} %copy-done.1, f32[2,1024,512]{2,1,0:T(8,128)} %master.3), custom_call_target="tpu_custom_call" | custom-call | tf_op jit(solution)/shard_map/apply/pallas_call | solution.py:364
  148.0 2.2 %collective-permute-done.24.refs_6_ = s16[264,256]{1,0:T(8,128)(2,1)S(1)} collective-permute-done((s16[264,256]{1,0:T(8,128)(2,1)S(1)}, s16[264,256]{1,0:T(8,128)(2,1)S(1)}, u32[]{:S(2)}, u32[]{:S(2)}) %collective-permute-start.24) | collective-permute-done | bytes 135200 | tf_op jit(solution)/shard_map/ppermute | solution.py:503
  (45 shorter events, 11.8 us)
Async XLA Ops:
  1.4 14.8 %copy-start.3 = (bf16[256,2048]{1,0:T(8,128)(2,1)S(1)}, bf16[256,2048]{1,0:T(8,128)(2,1)}, u32[]{:S(2)}) copy-start(bf16[256,2048]{1,0:T(8,128)(2,1)} %param.10) | copy-start | bytes 3145732
  10.4 65.8 %copy-start.1 = (f32[2,1024,512]{2,1,0:T(8,128)}, f32[2,1024,512]{2,1,0:T(8,128)S(1)}, u32[]{:S(2)}) copy-start(f32[2,1024,512]{2,1,0:T(8,128)S(1)} %get-tuple-element.31.refs_4_.update) | copy-start | bytes 12582916
  10.4 62.9 %copy-start = (f32[2,1024,512]{2,1,0:T(8,128)S(1)}, f32[2,1024,512]{2,1,0:T(8,128)}, u32[]{:S(2)}) copy-start(f32[2,1024,512]{2,1,0:T(8,128)} %master.3) | copy-start | bytes 12582916
  10.4 13.5 %collective-permute-start.2 = (f32[264,128]{1,0:T(8,128)S(1)}, f32[264,128]{1,0:T(8,128)S(1)}, u32[]{:S(2)}, u32[]{:S(2)}) collective-permute-start(f32[264,128]{1,0:T(8,128)S(1)} %get-tuple-element.30), channel_id=1, source_target_pairs={{0,24},{4,28},{8,16},{12,20},{16,8},{20,12},{24,0},{28,4},{1,25},{... | collective-permute-start | bytes 405512 | tf_op jit(solution)/shard_map/ppermute | solution.py:503
  15.6 23.6 %collective-permute-start.1 = (f32[264,128]{1,0:T(8,128)S(1)}, f32[264,128]{1,0:T(8,128)S(1)}, u32[]{:S(2)}, u32[]{:S(2)}) collective-permute-start(f32[264,128]{1,0:T(8,128)S(1)} %get-tuple-element.29), channel_id=1, source_target_pairs={{0,16},{4,20},{8,24},{12,28},{16,0},{20,4},{24,8},{28,12},{1,17},{... | collective-permute-start | bytes 405512 | tf_op jit(solution)/shard_map/ppermute | solution.py:503
  15.6 23.6 %collective-permute-start = (f32[264,128]{1,0:T(8,128)S(1)}, f32[264,128]{1,0:T(8,128)S(1)}, u32[]{:S(2)}, u32[]{:S(2)}) collective-permute-start(f32[264,128]{1,0:T(8,128)S(1)} %get-tuple-element.28), channel_id=1, source_target_pairs={{0,8},{4,12},{8,0},{12,4},{16,24},{20,28},{24,16},{28,20},{1,9},{5... | collective-permute-start | bytes 405512 | tf_op jit(solution)/shard_map/ppermute | solution.py:503
  16.5 3.6 %collective-permute-start.4 = (f32[256]{0:T(256)S(1)}, f32[256]{0:T(256)S(1)}, u32[]{:S(2)}, u32[]{:S(2)}) collective-permute-start(f32[256]{0:T(256)S(1)} %multiply_reduce_fusion), channel_id=1, source_target_pairs={{0,2},{1,3},{2,0},{3,1},{4,6},{5,7},{6,4},{7,5},{8,10},{9,11},{10,... | collective-permute-start | bytes 3080 | tf_op jit(solution)/shard_map/ppermute | solution.py:506
  18.2 30.3 %collective-permute-start.9 = (bf16[128,2048]{1,0:T(8,128)(2,1)S(1)}, bf16[128,2048]{1,0:T(8,128)(2,1)S(1)}, u32[]{:S(2)}, u32[]{:S(2)}) collective-permute-start(bf16[128,2048]{1,0:T(8,128)(2,1)S(1)} %slice.6), channel_id=1, source_target_pairs={{0,0},{1,8},{2,16},{3,24},{4,4},{5,12},{6,20},{7,28},{8,1},{9,9},{... | collective-permute-start | bytes 1572872 | tf_op jit(solution)/shard_map/ppermute | solution.py:519
  20.1 30.9 %collective-permute-start.13 = (bf16[128,2048]{1,0:T(8,128)(2,1)S(1)}, bf16[128,2048]{1,0:T(8,128)(2,1)S(1)}, u32[]{:S(2)}, u32[]{:S(2)}) collective-permute-start(bf16[128,2048]{1,0:T(8,128)(2,1)S(1)} %slice.7), channel_id=1, source_target_pairs={{0,2},{1,3},{2,0},{3,1},{4,6},{5,7},{6,4},{7,5},{8,10},{9,11},{10,... | collective-permute-start | bytes 1572872 | tf_op jit(solution)/shard_map/ppermute | solution.py:506
  23.9 16.9 %collective-permute-start.5 = (f32[256]{0:T(256)S(1)}, f32[256]{0:T(256)S(1)}, u32[]{:S(2)}, u32[]{:S(2)}) collective-permute-start(f32[256]{0:T(256)S(1)} %add.24), channel_id=1, source_target_pairs={{0,1},{1,0},{2,3},{3,2},{4,5},{5,4},{6,7},{7,6},{8,9},{9,8},{10,11... | collective-permute-start | bytes 3080 | tf_op jit(solution)/shard_map/ppermute | solution.py:506
  39.2 5.1 %collective-permute-start.3 = (f32[264,128]{1,0:T(8,128)S(1)}, f32[264,128]{1,0:T(8,128)S(1)}, u32[]{:S(2)}, u32[]{:S(2)}) collective-permute-start(f32[264,128]{1,0:T(8,128)S(1)} %add_add_fusion.refs_0_), channel_id=1, source_target_pairs={{0,4},{4,0},{8,12},{12,8},{16,20},{20,16},{24,28},{28,24},{1,5},{5... | collective-permute-start | bytes 405512 | tf_op jit(solution)/shard_map/ppermute | solution.py:503
  48.6 30.9 %collective-permute-start.11 = (bf16[128,2048]{1,0:T(8,128)(2,1)S(1)}, bf16[128,2048]{1,0:T(8,128)(2,1)S(1)}, u32[]{:S(2)}, u32[]{:S(2)}) collective-permute-start(bf16[128,2048]{1,0:T(8,128)(2,1)S(1)} %collective-permute-done.9.refs_0_), channel_id=1, source_target_pairs={{0,2},{1,3},{2,0},{3,1},{4,6},{5,7},{6,4},{7,5},{8,10},{9,11},{10,... | collective-permute-start | bytes 1572872 | tf_op jit(solution)/shard_map/ppermute | solution.py:506
  51.0 32.9 %collective-permute-start.14 = (bf16[128,2048]{1,0:T(8,128)(2,1)S(1)}, bf16[128,2048]{1,0:T(8,128)(2,1)S(1)}, u32[]{:S(2)}, u32[]{:S(2)}) collective-permute-start(bf16[128,2048]{1,0:T(8,128)(2,1)S(1)} %collective-permute-done.13), channel_id=1, source_target_pairs={{0,18},{1,26},{2,2},{3,10},{4,22},{5,30},{6,6},{7,14},{8,19},{9,27... | collective-permute-start | bytes 1572872 | tf_op jit(solution)/shard_map/ppermute | solution.py:519
  53.1 14.3 %collective-permute-start.6 = (f32[264,128]{1,0:T(8,128)S(1)}, f32[264,128]{1,0:T(8,128)S(1)}, u32[]{:S(2)}, u32[]{:S(2)}) collective-permute-start(f32[264,128]{1,0:T(8,128)S(1)} %series.1.refs_0_.refs_4_), channel_id=1, source_target_pairs={{0,8},{4,12},{8,0},{12,4},{16,24},{20,28},{24,16},{28,20},{1,9},{5... | collective-permute-start | bytes 405512 | tf_op jit(solution)/shard_map/ppermute | solution.py:503
  55.4 15.1 %collective-permute-start.7 = (f32[264,128]{1,0:T(8,128)S(1)}, f32[264,128]{1,0:T(8,128)S(1)}, u32[]{:S(2)}, u32[]{:S(2)}) collective-permute-start(f32[264,128]{1,0:T(8,128)S(1)} %series.1.refs_0_.refs_4_), channel_id=1, source_target_pairs={{0,16},{4,20},{8,24},{12,28},{16,0},{20,4},{24,8},{28,12},{1,17},{... | collective-permute-start | bytes 405512 | tf_op jit(solution)/shard_map/ppermute | solution.py:503
  55.6 17.7 %collective-permute-start.8 = (f32[264,128]{1,0:T(8,128)S(1)}, f32[264,128]{1,0:T(8,128)S(1)}, u32[]{:S(2)}, u32[]{:S(2)}) collective-permute-start(f32[264,128]{1,0:T(8,128)S(1)} %series.1.refs_0_.refs_4_), channel_id=1, source_target_pairs={{0,24},{4,28},{8,16},{12,20},{16,8},{20,12},{24,0},{28,4},{1,25},{... | collective-permute-start | bytes 405512 | tf_op jit(solution)/shard_map/ppermute | solution.py:503
  76.2 17.1 %copy-start.2 = (f32[8192]{0:T(1024)S(1)}, f32[8192]{0:T(1024)}, u32[]{:S(2)}) copy-start(f32[8192]{0:T(1024)} %param.11) | copy-start | bytes 98308
  78.6 14.6 %collective-permute-start.10 = (bf16[128,2048]{1,0:T(8,128)(2,1)S(1)}, bf16[128,2048]{1,0:T(8,128)(2,1)S(1)}, u32[]{:S(2)}, u32[]{:S(2)}) collective-permute-start(bf16[128,2048]{1,0:T(8,128)(2,1)S(1)} %collective-permute-done.9.refs_0_), channel_id=1, source_target_pairs={{0,1},{1,0},{2,3},{3,2},{4,5},{5,4},{6,7},{7,6},{8,9},{9,8},{10,11... | collective-permute-start | bytes 1572872 | tf_op jit(solution)/shard_map/ppermute | solution.py:506
  79.5 13.7 %collective-permute-start.12 = (bf16[128,2048]{1,0:T(8,128)(2,1)S(1)}, bf16[128,2048]{1,0:T(8,128)(2,1)S(1)}, u32[]{:S(2)}, u32[]{:S(2)}) collective-permute-start(bf16[128,2048]{1,0:T(8,128)(2,1)S(1)} %collective-permute-done.11.refs_2_), channel_id=1, source_target_pairs={{0,1},{1,0},{2,3},{3,2},{4,5},{5,4},{6,7},{7,6},{8,9},{9,8},{10,11... | collective-permute-start | bytes 1572872 | tf_op jit(solution)/shard_map/ppermute | solution.py:506
  83.9 21.5 %collective-permute-start.15 = (bf16[128,2048]{1,0:T(8,128)(2,1)S(1)}, bf16[128,2048]{1,0:T(8,128)(2,1)S(1)}, u32[]{:S(2)}, u32[]{:S(2)}) collective-permute-start(bf16[128,2048]{1,0:T(8,128)(2,1)S(1)} %collective-permute-done.14.refs_2_), channel_id=1, source_target_pairs={{0,2},{1,3},{2,0},{3,1},{4,6},{5,7},{6,4},{7,5},{8,10},{9,11},{10,... | collective-permute-start | bytes 1572872 | tf_op jit(solution)/shard_map/ppermute | solution.py:506
  93.2 14.2 %collective-permute-start.17 = (bf16[128,2048]{1,0:T(8,128)(2,1)S(1)}, bf16[128,2048]{1,0:T(8,128)(2,1)S(1)}, u32[]{:S(2)}, u32[]{:S(2)}) collective-permute-start(bf16[128,2048]{1,0:T(8,128)(2,1)S(1)} %collective-permute-done.14.refs_2_), channel_id=1, source_target_pairs={{0,1},{1,0},{2,3},{3,2},{4,5},{5,4},{6,7},{7,6},{8,9},{9,8},{10,11... | collective-permute-start | bytes 1572872 | tf_op jit(solution)/shard_map/ppermute | solution.py:506
  105.4 2.0 %collective-permute-start.16 = (bf16[128,2048]{1,0:T(8,128)(2,1)S(1)}, bf16[128,2048]{1,0:T(8,128)(2,1)S(1)}, u32[]{:S(2)}, u32[]{:S(2)}) collective-permute-start(bf16[128,2048]{1,0:T(8,128)(2,1)S(1)} %collective-permute-done.15.refs_0_), channel_id=1, source_target_pairs={{0,1},{1,0},{2,3},{3,2},{4,5},{5,4},{6,7},{7,6},{8,9},{9,8},{10,11... | collective-permute-start | bytes 1572872 | tf_op jit(solution)/shard_map/ppermute | solution.py:506
  105.4 14.8 %collective-permute-start.18 = (bf16[1024,256]{1,0:T(8,128)(2,1)S(1)}, bf16[1024,256]{1,0:T(8,128)(2,1)S(1)}, u32[]{:S(2)}, u32[]{:S(2)}) collective-permute-start(bf16[1024,256]{1,0:T(8,128)(2,1)S(1)} %get-tuple-element.42.refs_0_), channel_id=1, source_target_pairs={{0,4},{4,0},{8,12},{12,8},{16,20},{20,16},{24,28},{28,24},{1,5},{5... | collective-permute-start | bytes 1572872 | tf_op jit(solution)/shard_map/ppermute | solution.py:503
  106.9 24.1 %collective-permute-start.22 = (bf16[1024,256]{1,0:T(8,128)(2,1)S(1)}, bf16[1024,256]{1,0:T(8,128)(2,1)S(1)}, u32[]{:S(2)}, u32[]{:S(2)}) collective-permute-start(bf16[1024,256]{1,0:T(8,128)(2,1)S(1)} %next.1.refs_0_), channel_id=1, source_target_pairs={{0,4},{4,0},{8,12},{12,8},{16,20},{20,16},{24,28},{28,24},{1,5},{5... | collective-permute-start | bytes 1572872 | tf_op jit(solution)/shard_map/ppermute | solution.py:503
  122.2 16.6 %collective-permute-start.19 = (s16[264,256]{1,0:T(8,128)(2,1)S(1)}, s16[264,256]{1,0:T(8,128)(2,1)S(1)}, u32[]{:S(2)}, u32[]{:S(2)}) collective-permute-start(s16[264,256]{1,0:T(8,128)(2,1)S(1)} %get-tuple-element.44), channel_id=1, source_target_pairs={{0,8},{4,12},{8,0},{12,4},{16,24},{20,28},{24,16},{28,20},{1,9},{5... | collective-permute-start | bytes 405512 | tf_op jit(solution)/shard_map/ppermute | solution.py:503
  126.0 22.0 %collective-permute-start.20 = (s16[264,256]{1,0:T(8,128)(2,1)S(1)}, s16[264,256]{1,0:T(8,128)(2,1)S(1)}, u32[]{:S(2)}, u32[]{:S(2)}) collective-permute-start(s16[264,256]{1,0:T(8,128)(2,1)S(1)} %get-tuple-element.45), channel_id=1, source_target_pairs={{0,16},{4,20},{8,24},{12,28},{16,0},{20,4},{24,8},{28,12},{1,17},{... | collective-permute-start | bytes 405512 | tf_op jit(solution)/shard_map/ppermute | solution.py:503
  128.0 20.0 %collective-permute-start.21 = (s16[264,256]{1,0:T(8,128)(2,1)S(1)}, s16[264,256]{1,0:T(8,128)(2,1)S(1)}, u32[]{:S(2)}, u32[]{:S(2)}) collective-permute-start(s16[264,256]{1,0:T(8,128)(2,1)S(1)} %get-tuple-element.46), channel_id=1, source_target_pairs={{0,24},{4,28},{8,16},{12,20},{16,8},{20,12},{24,0},{28,4},{1,25},{... | collective-permute-start | bytes 405512 | tf_op jit(solution)/shard_map/ppermute | solution.py:503
  132.9 15.1 %collective-permute-start.23 = (s16[264,256]{1,0:T(8,128)(2,1)S(1)}, s16[264,256]{1,0:T(8,128)(2,1)S(1)}, u32[]{:S(2)}, u32[]{:S(2)}) collective-permute-start(s16[264,256]{1,0:T(8,128)(2,1)S(1)} %get-tuple-element.48), channel_id=1, source_target_pairs={{0,8},{4,12},{8,0},{12,4},{16,24},{20,28},{24,16},{28,20},{1,9},{5... | collective-permute-start | bytes 405512 | tf_op jit(solution)/shard_map/ppermute | solution.py:503
  136.8 13.5 %collective-permute-start.24 = (s16[264,256]{1,0:T(8,128)(2,1)S(1)}, s16[264,256]{1,0:T(8,128)(2,1)S(1)}, u32[]{:S(2)}, u32[]{:S(2)}) collective-permute-start(s16[264,256]{1,0:T(8,128)(2,1)S(1)} %get-tuple-element.49), channel_id=1, source_target_pairs={{0,16},{4,20},{8,24},{12,28},{16,0},{20,4},{24,8},{28,12},{1,17},{... | collective-permute-start | bytes 405512 | tf_op jit(solution)/shard_map/ppermute | solution.py:503
  138.8 11.5 %collective-permute-start.25 = (s16[264,256]{1,0:T(8,128)(2,1)S(1)}, s16[264,256]{1,0:T(8,128)(2,1)S(1)}, u32[]{:S(2)}, u32[]{:S(2)}) collective-permute-start(s16[264,256]{1,0:T(8,128)(2,1)S(1)} %get-tuple-element.50), channel_id=1, source_target_pairs={{0,24},{4,28},{8,16},{12,20},{16,8},{20,12},{24,0},{28,4},{1,25},{... | collective-permute-start | bytes 405512 | tf_op jit(solution)/shard_map/ppermute | solution.py:503
